TPU v7x, 256 devices: a whole 4x4x8 slice. The times are simulated.
256 devices in a mesh: rows: 32 (over x, z_hi, core), mask: 8 (over z_lo, y).
Axes of the slice: x: 4, y: 4, z: 8 (z_hi: 4, z_lo: 2; z = z_hi * 2 + z_lo), core: 2. Of those that a mesh axis runs over, the one named last changes fastest.
Arguments:
- image_field: bfloat16 [2, 8192, 8192], P(None, ('rows', 'mask')), may hold values from -6 to 6
- amplitudes: bfloat16 [8, 8192, 8192], P('mask', None, 'rows'), may hold values from 0 to 12, as said below
- mask_ids: int32 [8], P('mask'), may hold values from 0 to 63
Outputs:
- gradient: float32 [2, 8192, 8192], P(None, ('rows', 'mask'))
- loss_value: float32 [], replicated
Inputs may be any that keep to these rules, and one draw needn't show every extreme that they name: `amplitudes`: magnitudes are non-negative.
All inputs are finite; a program needn't handle non-finite values.
Results may differ from a plain program's by a relative error of at most 0.024.
Values may be sent and summed in bfloat16 or wider, within the bound.
A program may use at most 128 MiB of HBM per device.

v0:
```python
import math

import jax
import jax.numpy as jnp
from jax import lax
from jax.sharding import PartitionSpec as P

INNER = 128


EPSILON = 0.25


def shift_bits(values, count):
    return lax.shift_right_logical(values, jnp.full(values.shape, count, jnp.int32))


def mask_code(window_id, row_index, column_index):
    mixed = (
        row_index * jnp.int32(73856093)
        ^ column_index * jnp.int32(19349663)
        ^ (window_id + jnp.int32(1)) * jnp.int32(83492791)
    )
    mixed = mixed ^ shift_bits(mixed, 13)
    mixed = mixed * jnp.int32(1274126177)
    mixed = mixed ^ shift_bits(mixed, 16)
    return shift_bits(mixed, 28) & jnp.int32(3)


def rotate(real_part, imag_part, phase_code, direction):
    cosine = (phase_code == 0).astype(jnp.float32) - (phase_code == 2).astype(jnp.float32)
    sine = direction * (
        (phase_code == 1).astype(jnp.float32) - (phase_code == 3).astype(jnp.float32)
    )
    return (real_part * cosine - imag_part * sine, real_part * sine + imag_part * cosine)


def factor_table(length, direction):
    index = jnp.arange(length, dtype=jnp.int32)
    angles = (index[:, None] * index[None, :] % length).astype(jnp.float32) * (
        2.0 * math.pi / length
    )
    cosine = jnp.cos(angles)
    sine = direction * jnp.sin(angles)
    upper = jnp.stack([cosine, -sine], axis=1)
    lower = jnp.stack([sine, cosine], axis=1)
    return jnp.stack([upper, lower]).astype(jnp.bfloat16)


def turn_table(outer, inner, length, direction):
    first = jnp.arange(outer, dtype=jnp.int32)[:, None]
    second = jnp.arange(inner, dtype=jnp.int32)[None, :]
    angles = (first * second % length).astype(jnp.float32) * (2.0 * math.pi / length)
    return (jnp.cos(angles), direction * jnp.sin(angles))


def factor(form, table, values):
    return jnp.einsum(form, table, values, preferred_element_type=jnp.float32)


def twist(real_part, imag_part, cosine, sine, axis):
    return jnp.stack(
        [real_part * cosine - imag_part * sine, real_part * sine + imag_part * cosine], axis=axis
    ).astype(jnp.bfloat16)


def rows_forward(values, tables):
    lead_table, sub_table, cosine, sine = tables
    batch, parts, count, length = values.shape
    view = values.reshape(batch, parts, count, lead_table.shape[1], sub_table.shape[1])
    first = factor("pkqj,xqrjb->xprkb", lead_table, view)
    middle = twist(first[:, 0], first[:, 1], cosine, sine, 1)
    second = factor("pkqj,xqraj->xprak", sub_table, middle)
    return second.reshape(batch, parts, count, length) * (1.0 / math.sqrt(length))


def rows_inverse(values, tables):
    lead_table, sub_table, cosine, sine = tables
    batch, parts, count, length = values.shape
    view = values.reshape(batch, parts, count, lead_table.shape[1], sub_table.shape[1])
    first = factor("pkqj,xqraj->xprak", sub_table, view)
    middle = twist(first[:, 0], first[:, 1], cosine, sine, 1)
    second = factor("pkqj,xqrjb->xprkb", lead_table, middle)
    return second.reshape(batch, parts, count, length) * (1.0 / math.sqrt(length))


def cols_forward(values, tables):
    lead_table, sub_table, cosine, sine = tables
    parts, length, width = values.shape
    view = values.reshape(parts, lead_table.shape[1], sub_table.shape[1], width)
    first = factor("pkqj,qjbw->pkbw", lead_table, view)
    middle = twist(first[0], first[1], cosine[:, :, None], sine[:, :, None], 0)
    second = factor("pkqj,qajw->pakw", sub_table, middle)
    return second.reshape(parts, length, width) * (1.0 / math.sqrt(length))


def cols_inverse(values, tables):
    lead_table, sub_table, cosine, sine = tables
    parts, length, width = values.shape
    view = values.reshape(parts, lead_table.shape[1], sub_table.shape[1], width)
    first = factor("pkqj,qajw->pakw", sub_table, view)
    middle = twist(first[0], first[1], cosine[:, :, None], sine[:, :, None], 0)
    second = factor("pkqj,qjbw->pkbw", lead_table, middle)
    return second.reshape(parts, length, width) * (1.0 / math.sqrt(length))


def shards(image_field, amplitudes, mask_ids):
    slab = lax.all_gather(image_field, "mask", axis=1, tiled=True)
    slab_rows = slab.shape[1]
    width = slab.shape[2]
    outer = width // INNER
    forward_cos, forward_sin = turn_table(outer, INNER, width, -1.0)
    inverse_cos, inverse_sin = turn_table(outer, INNER, width, 1.0)
    forward_tables = (
        factor_table(outer, -1.0),
        factor_table(INNER, -1.0),
        forward_cos,
        forward_sin,
    )
    inverse_tables = (factor_table(outer, 1.0), factor_table(INNER, 1.0), inverse_cos, inverse_sin)
    first_row = lax.axis_index("rows") * slab_rows
    row_index = first_row + jnp.arange(slab_rows, dtype=jnp.int32)[:, None]
    column_index = jnp.arange(width, dtype=jnp.int32)[None, :]
    phase_code = mask_code(mask_ids[0], row_index, column_index)
    masked_real, masked_imag = rotate(
        slab[0].astype(jnp.float32), slab[1].astype(jnp.float32), phase_code, 1.0
    )
    masked = jnp.stack([masked_real, masked_imag]).astype(jnp.bfloat16)
    outgoing = rows_forward(masked[None], forward_tables)[0].astype(jnp.bfloat16)
    column_slab = lax.all_to_all(outgoing, "rows", split_axis=2, concat_axis=1, tiled=True)
    spectrum = cols_forward(column_slab, forward_tables)
    spec_real = spectrum[0]
    spec_imag = spectrum[1]
    measured = amplitudes[0].astype(jnp.float32)
    magnitude = jnp.sqrt(spec_real * spec_real + spec_imag * spec_imag + EPSILON)
    factor_kept = 1.0 - measured / magnitude
    misfit = magnitude - measured
    loss_part = jnp.sum(misfit * misfit)
    weighted = jnp.stack([spec_real * factor_kept, spec_imag * factor_kept]).astype(jnp.bfloat16)
    returning = cols_inverse(weighted, inverse_tables).astype(jnp.bfloat16)
    row_slab = lax.all_to_all(returning, "rows", split_axis=1, concat_axis=2, tiled=True)
    back = rows_inverse(row_slab[None], inverse_tables)[0]
    term_real, term_imag = rotate(back[0], back[1], phase_code, -1.0)
    gradient = lax.psum_scatter(
        jnp.stack([term_real, term_imag]).astype(jnp.bfloat16),
        "mask",
        scatter_dimension=1,
        tiled=True,
    ).astype(jnp.float32)
    loss_total = lax.psum(loss_part, ("rows", "mask"))
    loss_value = loss_total / (lax.axis_size("mask") * width * width)
    return (gradient, loss_value)


def solution(mesh):
    return jax.shard_map(
        shards,
        mesh=mesh,
        in_specs=(P(None, ("rows", "mask"), None), P("mask", None, "rows"), P("mask")),
        out_specs=(P(None, ("rows", "mask"), None), P()),
        check_vma=False,
    )
```

profile of v0, /device:TPU:1, one launch (start us, length us, event | category | flops | bytes accessed | tf_op | source)
XLA Modules:
  0.0 996.1 jit_solution(3554799397838370587)
XLA Ops:
  10.1 98.1 %all-gather.2.cloned.1.call-done = bf16[2,256,8192]{2,1,0:T(8,128)(2,1)} async-done(((bf16[2,32,8192]{2,1,0:T(8,128)(2,1)}), bf16[2,256,8192]{2,1,0:T(8,128)(2,1)}) %all-gather.2.cloned.1.call-update) | async-done | bytes 8388624 | tf_op jit(solution)/shard_map/all_gather | solution.py:108
  108.2 9.7 fusion.49
  133.0 6.2 maximum_bitcast_fusion.2
  139.2 16.8 %fusion.41 = bf16[1,2,256,64,128]{2,4,1,3,0:T(8,128)(2,1)} fusion(bf16[2,256,64,128,1]{3,2,1,0,4:T(8,128)(2,1)} %maximum_bitcast_fusion.2, bf16[1,128,2,128]{3,1,2,0:T(8,128)(2,1)S(1)} %get-tuple-element.21, bf16[1,128,2,128]{3,1,2,0:T(8,128)(2,1)S(1)} %get-tuple-element.22), kind=kOutput, calls=%fused_computation.77 | convolution fusion | flops 2156134400 | bytes 16908288 | tf_op jit(solution)/shard_map/pkqj,xqraj->xprak/dot_general | solution.py:58
  156.0 7.7 copy.71
  163.7 16.4 %copy.72 = bf16[2,256,8192]{1,0,2:T(2,128)(2,1)} copy(bf16[2,256,8192]{1,2,0:T(8,128)(2,1)} %bitcast.205) | data formatting | bytes 16777216 | tf_op jit(solution)/shard_map/convert_element_type | solution.py:129
  180.1 9.4 all-to-all-start
  190.5 148.9 %all-to-all-done = bf16[2,256,8192]{1,0,2:T(2,128)(2,1)} async-done(((bf16[2,256,8192]{1,0,2:T(2,128)(2,1)}), bf16[2,256,8192]{1,0,2:T(2,128)(2,1)}, u32[]{:S(2)}, u32[]{:S(2)}) %all-to-all-start) | async-done | bytes 8388640 | tf_op jit(solution)/shard_map/all_to_all | solution.py:130
  339.4 7.7 copy.73
  347.1 12.0 %copy.74 = bf16[2,32,256,256]{3,2,1,0:T(8,128)(2,1)} copy(bf16[2,32,256,256]{2,3,1,0:T(8,128)(2,1)} %bitcast.206) | data formatting | bytes 16777216 | tf_op jit(solution)/shard_map/all_to_all | solution.py:130
  359.1 9.7 fusion.36
  374.2 6.2 maximum_bitcast_fusion.3
  380.4 10.0 %fusion.2 = f32[2,64,128,256]{3,2,0,1:T(8,128)S(1)} fusion(bf16[2,64,128,256,1]{3,1,2,0,4:T(8,128)(2,1)} %maximum_bitcast_fusion.3, bf16[1,128,2,128]{3,1,2,0:T(8,128)(2,1)S(1)} %get-tuple-element.21, bf16[1,128,2,128]{3,1,2,0:T(8,128)(2,1)S(1)} %get-tuple-element.22), kind=kOutput, calls=%fused_computation.5 | convolution fusion | flops 2151940096 | bytes 25296896 | tf_op jit(solution)/shard_map/pkqj,qajw->pakw/dot_general | solution.py:58
  390.4 6.6 fusion.97
  397.0 12.9 %fusion.10 = (f32[]{:T(128)}, bf16[1,8192,256]{2,1,0:T(8,128)(2,1)}, bf16[1,8192,256]{2,1,0:T(8,128)(2,1)}) fusion(bf16[1,8192,256]{2,1,0:T(8,128)(2,1)S(1)} %copy-done, f32[1,8192,256]{2,1,0:T(8,128)} %bitcast.211, f32[1,8192,256]{2,1,0:T(8,128)} %bitcast.210), kind=kLoop, calls=%fused_computation.24 | loop fusion | flops 29360128 | bytes 29360132 | tf_op jit(solution)/shard_map/reduce_sum | solution.py:138
  409.8 6.4 copy.80
  416.2 6.4 copy.79
  422.7 11.6 %convolution_bitcast_fusion.1 = f32[64,256,2,128]{3,1,2,0:T(8,128)} fusion(bf16[1,64,128,256]{2,3,0,1:T(8,128)(2,1)} %copy.80, bf16[1,64,128,256]{2,3,0,1:T(8,128)(2,1)} %copy.79, bf16[1,128,2,128]{3,1,2,0:T(8,128)(2,1)S(1)} %get-tuple-element.20, bf16[1,128,2,128]{3,1,2,0:T(8,128)(2,1)S(1)} %get-tuple-element.19), kind=kOutput, calls=%fused_computation.17 | convolution fusion | flops 2164523008 | bytes 25296896 | tf_op jit(solution)/shard_map/pkqj,qajw->pakw/dot_general | solution.py:58
  434.2 17.4 %copy.81 = f32[64,256,2,128]{1,0,3,2:T(8,128)} copy(f32[64,256,2,128]{3,1,2,0:T(8,128)} %convolution_bitcast_fusion.1) | data formatting | bytes 33554432 | tf_op jit(solution)/shard_map/pkqj,qajw->pakw/dot_general | solution.py:58
  451.7 7.9 subtract_convert_fusion.2
  464.5 11.4 %copy.84 = bf16[2,64,128,256]{3,2,1,0:T(8,128)(2,1)} copy(bf16[2,64,128,256]{3,1,2,0:T(8,128)(2,1)} %fusion.1) | data formatting | bytes 16777216 | tf_op jit(solution)/shard_map/convert_element_type | solution.py:140
  475.9 14.5 %copy.85 = bf16[2,8192,256]{2,0,1:T(2,128)(2,1)S(1)} copy(bf16[2,8192,256]{2,1,0:T(8,128)(2,1)} %bitcast.207) | data formatting | bytes 16777216 | tf_op jit(solution)/shard_map/convert_element_type | solution.py:140
  490.4 167.5 %all_to_all.30 = bf16[2,8192,256]{2,0,1:T(2,128)(2,1)} all-to-all(bf16[2,8192,256]{2,0,1:T(2,128)(2,1)S(1)} %copy.85), channel_id=1, replica_groups=mesh['rows'=32,'mask'=8] {'rows'}, dimensions={1} | all-to-all | bytes 16777216 | tf_op jit(solution)/shard_map/all_to_all | solution.py:141
  657.9 7.7 copy.86
  665.6 12.0 %copy.87 = bf16[2,256,32,256]{1,3,2,0:T(8,128)(2,1)} copy(bf16[2,256,32,256]{3,1,2,0:T(8,128)(2,1)} %bitcast.208) | data formatting | bytes 16777216 | tf_op jit(solution)/shard_map/all_to_all | solution.py:141
  677.6 12.0 %copy.105 = bf16[2,256,64,128,1]{3,2,0,1,4:T(8,128)(2,1)} copy(bf16[2,256,64,128,1]{1,3,2,0,4:T(8,128)(2,1)} %bitcast.209) | data formatting | bytes 16777216 | tf_op jit(solution)/shard_map/reshape.18
  697.6 7.1 fusion
  704.7 20.0 %mul.910 = f32[1,2,256,8192]{3,1,2,0:T(2,128)} reshape(f32[1,2,256,64,128]{4,3,1,2,0:T(8,128)} %fusion) | data formatting | bytes 33554432 | tf_op jit(solution)/shard_map/mul | solution.py:84
  724.7 21.0 %fusion.96 = (f32[1,1,256,8192]{3,1,2,0:T(1,128)S(1)}, f32[1,1,256,8192]{3,1,2,0:T(1,128)}) fusion(f32[1,2,256,8192]{3,1,2,0:T(2,128)} %mul.910), kind=kLoop, calls=%fused_computation.162 | loop fusion | bytes 33554432 | tf_op jit(solution)/shard_map/slice | solution.py:143
  745.8 20.7 %subtract_convert_fusion = (bf16[1,256,8192]{2,1,0:T(8,128)(2,1)S(1)}, bf16[1,256,8192]{2,1,0:T(8,128)(2,1)}) fusion(f32[1,1,256,8192]{3,1,2,0:T(1,128)} %get-tuple-element.14, f32[1,1,256,8192]{3,1,2,0:T(1,128)S(1)} %get-tuple-element.13, s32[]{:T(128)} %bitcast.8, s32[8192]{0:T(1024)S(1)} %copy-done.2, s32[256]{0:T(256)S(1)} %copy-done.4), kind=kLoop, calls=%fused_computation.58 | loop fusion | flops 58720256 | bytes 25199620 | tf_op jit(solution)/shard_map/convert.1
  766.5 6.2 pad_maximum_fusion.1
  772.7 211.5 %psum.7 = f32[]{:T(128)} all-reduce(f32[]{:T(128)} %get-tuple-element.2), channel_id=1, replica_groups=mesh['rows'=32,'mask'=8] {'rows','mask'}, use_global_device_ids=true, to_apply=%region_2.3 | all-reduce | flops 1 | bytes 8 | tf_op jit(solution)/shard_map/psum | solution.py:150
  (40 shorter events, 39.1 us)
Async XLA Ops:
  7.2 101.0 %all-gather.2.cloned.1.call-start = ((), (), s32[]{:S(2)}) async-start(), calls=%async_computation.3 | async-start | bytes 9437184 | tf_op jit(solution)/shard_map/all_gather | solution.py:108
  8.6 109.4 %copy-start.3 = (s32[256]{0:T(256)}, s32[256]{0:T(256)S(1)}, u32[]{:S(2)}) copy-start(s32[256]{0:T(256)S(1)} %add_multiply_fusion) | copy-start | bytes 3076
  9.0 108.9 %copy-start.1 = (s32[8192]{0:T(1024)}, s32[8192]{0:T(1024)S(1)}, u32[]{:S(2)}) copy-start(s32[8192]{0:T(1024)S(1)} %iota_multiply_fusion) | copy-start | bytes 98308
  180.1 159.3 %all-to-all-start = ((bf16[2,256,8192]{1,0,2:T(2,128)(2,1)}), bf16[2,256,8192]{1,0,2:T(2,128)(2,1)}, u32[]{:S(2)}, u32[]{:S(2)}) async-start(bf16[2,256,8192]{1,0,2:T(2,128)(2,1)} %copy.72), calls=%async_computation | async-start | bytes 16777216 | tf_op jit(solution)/shard_map/all_to_all | solution.py:130
  189.6 795.3 %reduce-scatter.2.cloned.1.call-start = ((), (), s32[]{:S(2)}) async-start(), calls=%async_computation.4 | async-start | bytes 9437184 | tf_op jit(solution)/shard_map/reduce_scatter | solution.py:144
  390.4 6.6 copy-start
  724.7 21.1 %copy-start.2 = (s32[8192]{0:T(1024)S(1)}, s32[8192]{0:T(1024)}, u32[]{:S(2)}) copy-start(s32[8192]{0:T(1024)} %copy-done.1) | copy-start | bytes 98308
  724.7 21.1 %copy-start.4 = (s32[256]{0:T(256)S(1)}, s32[256]{0:T(256)}, u32[]{:S(2)}) copy-start(s32[256]{0:T(256)} %copy-done.3) | copy-start | bytes 3076
Sparse Core Ops, SparseCore 0:
  9.8 98.3 all-gather.1
  772.8 152.2 reduce-scatter.1
where the time goes:
time: 1010 us; the launch traced here: 996 us
  blocking collectives  379 us (38%)
  waiting for transfers between devices  248 us (25%)
  local copies, waits for them, and re-layouts  184 us (18%)
  other arithmetic  88.1 us (9%)
  matrix products  70.1 us (7%)
  between operations  17.2 us (2%)
    psum x1, blocking collectives, shards(): loss_total = lax.psum(loss_part, ('rows', 'mask'))  212 us
    all_to_all x1, blocking collectives, shards(): lax.all_to_all(returning, 'rows', split_axis=1, concat_axis=2, tiled=True)  168 us
    all_to_all x1, waiting for transfers between devices, shards(): lax.all_to_all(outgoing, 'rows', split_axis=2, concat_axis=1, tiled=True)  149 us
    all_gather x1, waiting for transfers between devices, shards(): slab = lax.all_gather(image_field, 'mask', axis=1, tiled=True)  98.1 us
    dot_general x8, matrix products, factor(): return jnp.einsum(form, table, values, preferred_element_type=jnp.float32)  70.1 us
    another operation x9, other arithmetic  35.3 us
    convert_element_type x2, local copies, waits for them, and re-layouts, shards(): returning = cols_inverse(weighted, inverse_tables).astype(jnp.bfloat16)  25.9 us
    convert_element_type x2, local copies, waits for them, and re-layouts, shards(): rows_forward(masked[None], forward_tables)[0].astype(jnp.bfloat16)  24.1 us
  transfers between devices with their start and end apart: 3, of which 2 were waited for; matrix products, arithmetic and copies ran while one was open for 0% of the time, Pallas kernels for 0%

commit v1 on v0

v1 whole, which is shorter than its diff:
```python
import functools
import math

import jax
import jax.numpy as jnp
import ml_dtypes
import numpy as np
from jax import lax
from jax.experimental import pallas as pl
from jax.experimental.pallas import tpu as pltpu
from jax.sharding import Mesh
from jax.sharding import PartitionSpec as P

N = 8192
LEAD = 64
SUB = 128
SLAB = 32
STRIDE = 136
EPSILON = 0.25
CHUNKS = 2
ROW_PRIME, COLUMN_PRIME, MASK_PRIME, MIX_PRIME = 73856093, 19349663, 83492791, 1274126177
BF16 = jnp.bfloat16
F32 = jnp.float32


def rounded(values):
    return values.astype(ml_dtypes.bfloat16).astype(np.float32)


def unit_table(outputs, inputs, length, direction):
    angles = (outputs[:, None] * inputs[None, :] % length) * (2.0 * math.pi / length)
    return np.cos(angles), direction * np.sin(angles)


def block_form(real_part, imag_part):
    return np.block([[real_part, -imag_part], [imag_part, real_part]])


def orders():
    x, core, jh, b = np.meshgrid(np.arange(4), np.arange(2), np.arange(2), np.arange(4), indexing="ij")
    k1 = (x * 16 + b * 4 + core * 2 + jh).reshape(-1)
    x, core, zh, zl = np.meshgrid(np.arange(4), np.arange(2), np.arange(4), np.arange(2), indexing="ij")
    n1 = (x * 16 + zh * 4 + core * 2 + zl).reshape(-1)
    return k1, n1


def tables():
    k1_order, n1_order = orders()
    lead, sub = np.arange(LEAD), np.arange(SUB)
    out = {}
    lanes = np.arange(256)
    half, part, low = lanes // 128, (lanes // 64) % 2, lanes % 64
    split = part * 128 + half * 64 + low
    for name, direction in (("forward", -1.0), ("inverse", 1.0)):
        sub_full = block_form(*map(rounded, unit_table(sub, sub, SUB, direction)))
        out[name + "_sub"] = sub_full.astype(ml_dtypes.bfloat16)
        if name == "forward":
            row_lead = block_form(*map(rounded, unit_table(k1_order, lead, LEAD, direction)))
            row_sub = sub_full.T[:, split]
            turn = unit_table(k1_order, sub, N, direction)
            col = tuple(map(rounded, unit_table(lead, n1_order, LEAD, direction)))
        else:
            row_lead = block_form(*map(rounded, unit_table(lead, k1_order, LEAD, direction)))
            row_sub = sub_full.T[split, :]
            turn = tuple(np.repeat(t, 8, axis=0) for t in unit_table(k1_order, sub, N, direction))
            col = tuple(map(rounded, unit_table(n1_order, lead, LEAD, direction)))
        out[name + "_row_lead"] = row_lead.astype(ml_dtypes.bfloat16)
        out[name + "_row_sub"] = row_sub.astype(ml_dtypes.bfloat16)
        out[name + "_turn"] = np.stack(turn).astype(np.float32)
        col_plain = block_form(*col).astype(np.float32)
        col_quarter = block_form(-col[1], col[0]).astype(np.float32)
        out[name + "_col"] = np.stack([col_plain, col_quarter])
        twist = unit_table(sub, np.concatenate([lead, lead]), N, direction)
        out[name + "_col_turn"] = np.stack(twist).astype(np.float32)
    return out


def column_tables(table, name):
    plain, quarter = table[name + "_col"]
    cosine, sine = table[name + "_col_turn"]
    plain, quarter, cosine, sine = map(jnp.asarray, (plain, quarter, cosine, sine))
    if name == "forward":
        cosine, sine = cosine[:, :, None], sine[:, :, None]
    else:
        cosine, sine = cosine[:, None, :], sine[:, None, :]
    return (plain[None] * cosine + quarter[None] * sine).astype(BF16)


def phase_code(hashed_columns, row_term):
    mixed = hashed_columns ^ row_term
    mixed = mixed ^ lax.shift_right_logical(mixed, jnp.int32(13))
    mixed = mixed * jnp.int32(MIX_PRIME)
    mixed = mixed ^ lax.shift_right_logical(mixed, jnp.int32(16))
    return lax.shift_right_logical(mixed, jnp.int32(28))


def column_hash():
    shape = (LEAD, SUB)
    column = lax.broadcasted_iota(jnp.int32, shape, 0) * SUB + lax.broadcasted_iota(jnp.int32, shape, 1)
    return column * jnp.int32(COLUMN_PRIME)


def quarter_turn(real_part, imag_part, code, forward):
    odd = (code & 1) == 1
    first = jnp.where(odd, imag_part, real_part)
    second = jnp.where(odd, real_part, imag_part)
    high = (code & 2) == 2
    mixed = ((code ^ lax.shift_right_logical(code, jnp.int32(1))) & 1) == 1
    flip_real, flip_imag = (mixed, high) if forward else (high, mixed)
    return jnp.where(flip_real, -first, first), jnp.where(flip_imag, -second, second)


def row_forward_kernel(first_row, scalars, image, lead_table, sub_table, turn, out, swap):
    count = image.shape[2]
    columns = column_hash()

    def body(r, carry):
        stacked = []
        for zs in range(8):
            row = scalars[zs] + first_row + r
            code = phase_code(columns, (row * jnp.int32(ROW_PRIME)) ^ scalars[8])
            real_part, imag_part = image[zs, 0, r].astype(F32), image[zs, 1, r].astype(F32)
            real_part, imag_part = quarter_turn(real_part, imag_part, code, True)
            stacked.append(jnp.concatenate([real_part, imag_part], axis=0).astype(BF16))
        first = jnp.dot(lead_table[...], jnp.concatenate(stacked, axis=1), preferred_element_type=F32)
        cosine, sine = turn[0], turn[1]
        middle = []
        for zs in range(8):
            real_part, imag_part = first[:LEAD, zs * 128 : zs * 128 + 128], first[LEAD:, zs * 128 : zs * 128 + 128]
            turned = [real_part * cosine - imag_part * sine, real_part * sine + imag_part * cosine]
            middle.append(jnp.concatenate(turned, axis=1).astype(BF16))
        second = jnp.dot(jnp.concatenate(middle, axis=0), sub_table[...], preferred_element_type=F32)
        for zs in range(8):
            for half in range(2):
                swap[half, pl.ds(zs, LEAD, stride=8), :] = second[zs * LEAD : (zs + 1) * LEAD, half * 128 : half * 128 + 128]
        for x in range(4):
            for core in range(2):
                for jh in range(2):
                    at = ((x * 2 + core) * 2 + jh) * 32
                    for half in range(2):
                        out[(x * 4 + jh * 2 + half) * 2 + core, r] = swap[half, at : at + 32, :].astype(BF16)
        return carry

    lax.fori_loop(0, count, body, 0)


def row_inverse_kernel(first_row, scalars, field, lead_table, sub_table, turn, out, swap):
    count = field.shape[1]
    columns = column_hash()

    def body(r, carry):
        blocks = []
        for x in range(4):
            for core in range(2):
                for jh in range(2):
                    pair = [field[(x * 4 + jh * 2 + half) * 2 + core, r] for half in range(2)]
                    blocks.append(jnp.concatenate(pair, axis=1))
        first = jnp.dot(jnp.concatenate(blocks, axis=0), sub_table[...], preferred_element_type=F32)
        real_part, imag_part = first[:, :128], first[:, 128:]
        cosine, sine = turn[0], turn[1]
        swap[0] = real_part * cosine - imag_part * sine
        swap[1] = real_part * sine + imag_part * cosine
        middle = []
        for zs in range(8):
            parts = [swap[part, pl.ds(zs, LEAD, stride=8), :] for part in range(2)]
            middle.append(jnp.concatenate(parts, axis=0).astype(BF16))
        second = jnp.dot(lead_table[...], jnp.concatenate(middle, axis=1), preferred_element_type=F32)
        second = second * (1.0 / N)
        for zs in range(8):
            row = scalars[zs] + first_row + r
            code = phase_code(columns, (row * jnp.int32(ROW_PRIME)) ^ scalars[8])
            real_part, imag_part = second[:LEAD, zs * 128 : zs * 128 + 128], second[LEAD:, zs * 128 : zs * 128 + 128]
            real_part, imag_part = quarter_turn(real_part, imag_part, code, False)
            out[zs, 0, r] = real_part.astype(BF16)
            out[zs, 1, r] = imag_part.astype(BF16)
        return carry

    lax.fori_loop(0, count, body, 0)


def pair_up(first, second, low):
    return jnp.where(low, first, pltpu.roll(second, 64, 1)), jnp.where(low, pltpu.roll(first, 64, 1), second)


def pack_kernel(place, amplitudes, *outs):
    for shift, out in enumerate(outs):
        piece = lax.rem(place[0] + shift, 4)
        lanes = pl.ds(pl.multiple_of(piece // 2 * 128, 128), 128)
        upper, lower = amplitudes[0, :, lanes].astype(F32), amplitudes[1, :, lanes].astype(F32)
        low = lax.broadcasted_iota(jnp.int32, upper.shape, 1) < 64
        left, right = pair_up(upper, lower, low)
        out[...] = jnp.where(lax.rem(piece, 2) == 0, left, right).astype(BF16)


def column_kernel(*refs):
    fields = refs[:CHUNKS]
    place, amplitudes, forward_lead, inverse_lead, forward_sub, inverse_sub = refs[CHUNKS : CHUNKS + 6]
    outs = refs[CHUNKS + 6 : 2 * CHUNKS + 6]
    loss, hold = refs[2 * CHUNKS + 6 :]
    count = SLAB // CHUNKS

    for chunk in range(CHUNKS):

        def forward(step, carry, chunk=chunk):
            y, r = step // count, lax.rem(step, count)
            at = y * SLAB + chunk * count + r
            low = lax.broadcasted_iota(jnp.int32, (8, 128), 1) < 64
            parts = [[[], []], [[], []]]
            for x in range(4):
                for core in range(2):
                    block = fields[chunk][(x * 4 + y) * 2 + core, r].astype(F32)
                    for pair in range(2):
                        real_part, imag_part = pair_up(block[pair * 16 : pair * 16 + 8], block[pair * 16 + 8 : pair * 16 + 16], low)
                        parts[0][pair].append(real_part)
                        parts[1][pair].append(imag_part)
            stacked = jnp.concatenate(
                [jnp.concatenate([jnp.concatenate(parts[part][pair], axis=0) for pair in range(2)], axis=1) for part in range(2)], axis=0
            ).astype(BF16)
            result = jnp.dot(forward_lead[at], stacked, preferred_element_type=F32)
            for part in range(2):
                for pair in range(2):
                    hold[part, pair, pl.ds(at, LEAD, stride=STRIDE), :] = result[part * 64 : part * 64 + 64, pair * 128 : pair * 128 + 128]
            return carry

        lax.fori_loop(0, 4 * count, forward, 0, unroll=8)

    loss[...] = jnp.zeros_like(loss)

    def middle(k1_low, carry):
        low = lax.broadcasted_iota(jnp.int32, (SUB, 128), 1) < 64
        measured = [[], []]
        for pair in range(2):
            first, second = (amplitudes[lax.rem(place[0] + 4 - b, 4), k1_low].astype(F32) for b in (pair * 2, pair * 2 + 1))
            for high, values in enumerate(pair_up(first, second, low)):
                measured[high].append(values)
        places = [pl.ds(pl.multiple_of((k1_low + high * 32) * STRIDE, 8), SUB) for high in range(2)]
        stacked = [
            jnp.concatenate(
                [jnp.concatenate([hold[part, pair, at, :].astype(BF16) for pair in range(2)], axis=1) for part in range(2)], axis=0
            )
            for at in places
        ]
        spectra = [jnp.dot(forward_sub[...], values, preferred_element_type=F32) for values in stacked]
        weighted, total = [], 0.0
        for spectrum, values in zip(spectra, measured):
            real_part, imag_part = spectrum[:SUB] * (1.0 / N), spectrum[SUB:] * (1.0 / N)
            amplitude = jnp.concatenate(values, axis=1)
            squared = real_part * real_part + imag_part * imag_part + EPSILON
            inverse = lax.rsqrt(squared)
            kept = 1.0 - amplitude * inverse
            misfit = squared * inverse - amplitude
            total = total + jnp.sum((misfit * misfit).reshape(SUB // 8, 8, 256), axis=0)
            weighted.append(jnp.concatenate([(real_part * kept).astype(BF16), (imag_part * kept).astype(BF16)], axis=0))
        results = [jnp.dot(inverse_sub[...], values, preferred_element_type=F32) for values in weighted]
        loss[...] += total
        for at, result in zip(places, results):
            for part in range(2):
                for pair in range(2):
                    hold[part, pair, at, :] = result[part * SUB : part * SUB + SUB, pair * 128 : pair * 128 + 128]
        return carry

    lax.fori_loop(0, 32, middle, 0, unroll=2)

    for chunk in range(CHUNKS):

        def inverse(step, carry, chunk=chunk):
            y, r = step // count, lax.rem(step, count)
            at = y * SLAB + chunk * count + r
            low = lax.broadcasted_iota(jnp.int32, (8, 128), 1) < 64
            stacked = jnp.concatenate(
                [jnp.concatenate([hold[part, pair, pl.ds(at, LEAD, stride=STRIDE), :] for pair in range(2)], axis=1) for part in range(2)],
                axis=0,
            ).astype(BF16)
            result = jnp.dot(inverse_lead[at], stacked, preferred_element_type=F32)
            for x in range(4):
                for core in range(2):
                    row = (x * 2 + core) * 8
                    block = []
                    for pair in range(2):
                        real_part = result[row : row + 8, pair * 128 : pair * 128 + 128]
                        imag_part = result[64 + row : 64 + row + 8, pair * 128 : pair * 128 + 128]
                        block.extend(pair_up(real_part, imag_part, low))
                    outs[chunk][(x * 4 + y) * 2 + core, r] = jnp.concatenate(block, axis=0).astype(BF16)
            return carry

        lax.fori_loop(0, 4 * count, inverse, 0, unroll=8)


VMEM = pl.BlockSpec(memory_space=pltpu.VMEM)
SMEM = pl.BlockSpec(memory_space=pltpu.SMEM)


def params(mib):
    return pltpu.CompilerParams(vmem_limit_bytes=mib * 2**20)


def cost(flops, moved):
    return pl.CostEstimate(flops=flops, bytes_accessed=moved, transcendentals=0)


def row_forward(table, first_row, scalars, image):
    count = image.shape[2]
    return pl.pallas_call(
        functools.partial(row_forward_kernel, first_row),
        out_shape=jax.ShapeDtypeStruct((32, count, 32, 128), BF16),
        in_specs=[SMEM] + [VMEM] * 4,
        out_specs=VMEM,
        scratch_shapes=[pltpu.VMEM((2, 512, 128), F32)],
        compiler_params=params(40),
        cost_estimate=cost(count * 10**9, count * 2**19),
        name="row_forward",
    )(scalars, image, table["forward_row_lead"], table["forward_row_sub"], table["forward_turn"])


def row_inverse(table, first_row, scalars, field):
    count = field.shape[1]
    return pl.pallas_call(
        functools.partial(row_inverse_kernel, first_row),
        out_shape=jax.ShapeDtypeStruct((8, 2, count, LEAD, SUB), BF16),
        in_specs=[SMEM] + [VMEM] * 4,
        out_specs=VMEM,
        scratch_shapes=[pltpu.VMEM((2, 512, 128), F32)],
        compiler_params=params(40),
        cost_estimate=cost(count * 10**9, count * 2**19),
        name="row_inverse",
    )(scalars, field, table["inverse_row_lead"], table["inverse_row_sub"], table["inverse_turn"])


def pack(place, amplitudes):
    rows = N // 2
    step = 512
    return pl.pallas_call(
        pack_kernel,
        grid=(rows // step,),
        out_shape=[jax.ShapeDtypeStruct((rows, 128), BF16)] * 4,
        in_specs=[SMEM, pl.BlockSpec((2, step, 256), lambda i: (0, i, 0))],
        out_specs=[pl.BlockSpec((step, 128), lambda i: (i, 0))] * 4,
        cost_estimate=cost(10**7, 2**23),
        name="pack",
    )(place, amplitudes.reshape(2, rows, 256))


def columns(table, fields, place, amplitudes, forward_lead, inverse_lead):
    count = SLAB // CHUNKS
    result = pl.pallas_call(
        column_kernel,
        out_shape=[jax.ShapeDtypeStruct((32, count, 32, 128), BF16)] * CHUNKS + [jax.ShapeDtypeStruct((8, 256), F32)],
        in_specs=[VMEM] * CHUNKS + [SMEM] + [VMEM] * 5,
        out_specs=[VMEM] * (CHUNKS + 1),
        scratch_shapes=[pltpu.VMEM((2, 2, LEAD * STRIDE, 128), F32)],
        compiler_params=params(58),
        cost_estimate=cost(40 * 10**9, 2**25),
        name="columns",
    )(*fields, place, amplitudes, forward_lead, inverse_lead, table["forward_sub"], table["inverse_sub"])
    return result[:-1], result[-1]


def shift_by(piece, axis, shift):
    return piece if shift == 0 else lax.ppermute(piece, axis, [(i, (i + shift) % 4) for i in range(4)])


def fold(value, axis, distance):
    return value + lax.ppermute(value, axis, [(i, i ^ distance) for i in range(lax.axis_size(axis))])


def shards(table, image_field, amplitudes, mask_ids):
    plane = ("x", "y", "core")
    x, zh, core, zl, y = (lax.axis_index(name) for name in ("x", "zh", "core", "zl", "y"))
    swap = [(a * 4 + b, b * 4 + a) for a in range(4) for b in range(4)]
    mask_term = (lax.ppermute(mask_ids, ("zh", "y"), swap) + 1) * jnp.int32(MASK_PRIME)
    zs = jnp.arange(8, dtype=jnp.int32)
    first_rows = (((x * 4 + zs // 2) * 2 + core) * 8 + zs % 2 * 4 + y) * SLAB
    scalars = jnp.concatenate([first_rows.astype(jnp.int32), mask_term])
    count = SLAB // CHUNKS

    image = image_field.reshape(2, SLAB, LEAD, SUB)
    slabs = [lax.all_gather(image[:, c * count : (c + 1) * count], ("zh", "zl"), axis=0) for c in range(CHUNKS)]

    packed = pack(y[None].astype(jnp.int32), amplitudes)
    spread = [shift_by(piece, "y", s) for s, piece in enumerate(packed)]
    spread, slabs[0] = lax.optimization_barrier((spread, slabs[0]))
    spread = jnp.stack(spread)
    sent = [row_forward(table, 0, scalars, slabs[0])]
    fields = [lax.all_to_all(sent[0], plane, 0, 0, tiled=True)]
    spread, slabs[-1], fields[0] = lax.optimization_barrier((spread, slabs[-1], fields[0]))
    packed = [lax.dynamic_index_in_dim(spread, lax.rem(y - zh - t + 8, 4), 0, False) for t in range(4)]
    packed = jnp.stack([shift_by(piece, "zh", t) for t, piece in enumerate(packed)])
    packed = packed.reshape(4, 32, SUB, 128)
    forward_lead = column_tables(table, "forward")
    inverse_lead = column_tables(table, "inverse")
    sent.extend(row_forward(table, c * count, scalars, slabs[c]) for c in range(1, CHUNKS))
    fields.extend(lax.all_to_all(piece, plane, 0, 0, tiled=True) for piece in sent[1:])
    returned, loss = columns(table, fields, zh[None].astype(jnp.int32), packed, forward_lead, inverse_lead)
    loss_total = jnp.sum(loss).reshape(1)
    for axis, distance in (("zl", 1), ("zh", 1), ("zh", 2), ("core", 1), ("x", 1), ("x", 2), ("y", 1), ("y", 2)):
        loss_total = fold(loss_total, axis, distance)
    pieces = []
    returned = list(returned)
    for c in range(CHUNKS):
        back = lax.all_to_all(returned[c], plane, 0, 0, tiled=True)
        if c == 0:
            loss_total, back, returned[1:] = lax.optimization_barrier((loss_total, back, returned[1:]))
        term = row_inverse(table, c * count, scalars, back)
        pieces.append(lax.psum_scatter(term, ("zh", "zl"), scatter_dimension=0, tiled=False))
    gradient = jnp.concatenate(pieces, axis=1).astype(F32).reshape(2, SLAB, N)
    return gradient, loss_total[0] / (8 * N * N)


def solution(mesh):
    fine = Mesh(mesh.devices.reshape(4, 4, 2, 2, 4), ("x", "zh", "core", "zl", "y"))
    rows, mask = ("x", "zh", "core"), ("zl", "y")
    return jax.shard_map(
        functools.partial(shards, tables()),
        mesh=fine,
        in_specs=(P(None, rows + mask, None), P(mask, None, rows), P(mask)),
        out_specs=(P(None, rows + mask, None), P()),
        check_vma=False,
    )
```

time: 1010 us -> 535 us (0.53); the launches traced: 996 us -> 534 us
  blocking collectives: 379 us -> 60.7 us
  local copies, waits for them, and re-layouts: 184 us -> 20.4 us
  starting transfers between devices: 9.93 us -> 110 us
  Pallas kernels: 0 us -> 93.4 us
  other arithmetic: 88.1 us -> 15.5 us
  matrix products: 70.1 us -> 0 us
  waiting for transfers between devices: 248 us -> 213 us
    psum x1 -> x0, blocking collectives: 212 us -> none  [shards(): loss_total = lax.psum(loss_part, ('rows', 'mask'))]
    all_to_all x1 -> x3, waiting for transfers between devices: 149 us -> 18.6 us  [the longest x1 18.6 us: shards(): fields = [lax.all_to_all(sent[0], plane, 0, 0, tiled=True)]]
    ppermute x0 -> x15, waiting for transfers between devices: none -> 109 us  [the longest x6 101 us: shift_by(): lax.ppermute(piece, axis, [(i, (i + shift) % 4) for i in range(4)])]
    all_to_all x1, blocking collectives: 168 us -> 60.7 us  [shards(): back = lax.all_to_all(returned[c], plane, 0, 0, tiled=True)]
    pallas_call x0 -> x6, Pallas kernels: none -> 93.4 us  [the longest x1 43.6 us: columns(): pl.pallas_call(column_kernel, out_shape=[jax.ShapeDtypeStruct((32, count,...]
    dot_general x8 -> x0, matrix products: 70.1 us -> none  [factor(): return jnp.einsum(form, table, values, preferred_element_type=jnp.float32)]
    all_gather x1 -> x2, waiting for transfers between devices: 98.1 us -> 30.7 us  [shards(): lax.all_gather(image[:, c * count:(c + 1) * count], ('zh', 'zl'), axis=0)]
    ppermute x0 -> x15, starting transfers between devices: none -> 67.3 us  [the longest x8 50.3 us: fold(): lax.ppermute(value, axis, [(i, i ^ distance) for i in range(lax.axis_size...]
  transfers between devices with their start and end apart: 3 -> 22, of which waited for: 2 -> 15; matrix products, arithmetic and copies ran while one was open for 0% -> 3% of each run, Pallas kernels for 0% -> 5%
where the time goes in v1:
time: 535 us; the launch traced here: 534 us
  waiting for transfers between devices  213 us (40%)
  starting transfers between devices  110 us (21%)
  Pallas kernels  93.4 us (17%)
  blocking collectives  60.7 us (11%)
  between operations  21.5 us (4%)
  local copies, waits for them, and re-layouts  20.4 us (4%)
  other arithmetic  15.5 us (3%)
    ppermute x6, waiting for transfers between devices, shift_by(): lax.ppermute(piece, axis, [(i, (i + shift) % 4) for i in range(4)])  101 us
    all_to_all x1, blocking collectives, shards(): back = lax.all_to_all(returned[c], plane, 0, 0, tiled=True)  60.7 us
    reduce_scatter x2, waiting for transfers between devices, shards(): lax.psum_scatter(term, ('zh', 'zl'), scatter_dimension=0, tiled=False)  53.7 us
    ppermute x8, starting transfers between devices, fold(): lax.ppermute(value, axis, [(i, i ^ distance) for i in range(lax.axis_size...  50.3 us
    pallas_call x1, Pallas kernels, columns(): pl.pallas_call(column_kernel, out_shape=[jax.ShapeDtypeStruct((32, count,...  43.6 us
    all_gather x2, waiting for transfers between devices, shards(): lax.all_gather(image[:, c * count:(c + 1) * count], ('zh', 'zl'), axis=0)  30.7 us
    all_to_all x1, starting transfers between devices, shards(): back = lax.all_to_all(returned[c], plane, 0, 0, tiled=True)  28 us
    pallas_call x2, Pallas kernels, row_inverse(): pl.pallas_call(functools.partial(row_inverse_kernel, first_row), out_shap...  22.9 us
  transfers between devices with their start and end apart: 22, of which 15 were waited for; matrix products, arithmetic and copies ran while one was open for 3% of the time, Pallas kernels for 5%

profile of v1, /device:TPU:1, one launch (start us, length us, event | category | flops | bytes accessed | tf_op | source)
XLA Modules:
  0.0 534.3 jit_solution(11390079262661486114)
XLA Ops:
  10.6 7.5 %pack.1 = (bf16[4096,128]{1,0:T(8,128)(2,1)}, bf16[4096,128]{1,0:T(8,128)(2,1)}, bf16[4096,128]{1,0:T(8,128)(2,1)}, bf16[4096,128]{1,0:T(8,128)(2,1)}) custom-call(s32[1]{0:T(128)} %bitcast.place, bf16[2,4096,256]{2,1,0:T(8,128)(2,1)} %bitcast.31), custom_call_target="tpu_custom_call" | custom-call | flops 10000000 | bytes 8388608 | tf_op jit(solution)/shard_map/pack/pallas_call | solution.py:332
  20.2 2.6 collective-permute-start.2
  26.3 16.5 %collective-permute-done.1 = bf16[4096,128]{1,0:T(8,128)(2,1)S(1)} collective-permute-done((bf16[4096,128]{1,0:T(8,128)(2,1)}, bf16[4096,128]{1,0:T(8,128)(2,1)S(1)}, u32[]{:S(2)}, u32[]{:S(2)}) %collective-permute-start.1) | collective-permute-done | bytes 1048608 | tf_op jit(solution)/shard_map/ppermute | solution.py:359
  42.8 25.3 %collective-permute-done.2 = bf16[4096,128]{1,0:T(8,128)(2,1)S(1)} collective-permute-done((bf16[4096,128]{1,0:T(8,128)(2,1)}, bf16[4096,128]{1,0:T(8,128)(2,1)S(1)}, u32[]{:S(2)}, u32[]{:S(2)}) %collective-permute-start.2) | collective-permute-done | bytes 1048608 | tf_op jit(solution)/shard_map/ppermute | solution.py:359
  71.2 9.7 %row_forward.2 = bf16[32,16,32,128]{3,2,1,0:T(8,128)(2,1)S(1)} custom-call(s32[9]{0:T(128)S(1)} %pad_add_fusion.scalars, bf16[8,2,16,64,128]{4,3,2,1,0:T(8,128)(2,1)S(1)} %bitcast.30, bf16[128,128]{1,0:T(8,128)(2,1)S(1)} %copy-done.11, bf16[256,256]{1,0:T(8,128)(2,1)S(1)} %copy-done.8, f32[2,64,128]{2,1,0:T(8,128)S(1)} %copy-done.9), custom_call_target="tpu_custom_call" | custom-call | flops 16000000000 | bytes 8388608 | tf_op jit(solution)/shard_map/row_forward/pallas_call | solution.py:303
  82.9 7.3 %all-to-all-start = ((bf16[32,16,32,128]{3,2,1,0:T(8,128)(2,1)}), bf16[32,16,32,128]{3,2,1,0:T(8,128)(2,1)}, u32[]{:S(2)}, u32[]{:S(2)}) async-start(bf16[32,16,32,128]{3,2,1,0:T(8,128)(2,1)} %copy-done.3), calls=%async_computation | async-start | bytes 8388608 | tf_op jit(solution)/shard_map/all_to_all | solution.py:384
  90.2 3.5 pad_maximum_fusion
  93.8 30.1 %all-gather.7.cloned.1.call-done = bf16[16,16,64,128]{3,2,1,0:T(8,128)(2,1)} async-done(((bf16[2,16,64,128]{3,2,1,0:T(8,128)(2,1)}), bf16[16,16,64,128]{3,2,1,0:T(8,128)(2,1)}) %all-gather.7.cloned.1.call-update) | async-done | bytes 4194320 | tf_op jit(solution)/shard_map/all_gather | solution.py:377
  123.9 18.6 %all-to-all-done.refs_0_ = bf16[32,16,32,128]{3,2,1,0:T(8,128)(2,1)} async-done(((bf16[32,16,32,128]{3,2,1,0:T(8,128)(2,1)}), bf16[32,16,32,128]{3,2,1,0:T(8,128)(2,1)}, u32[]{:S(2)}, u32[]{:S(2)}) %all-to-all-start) | async-done | bytes 4194336 | tf_op jit(solution)/shard_map/all_to_all | solution.py:384
  142.4 2.2 copy-done.4
  144.6 9.7 %row_forward.3 = bf16[32,16,32,128]{3,2,1,0:T(8,128)(2,1)S(1)} custom-call(s32[9]{0:T(128)S(1)} %pad_add_fusion.scalars, bf16[8,2,16,64,128]{4,3,2,1,0:T(8,128)(2,1)S(1)} %bitcast.29, bf16[128,128]{1,0:T(8,128)(2,1)S(1)} %copy-done.11, bf16[256,256]{1,0:T(8,128)(2,1)S(1)} %copy-done.8, f32[2,64,128]{2,1,0:T(8,128)S(1)} %copy-done.9), custom_call_target="tpu_custom_call" | custom-call | flops 16000000000 | bytes 8388608 | tf_op jit(solution)/shard_map/row_forward/pallas_call | solution.py:303
  156.3 7.2 %all-to-all-start.1 = ((bf16[32,16,32,128]{3,2,1,0:T(8,128)(2,1)}), bf16[32,16,32,128]{3,2,1,0:T(8,128)(2,1)}, u32[]{:S(2)}, u32[]{:S(2)}) async-start(bf16[32,16,32,128]{3,2,1,0:T(8,128)(2,1)} %copy-done), calls=%async_computation.1 | async-start | bytes 8388608 | tf_op jit(solution)/shard_map/all_to_all | solution.py:392
  163.6 2.6 constant_dynamic-slice_fusion
  166.2 6.1 %collective-permute-start.6 = (bf16[4096,128]{1,0:T(8,128)(2,1)S(1)}, bf16[4096,128]{1,0:T(8,128)(2,1)S(1)}, u32[]{:S(2)}, u32[]{:S(2)}) collective-permute-start(bf16[4096,128]{1,0:T(8,128)(2,1)S(1)} %get-tuple-element.39), channel_id=1, source_target_pairs={{0,48},{16,0},{32,16},{48,32},{1,49},{17,1},{33,17},{49,33},{2,50}... | collective-permute-start | bytes 3145736 | tf_op jit(solution)/shard_map/ppermute | solution.py:359
  173.3 2.3 collective-permute-start.4
  175.6 7.6 %add_convert_fusion = (bf16[128,128,128]{2,1,0:T(8,128)(2,1)}, bf16[128,128,128]{2,1,0:T(8,128)(2,1)}) fusion(f32[128,128]{1,0:T(8,128)S(1)} %copy-done.15, f32[128,128]{1,0:T(8,128)S(1)} %copy-done.16, f32[128,128]{1,0:T(8,128)S(1)} %copy-done.14, f32[128,128]{1,0:T(8,128)S(1)} %copy-done.17, f32[128,128]{1,0:T(8,128)S(1)} %copy-done.18, ...), kind=kLoop, calls=%fused_computation | loop fusion | flops 16777216 | bytes 8847360 | tf_op jit(solution)/shard_map/convert_element_type | solution.py:86
  183.2 41.3 %collective-permute-done.6 = bf16[4096,128]{1,0:T(8,128)(2,1)S(1)} collective-permute-done((bf16[4096,128]{1,0:T(8,128)(2,1)S(1)}, bf16[4096,128]{1,0:T(8,128)(2,1)S(1)}, u32[]{:S(2)}, u32[]{:S(2)}) %collective-permute-start.6) | collective-permute-done | bytes 1048608 | tf_op jit(solution)/shard_map/ppermute | solution.py:359
  224.5 18.2 %collective-permute-done.4 = bf16[4096,128]{1,0:T(8,128)(2,1)S(1)} collective-permute-done((bf16[4096,128]{1,0:T(8,128)(2,1)S(1)}, bf16[4096,128]{1,0:T(8,128)(2,1)S(1)}, u32[]{:S(2)}, u32[]{:S(2)}) %collective-permute-start.4) | collective-permute-done | bytes 1048608 | tf_op jit(solution)/shard_map/ppermute | solution.py:359
  242.7 2.3 pad_maximum_fusion.1.refs_3_
  244.9 43.6 %columns.1 = (bf16[32,16,32,128]{3,2,1,0:T(8,128)(2,1)}, bf16[32,16,32,128]{3,2,1,0:T(8,128)(2,1)}, f32[8,256]{1,0:T(8,128)}) custom-call(bf16[32,16,32,128]{3,2,1,0:T(8,128)(2,1)} %all-to-all-done.refs_0_, bf16[32,16,32,128]{3,2,1,0:T(8,128)(2,1)} %all-to-all-done.1.refs_1_, s32[1]{0:T(128)} %bitcast.8.refs_2_, ...), custom_call_target="tpu_custom_call" | custom-call | flops 40000000000 | bytes 33554432 | tf_op jit(solution)/shard_map/columns/pallas_call | solution.py:345
  288.6 28.0 %all-to-all-start.2 = ((bf16[32,16,32,128]{3,2,1,0:T(8,128)(2,1)}), bf16[32,16,32,128]{3,2,1,0:T(8,128)(2,1)}, u32[]{:S(2)}, u32[]{:S(2)}) async-start(bf16[32,16,32,128]{3,2,1,0:T(8,128)(2,1)} %get-tuple-element.33), calls=%async_computation.2 | async-start | bytes 8388608 | tf_op jit(solution)/shard_map/all_to_all | solution.py:400
  317.3 3.3 collective-permute-start.7
  323.3 2.9 collective-permute-start.8
  327.7 6.0 %collective-permute-start.9 = (f32[1]{0:T(128)}, f32[1]{0:T(128)}, u32[]{:S(2)}, u32[]{:S(2)}) collective-permute-start(f32[1]{0:T(128)} %add.119), channel_id=1, source_target_pairs={{0,32},{16,48},{32,0},{48,16},{1,33},{17,49},{33,1},{49,17},{2,34}... | collective-permute-start | bytes 20 | tf_op jit(solution)/shard_map/ppermute | solution.py:363
  335.1 3.0 collective-permute-start.10
  338.8 27.5 %collective-permute-start.11 = (f32[1]{0:T(128)}, f32[1]{0:T(128)}, u32[]{:S(2)}, u32[]{:S(2)}) collective-permute-start(f32[1]{0:T(128)} %add.121), channel_id=1, source_target_pairs={{0,64},{64,0},{128,192},{192,128},{1,65},{65,1},{129,193},{193,129... | collective-permute-start | bytes 20 | tf_op jit(solution)/shard_map/ppermute | solution.py:363
  369.8 2.4 collective-permute-done.12
  376.0 4.3 collective-permute-start.14
  381.3 12.2 %row_inverse.2 = bf16[8,2,16,64,128]{4,3,2,1,0:T(8,128)(2,1)S(1)} custom-call(s32[9]{0:T(128)S(1)} %pad_add_fusion.scalars, bf16[32,16,32,128]{3,2,1,0:T(8,128)(2,1)} %all-to-all-done.2.field, bf16[128,128]{1,0:T(8,128)(2,1)S(1)} %copy-done.10, bf16[256,256]{1,0:T(8,128)(2,1)S(1)} %copy-done.7, f32[2,512,128]{2,1,0:T(8,128)S(1)} %copy-done.6), custom_call_target="tpu_custom_call" | custom-call | flops 16000000000 | bytes 8388608 | tf_op jit(solution)/shard_map/row_inverse/pallas_call | solution.py:317
  395.6 60.7 %all_to_all.20.field = bf16[32,16,32,128]{3,2,1,0:T(8,128)(2,1)S(1)} all-to-all(bf16[32,16,32,128]{3,2,1,0:T(8,128)(2,1)} %get-tuple-element.36), channel_id=1, replica_groups=mesh['x'=4,'zh'=4,'core'=2,'zl'=2,'y'=4] {'x','y','core'}, dimensions={0} | all-to-all | bytes 8388608 | tf_op jit(solution)/shard_map/all_to_all | solution.py:400
  456.3 10.6 %row_inverse.3 = bf16[8,2,16,64,128]{4,3,2,1,0:T(8,128)(2,1)S(1)} custom-call(s32[9]{0:T(128)S(1)} %pad_add_fusion.scalars, bf16[32,16,32,128]{3,2,1,0:T(8,128)(2,1)S(1)} %all_to_all.20.field, bf16[128,128]{1,0:T(8,128)(2,1)S(1)} %copy-done.10, bf16[256,256]{1,0:T(8,128)(2,1)S(1)} %copy-done.7, f32[2,512,128]{2,1,0:T(8,128)S(1)} %copy-done.6), custom_call_target="tpu_custom_call" | custom-call | flops 16000000000 | bytes 8388608 | tf_op jit(solution)/shard_map/row_inverse/pallas_call | solution.py:317
  470.2 53.7 %reduce-scatter.5.cloned.1.call-done = bf16[1,2,16,64,128]{4,3,2,1,0:T(8,128)(2,1)} async-done(((bf16[8,2,16,64,128]{4,3,2,1,0:T(8,128)(2,1)}), bf16[1,2,16,64,128]{4,3,2,1,0:T(8,128)(2,1)}) %reduce-scatter.5.cloned.1.call-update) | async-done | bytes 524304 | tf_op jit(solution)/shard_map/reduce_scatter | solution.py:404
  (79 shorter events, 34.1 us)
Async XLA Ops:
  7.2 61.5 %all-gather.5.cloned.1.call-start = ((), (), s32[]{:S(2)}) async-start(), calls=%async_computation.8 | async-start | bytes 4718592 | tf_op jit(solution)/shard_map/all_gather | solution.py:377
  8.7 60.3 %copy-start.8 = (bf16[256,256]{1,0:T(8,128)(2,1)S(1)}, bf16[256,256]{1,0:T(8,128)(2,1)}, u32[]{:S(2)}) copy-start(bf16[256,256]{1,0:T(8,128)(2,1)} %constant.126.clone.sub_table) | copy-start | bytes 393220
  8.7 60.3 %copy-start.9 = (f32[2,64,128]{2,1,0:T(8,128)S(1)}, f32[2,64,128]{2,1,0:T(8,128)}, u32[]{:S(2)}) copy-start(f32[2,64,128]{2,1,0:T(8,128)} %constant.127.clone.turn) | copy-start | bytes 196612
  8.7 60.3 %copy-start.11 = (bf16[128,128]{1,0:T(8,128)(2,1)S(1)}, bf16[128,128]{1,0:T(8,128)(2,1)}, u32[]{:S(2)}) copy-start(bf16[128,128]{1,0:T(8,128)(2,1)} %constant.125.clone.lead_table) | copy-start | bytes 98308
  9.8 114.0 %all-gather.7.cloned.1.call-start = ((), (), s32[]{:S(2)}) async-start(), calls=%async_computation.9 | async-start | bytes 4718592 | tf_op jit(solution)/shard_map/all_gather | solution.py:377
  18.1 24.7 %collective-permute-start.1 = (bf16[4096,128]{1,0:T(8,128)(2,1)}, bf16[4096,128]{1,0:T(8,128)(2,1)S(1)}, u32[]{:S(2)}, u32[]{:S(2)}) collective-permute-start(bf16[4096,128]{1,0:T(8,128)(2,1)} %get-tuple-element.21), channel_id=1, source_target_pairs={{0,1},{1,2},{2,3},{3,0},{4,5},{5,6},{6,7},{7,4},{8,9},{9,10},{10,1... | collective-permute-start | bytes 3145736 | tf_op jit(solution)/shard_map/ppermute | solution.py:359
  20.2 47.9 %collective-permute-start.2 = (bf16[4096,128]{1,0:T(8,128)(2,1)}, bf16[4096,128]{1,0:T(8,128)(2,1)S(1)}, u32[]{:S(2)}, u32[]{:S(2)}) collective-permute-start(bf16[4096,128]{1,0:T(8,128)(2,1)} %get-tuple-element.22), channel_id=1, source_target_pairs={{0,2},{1,3},{2,0},{3,1},{4,6},{5,7},{6,4},{7,5},{8,10},{9,11},{10,... | collective-permute-start | bytes 3145736 | tf_op jit(solution)/shard_map/ppermute | solution.py:359
  22.8 45.2 %collective-permute-start.3 = (bf16[4096,128]{1,0:T(8,128)(2,1)}, bf16[4096,128]{1,0:T(8,128)(2,1)}, u32[]{:S(2)}, u32[]{:S(2)}) collective-permute-start(bf16[4096,128]{1,0:T(8,128)(2,1)} %get-tuple-element.23), channel_id=1, source_target_pairs={{0,3},{1,0},{2,1},{3,2},{4,7},{5,4},{6,5},{7,6},{8,11},{9,8},{10,9... | collective-permute-start | bytes 3145736 | tf_op jit(solution)/shard_map/ppermute | solution.py:359
  23.9 1.8 collective-permute-start
  82.9 59.6 %all-to-all-start = ((bf16[32,16,32,128]{3,2,1,0:T(8,128)(2,1)}), bf16[32,16,32,128]{3,2,1,0:T(8,128)(2,1)}, u32[]{:S(2)}, u32[]{:S(2)}) async-start(bf16[32,16,32,128]{3,2,1,0:T(8,128)(2,1)} %copy-done.3), calls=%async_computation | async-start | bytes 8388608 | tf_op jit(solution)/shard_map/all_to_all | solution.py:384
  156.3 88.6 %all-to-all-start.1 = ((bf16[32,16,32,128]{3,2,1,0:T(8,128)(2,1)}), bf16[32,16,32,128]{3,2,1,0:T(8,128)(2,1)}, u32[]{:S(2)}, u32[]{:S(2)}) async-start(bf16[32,16,32,128]{3,2,1,0:T(8,128)(2,1)} %copy-done), calls=%async_computation.1 | async-start | bytes 8388608 | tf_op jit(solution)/shard_map/all_to_all | solution.py:392
  163.5 12.0 %copy-start.14 = (f32[128,128]{1,0:T(8,128)S(1)}, f32[128,128]{1,0:T(8,128)}, u32[]{:S(2)}) copy-start(f32[128,128]{1,0:T(8,128)} %constant.130.clone) | copy-start | bytes 196612
  163.5 12.0 %copy-start.15 = (f32[128,128]{1,0:T(8,128)S(1)}, f32[128,128]{1,0:T(8,128)}, u32[]{:S(2)}) copy-start(f32[128,128]{1,0:T(8,128)} %constant.134.clone) | copy-start | bytes 196612
  163.5 12.0 %copy-start.16 = (f32[128,128]{1,0:T(8,128)S(1)}, f32[128,128]{1,0:T(8,128)}, u32[]{:S(2)}) copy-start(f32[128,128]{1,0:T(8,128)} %constant.133.clone) | copy-start | bytes 196612
  166.2 58.3 %collective-permute-start.6 = (bf16[4096,128]{1,0:T(8,128)(2,1)S(1)}, bf16[4096,128]{1,0:T(8,128)(2,1)S(1)}, u32[]{:S(2)}, u32[]{:S(2)}) collective-permute-start(bf16[4096,128]{1,0:T(8,128)(2,1)S(1)} %get-tuple-element.39), channel_id=1, source_target_pairs={{0,48},{16,0},{32,16},{48,32},{1,49},{17,1},{33,17},{49,33},{2,50}... | collective-permute-start | bytes 3145736 | tf_op jit(solution)/shard_map/ppermute | solution.py:359
  172.3 52.2 %collective-permute-start.5 = (bf16[4096,128]{1,0:T(8,128)(2,1)S(1)}, bf16[4096,128]{1,0:T(8,128)(2,1)S(1)}, u32[]{:S(2)}, u32[]{:S(2)}) collective-permute-start(bf16[4096,128]{1,0:T(8,128)(2,1)S(1)} %get-tuple-element.40), channel_id=1, source_target_pairs={{0,32},{16,48},{32,0},{48,16},{1,33},{17,49},{33,1},{49,17},{2,34}... | collective-permute-start | bytes 3145736 | tf_op jit(solution)/shard_map/ppermute | solution.py:359
  173.3 69.4 %collective-permute-start.4 = (bf16[4096,128]{1,0:T(8,128)(2,1)S(1)}, bf16[4096,128]{1,0:T(8,128)(2,1)S(1)}, u32[]{:S(2)}, u32[]{:S(2)}) collective-permute-start(bf16[4096,128]{1,0:T(8,128)(2,1)S(1)} %get-tuple-element.41), channel_id=1, source_target_pairs={{0,16},{16,32},{32,48},{48,0},{1,17},{17,33},{33,49},{49,1},{2,18}... | collective-permute-start | bytes 3145736 | tf_op jit(solution)/shard_map/ppermute | solution.py:359
  288.5 28.1 %copy-start.21 = (f32[8,256]{1,0:T(8,128)S(1)}, f32[8,256]{1,0:T(8,128)}, u32[]{:S(2)}) copy-start(f32[8,256]{1,0:T(8,128)} %get-tuple-element.32) | copy-start | bytes 24580
  288.5 92.7 %copy-start.6 = (f32[2,512,128]{2,1,0:T(8,128)S(1)}, f32[2,512,128]{2,1,0:T(8,128)}, u32[]{:S(2)}) copy-start(f32[2,512,128]{2,1,0:T(8,128)} %constant.139.clone.turn) | copy-start | bytes 1572868
  288.5 92.7 %copy-start.7 = (bf16[256,256]{1,0:T(8,128)(2,1)S(1)}, bf16[256,256]{1,0:T(8,128)(2,1)}, u32[]{:S(2)}) copy-start(bf16[256,256]{1,0:T(8,128)(2,1)} %constant.138.clone.sub_table) | copy-start | bytes 393220
  288.6 92.7 %copy-start.10 = (bf16[128,128]{1,0:T(8,128)(2,1)S(1)}, bf16[128,128]{1,0:T(8,128)(2,1)}, u32[]{:S(2)}) copy-start(bf16[128,128]{1,0:T(8,128)(2,1)} %constant.137.clone.lead_table) | copy-start | bytes 98308
  288.6 92.7 %all-to-all-start.2 = ((bf16[32,16,32,128]{3,2,1,0:T(8,128)(2,1)}), bf16[32,16,32,128]{3,2,1,0:T(8,128)(2,1)}, u32[]{:S(2)}, u32[]{:S(2)}) async-start(bf16[32,16,32,128]{3,2,1,0:T(8,128)(2,1)} %get-tuple-element.33), calls=%async_computation.2 | async-start | bytes 8388608 | tf_op jit(solution)/shard_map/all_to_all | solution.py:400
  316.6 152.3 %reduce-scatter.3.cloned.1.call-start = ((), (), s32[]{:S(2)}) async-start(), calls=%async_computation.6 | async-start | bytes 4718592 | tf_op jit(solution)/shard_map/reduce_scatter | solution.py:404
  317.3 4.7 collective-permute-start.7
  323.3 3.8 collective-permute-start.8
  327.7 6.8 %collective-permute-start.9 = (f32[1]{0:T(128)}, f32[1]{0:T(128)}, u32[]{:S(2)}, u32[]{:S(2)}) collective-permute-start(f32[1]{0:T(128)} %add.119), channel_id=1, source_target_pairs={{0,32},{16,48},{32,0},{48,16},{1,33},{17,49},{33,1},{49,17},{2,34}... | collective-permute-start | bytes 20 | tf_op jit(solution)/shard_map/ppermute | solution.py:363
  335.1 3.0 collective-permute-start.10
  338.8 28.7 %collective-permute-start.11 = (f32[1]{0:T(128)}, f32[1]{0:T(128)}, u32[]{:S(2)}, u32[]{:S(2)}) collective-permute-start(f32[1]{0:T(128)} %add.121), channel_id=1, source_target_pairs={{0,64},{64,0},{128,192},{192,128},{1,65},{65,1},{129,193},{193,129... | collective-permute-start | bytes 20 | tf_op jit(solution)/shard_map/ppermute | solution.py:363
  368.1 4.1 collective-permute-start.12
  372.8 2.6 collective-permute-start.13
  376.0 4.6 collective-permute-start.14
  395.6 128.3 %reduce-scatter.5.cloned.1.call-start = ((), (), s32[]{:S(2)}) async-start(), calls=%async_computation.7 | async-start | bytes 4718592 | tf_op jit(solution)/shard_map/reduce_scatter | solution.py:404
  (12 other events, 68.6 us)
Sparse Core Ops, SparseCore 0:
  9.9 58.6 all-gather.4
  70.4 53.3 all-gather.6
  395.7 60.8 reduce-scatter.2
  469.0 54.8 reduce-scatter.4

commit v2 on v1

--- a/solution.py
+++ b/solution.py
@@ -18,6 +18,7 @@
 STRIDE = 136
 EPSILON = 0.25
 CHUNKS = 2
+EARLY = 1280
 ROW_PRIME, COLUMN_PRIME, MASK_PRIME, MIX_PRIME = 73856093, 19349663, 83492791, 1274126177
 BF16 = jnp.bfloat16
 F32 = jnp.float32
@@ -141,7 +142,7 @@
                         out[(x * 4 + jh * 2 + half) * 2 + core, r] = swap[half, at : at + 32, :].astype(BF16)
         return carry
 
-    lax.fori_loop(0, count, body, 0)
+    lax.fori_loop(0, count, body, 0, unroll=4)
 
 
 def row_inverse_kernel(first_row, scalars, field, lead_table, sub_table, turn, out, swap):
@@ -175,7 +176,7 @@
             out[zs, 1, r] = imag_part.astype(BF16)
         return carry
 
-    lax.fori_loop(0, count, body, 0)
+    lax.fori_loop(0, count, body, 0, unroll=4)
 
 
 def pair_up(first, second, low):
@@ -194,9 +195,9 @@
 
 def column_kernel(*refs):
     fields = refs[:CHUNKS]
-    place, amplitudes, forward_lead, inverse_lead, forward_sub, inverse_sub = refs[CHUNKS : CHUNKS + 6]
-    outs = refs[CHUNKS + 6 : 2 * CHUNKS + 6]
-    loss, hold = refs[2 * CHUNKS + 6 :]
+    place, early, late, forward_lead, inverse_lead, forward_sub, inverse_sub = refs[CHUNKS : CHUNKS + 7]
+    outs = refs[CHUNKS + 7 : 2 * CHUNKS + 7]
+    loss, hold = refs[2 * CHUNKS + 7 :]
     count = SLAB // CHUNKS
 
     for chunk in range(CHUNKS):
@@ -226,11 +227,12 @@
 
     loss[...] = jnp.zeros_like(loss)
 
-    def middle(k1_low, carry):
+    def middle(amplitudes, first_k1, index, carry):
+        k1_low = first_k1 + index
         low = lax.broadcasted_iota(jnp.int32, (SUB, 128), 1) < 64
         measured = [[], []]
         for pair in range(2):
-            first, second = (amplitudes[lax.rem(place[0] + 4 - b, 4), k1_low].astype(F32) for b in (pair * 2, pair * 2 + 1))
+            first, second = (amplitudes[lax.rem(place[0] + 4 - b, 4), index].astype(F32) for b in (pair * 2, pair * 2 + 1))
             for high, values in enumerate(pair_up(first, second, low)):
                 measured[high].append(values)
         places = [pl.ds(pl.multiple_of((k1_low + high * 32) * STRIDE, 8), SUB) for high in range(2)]
@@ -259,7 +261,8 @@
                     hold[part, pair, at, :] = result[part * SUB : part * SUB + SUB, pair * 128 : pair * 128 + 128]
         return carry
 
-    lax.fori_loop(0, 32, middle, 0, unroll=2)
+    lax.fori_loop(0, EARLY // SUB, functools.partial(middle, early, 0), 0, unroll=2)
+    lax.fori_loop(0, 32 - EARLY // SUB, functools.partial(middle, late, EARLY // SUB), 0, unroll=2)
 
     for chunk in range(CHUNKS):
 
@@ -345,13 +348,13 @@
     result = pl.pallas_call(
         column_kernel,
         out_shape=[jax.ShapeDtypeStruct((32, count, 32, 128), BF16)] * CHUNKS + [jax.ShapeDtypeStruct((8, 256), F32)],
-        in_specs=[VMEM] * CHUNKS + [SMEM] + [VMEM] * 5,
+        in_specs=[VMEM] * CHUNKS + [SMEM] + [VMEM] * 6,
         out_specs=[VMEM] * (CHUNKS + 1),
         scratch_shapes=[pltpu.VMEM((2, 2, LEAD * STRIDE, 128), F32)],
         compiler_params=params(58),
         cost_estimate=cost(40 * 10**9, 2**25),
         name="columns",
-    )(*fields, place, amplitudes, forward_lead, inverse_lead, table["forward_sub"], table["inverse_sub"])
+    )(*fields, place, *amplitudes, forward_lead, inverse_lead, table["forward_sub"], table["inverse_sub"])
     return result[:-1], result[-1]
 
 
@@ -382,17 +385,23 @@
     spread = jnp.stack(spread)
     sent = [row_forward(table, 0, scalars, slabs[0])]
     fields = [lax.all_to_all(sent[0], plane, 0, 0, tiled=True)]
-    spread, slabs[-1], fields[0] = lax.optimization_barrier((spread, slabs[-1], fields[0]))
-    packed = [lax.dynamic_index_in_dim(spread, lax.rem(y - zh - t + 8, 4), 0, False) for t in range(4)]
-    packed = jnp.stack([shift_by(piece, "zh", t) for t, piece in enumerate(packed)])
-    packed = packed.reshape(4, 32, SUB, 128)
+
+    def to_planes(rows, first, last):
+        cut = [lax.dynamic_slice_in_dim(rows[:, first:last], lax.rem(y - zh - t + 8, 4), 1, 0)[0] for t in range(4)]
+        return [shift_by(piece, "zh", t) for t, piece in enumerate(cut)]
+
+    early = to_planes(spread, 0, EARLY)
+    spread, slabs[-1] = lax.optimization_barrier((spread, slabs[-1]))
+    late = to_planes(spread, EARLY, N // 2)
+    slabs[-1], fields[0], early = lax.optimization_barrier((slabs[-1], fields[0], early))
+    packed = [jnp.stack(pieces).reshape(4, -1, SUB, 128) for pieces in (early, late)]
     forward_lead = column_tables(table, "forward")
     inverse_lead = column_tables(table, "inverse")
     sent.extend(row_forward(table, c * count, scalars, slabs[c]) for c in range(1, CHUNKS))
     fields.extend(lax.all_to_all(piece, plane, 0, 0, tiled=True) for piece in sent[1:])
     returned, loss = columns(table, fields, zh[None].astype(jnp.int32), packed, forward_lead, inverse_lead)
     loss_total = jnp.sum(loss).reshape(1)
-    for axis, distance in (("zl", 1), ("zh", 1), ("zh", 2), ("core", 1), ("x", 1), ("x", 2), ("y", 1), ("y", 2)):
+    for axis, distance in (("zl", 1), ("zh", 1), ("zh", 2), ("core", 1)):
         loss_total = fold(loss_total, axis, distance)
     pieces = []
     returned = list(returned)
@@ -400,6 +409,10 @@
         back = lax.all_to_all(returned[c], plane, 0, 0, tiled=True)
         if c == 0:
             loss_total, back, returned[1:] = lax.optimization_barrier((loss_total, back, returned[1:]))
+            for axis, distance in (("x", 1), ("x", 2), ("y", 1), ("y", 2)):
+                loss_total = fold(loss_total, axis, distance)
+        else:
+            loss_total, back = lax.optimization_barrier((loss_total, back))
         term = row_inverse(table, c * count, scalars, back)
         pieces.append(lax.psum_scatter(term, ("zh", "zl"), scatter_dimension=0, tiled=False))
     gradient = jnp.concatenate(pieces, axis=1).astype(F32).reshape(2, SLAB, N)

time: 535 us -> 511 us (0.955)
  blocking collectives: 60.7 us -> 0 us
  starting transfers between devices: 110 us -> 136 us
  waiting for transfers between devices: 213 us -> 231 us
  Pallas kernels: 93.4 us -> 84.2 us
    all_to_all x1 -> x0, blocking collectives: 60.7 us -> none  [shards(): back = lax.all_to_all(returned[c], plane, 0, 0, tiled=True)]
    ppermute x8, starting transfers between devices: 50.3 us -> 83.2 us  [fold(): lax.ppermute(value, axis, [(i, i ^ distance) for i in range(lax.axis_size...]
    all_gather x2, waiting for transfers between devices: 30.7 us -> 51 us  [shards(): lax.all_gather(image[:, c * count:(c + 1) * count], ('zh', 'zl'), axis=0)]
    ppermute x6 -> x9, waiting for transfers between devices: 101 us -> 81 us  [shift_by(): lax.ppermute(piece, axis, [(i, (i + shift) % 4) for i in range(4)])]
    all_to_all x1, waiting for transfers between devices: 18.6 us -> 0.01 us  [shards(): fields = [lax.all_to_all(sent[0], plane, 0, 0, tiled=True)]]
    reduce_scatter x2, waiting for transfers between devices: 53.7 us -> 70.8 us  [shards(): lax.psum_scatter(term, ('zh', 'zl'), scatter_dimension=0, tiled=False)]
    all_to_all x1 -> x2, waiting for transfers between devices: 0.01 us -> 16.2 us  [shards(): back = lax.all_to_all(returned[c], plane, 0, 0, tiled=True)]
    all_to_all x1 -> x2, starting transfers between devices: 28 us -> 15.9 us  [shards(): back = lax.all_to_all(returned[c], plane, 0, 0, tiled=True)]
  transfers between devices with their start and end apart: 22 -> 26, of which waited for: 15 -> 16; matrix products, arithmetic and copies ran while one was open for 3% -> 3% of each run, Pallas kernels for 5% -> 5%
where the time goes in v2:
time: 511 us
  waiting for transfers between devices  231 us (45%)
  starting transfers between devices  136 us (27%)
  Pallas kernels  84.2 us (16%)
  local copies, waits for them, and re-layouts  22.1 us (4%)
  between operations  21.7 us (4%)
  other arithmetic  14.6 us (3%)
    ppermute x8, starting transfers between devices, fold(): lax.ppermute(value, axis, [(i, i ^ distance) for i in range(lax.axis_size...  83.2 us
    ppermute x9, waiting for transfers between devices, shift_by(): lax.ppermute(piece, axis, [(i, (i + shift) % 4) for i in range(4)])  81 us
    reduce_scatter x2, waiting for transfers between devices, shards(): lax.psum_scatter(term, ('zh', 'zl'), scatter_dimension=0, tiled=False)  70.8 us
    all_gather x2, waiting for transfers between devices, shards(): lax.all_gather(image[:, c * count:(c + 1) * count], ('zh', 'zl'), axis=0)  51 us
    pallas_call x1, Pallas kernels, columns(): pl.pallas_call(column_kernel, out_shape=[jax.ShapeDtypeStruct((32, count,...  43.5 us
    ppermute x9, starting transfers between devices, shift_by(): lax.ppermute(piece, axis, [(i, (i + shift) % 4) for i in range(4)])  20.4 us
    pallas_call x2, Pallas kernels, row_inverse(): pl.pallas_call(functools.partial(row_inverse_kernel, first_row), out_shap...  18.4 us
    unnamed x47, local copies, waits for them, and re-layouts  16.3 us
  transfers between devices with their start and end apart: 26, of which 16 were waited for; matrix products, arithmetic and copies ran while one was open for 3% of the time, Pallas kernels for 5%

profile of v2, /device:TPU:1, one launch (start us, length us, event | category | flops | bytes accessed | tf_op | source)
XLA Modules:
  0.0 510.5 jit_solution(4162267336950031575)
XLA Ops:
  10.6 7.5 %pack.1 = (bf16[4096,128]{1,0:T(8,128)(2,1)}, bf16[4096,128]{1,0:T(8,128)(2,1)}, bf16[4096,128]{1,0:T(8,128)(2,1)}, bf16[4096,128]{1,0:T(8,128)(2,1)}) custom-call(s32[1]{0:T(128)} %bitcast.place, bf16[2,4096,256]{2,1,0:T(8,128)(2,1)} %bitcast.43), custom_call_target="tpu_custom_call" | custom-call | flops 10000000 | bytes 8388608 | tf_op jit(solution)/shard_map/pack/pallas_call | solution.py:335
  20.2 2.6 collective-permute-start.2
  26.5 16.2 %collective-permute-done.1 = bf16[4096,128]{1,0:T(8,128)(2,1)S(1)} collective-permute-done((bf16[4096,128]{1,0:T(8,128)(2,1)}, bf16[4096,128]{1,0:T(8,128)(2,1)S(1)}, u32[]{:S(2)}, u32[]{:S(2)}) %collective-permute-start.1) | collective-permute-done | bytes 1048608 | tf_op jit(solution)/shard_map/ppermute | solution.py:362
  42.8 25.3 %collective-permute-done.2 = bf16[4096,128]{1,0:T(8,128)(2,1)S(1)} collective-permute-done((bf16[4096,128]{1,0:T(8,128)(2,1)}, bf16[4096,128]{1,0:T(8,128)(2,1)S(1)}, u32[]{:S(2)}, u32[]{:S(2)}) %collective-permute-start.2) | collective-permute-done | bytes 1048608 | tf_op jit(solution)/shard_map/ppermute | solution.py:362
  69.0 2.2 copy-done.5
  71.2 7.4 %row_forward.2 = bf16[32,16,32,128]{3,2,1,0:T(8,128)(2,1)S(1)} custom-call(s32[9]{0:T(128)S(1)} %pad_add_fusion.scalars, bf16[8,2,16,64,128]{4,3,2,1,0:T(8,128)(2,1)S(1)} %bitcast.42, bf16[128,128]{1,0:T(8,128)(2,1)S(1)} %copy-done.11, bf16[256,256]{1,0:T(8,128)(2,1)S(1)} %copy-done.8, f32[2,64,128]{2,1,0:T(8,128)S(1)} %copy-done.9), custom_call_target="tpu_custom_call" | custom-call | flops 16000000000 | bytes 8388608 | tf_op jit(solution)/shard_map/row_forward/pallas_call | solution.py:306
  80.7 7.3 %all-to-all-start = ((bf16[32,16,32,128]{3,2,1,0:T(8,128)(2,1)}), bf16[32,16,32,128]{3,2,1,0:T(8,128)(2,1)}, u32[]{:S(2)}, u32[]{:S(2)}) async-start(bf16[32,16,32,128]{3,2,1,0:T(8,128)(2,1)} %copy-done), calls=%async_computation | async-start | bytes 8388608 | tf_op jit(solution)/shard_map/all_to_all | solution.py:387
  92.1 6.1 %collective-permute-start.6 = (bf16[1280,128]{1,0:T(8,128)(2,1)S(1)}, bf16[1280,128]{1,0:T(8,128)(2,1)S(1)}, u32[]{:S(2)}, u32[]{:S(2)}) collective-permute-start(bf16[1280,128]{1,0:T(8,128)(2,1)S(1)} %get-tuple-element.56), channel_id=1, source_target_pairs={{0,48},{16,0},{32,16},{48,32},{1,49},{17,1},{33,17},{49,33},{2,50}... | collective-permute-start | bytes 983048 | tf_op jit(solution)/shard_map/ppermute | solution.py:362
  99.2 2.3 collective-permute-start.4
  101.5 50.5 %all-gather.7.cloned.1.call-done = bf16[16,16,64,128]{3,2,1,0:T(8,128)(2,1)} async-done(((bf16[2,16,64,128]{3,2,1,0:T(8,128)(2,1)}), bf16[16,16,64,128]{3,2,1,0:T(8,128)(2,1)}) %all-gather.7.cloned.1.call-update) | async-done | bytes 4194320 | tf_op jit(solution)/shard_map/all_gather | solution.py:380
  152.0 2.2 copy-done.4
  154.2 7.4 %row_forward.3 = bf16[32,16,32,128]{3,2,1,0:T(8,128)(2,1)S(1)} custom-call(s32[9]{0:T(128)S(1)} %pad_add_fusion.scalars, bf16[8,2,16,64,128]{4,3,2,1,0:T(8,128)(2,1)S(1)} %bitcast.41, bf16[128,128]{1,0:T(8,128)(2,1)S(1)} %copy-done.11, bf16[256,256]{1,0:T(8,128)(2,1)S(1)} %copy-done.8, f32[2,64,128]{2,1,0:T(8,128)S(1)} %copy-done.9), custom_call_target="tpu_custom_call" | custom-call | flops 16000000000 | bytes 8388608 | tf_op jit(solution)/shard_map/row_forward/pallas_call | solution.py:306
  163.6 7.6 %all-to-all-start.1 = ((bf16[32,16,32,128]{3,2,1,0:T(8,128)(2,1)}), bf16[32,16,32,128]{3,2,1,0:T(8,128)(2,1)}, u32[]{:S(2)}, u32[]{:S(2)}) async-start(bf16[32,16,32,128]{3,2,1,0:T(8,128)(2,1)} %copy-done.2), calls=%async_computation.1 | async-start | bytes 8388608 | tf_op jit(solution)/shard_map/all_to_all | solution.py:401
  178.5 7.7 %add_convert_fusion = (bf16[128,128,128]{2,1,0:T(8,128)(2,1)}, bf16[128,128,128]{2,1,0:T(8,128)(2,1)}) fusion(f32[128,128]{1,0:T(8,128)S(1)} %copy-done.16, f32[128,128]{1,0:T(8,128)S(1)} %copy-done.17, f32[128,128]{1,0:T(8,128)S(1)} %copy-done.15, f32[128,128]{1,0:T(8,128)S(1)} %copy-done.18, f32[128,128]{1,0:T(8,128)S(1)} %copy-done.19, ...), kind=kLoop, calls=%fused_computation | loop fusion | flops 16777216 | bytes 8847360 | tf_op jit(solution)/shard_map/convert_element_type | solution.py:87
  186.2 18.0 %collective-permute-done.9 = bf16[2816,128]{1,0:T(8,128)(2,1)S(1)} collective-permute-done((bf16[2816,128]{1,0:T(8,128)(2,1)S(1)}, bf16[2816,128]{1,0:T(8,128)(2,1)S(1)}, u32[]{:S(2)}, u32[]{:S(2)}) %collective-permute-start.9) | collective-permute-done | bytes 720928 | tf_op jit(solution)/shard_map/ppermute | solution.py:362
  204.2 7.1 %collective-permute-done.8 = bf16[2816,128]{1,0:T(8,128)(2,1)S(1)} collective-permute-done((bf16[2816,128]{1,0:T(8,128)(2,1)S(1)}, bf16[2816,128]{1,0:T(8,128)(2,1)S(1)}, u32[]{:S(2)}, u32[]{:S(2)}) %collective-permute-start.8) | collective-permute-done | bytes 720928 | tf_op jit(solution)/shard_map/ppermute | solution.py:362
  211.2 14.5 %collective-permute-done.7 = bf16[2816,128]{1,0:T(8,128)(2,1)S(1)} collective-permute-done((bf16[2816,128]{1,0:T(8,128)(2,1)S(1)}, bf16[2816,128]{1,0:T(8,128)(2,1)S(1)}, u32[]{:S(2)}, u32[]{:S(2)}) %collective-permute-start.7) | collective-permute-done | bytes 720928 | tf_op jit(solution)/shard_map/ppermute | solution.py:362
  228.6 43.5 %columns.1 = (bf16[32,16,32,128]{3,2,1,0:T(8,128)(2,1)}, bf16[32,16,32,128]{3,2,1,0:T(8,128)(2,1)}, f32[8,256]{1,0:T(8,128)}) custom-call(bf16[32,16,32,128]{3,2,1,0:T(8,128)(2,1)} %all-to-all-done.refs_0_, bf16[32,16,32,128]{3,2,1,0:T(8,128)(2,1)} %all-to-all-done.1.refs_1_, s32[1]{0:T(128)} %bitcast.12.refs_2_, ...), custom_call_target="tpu_custom_call" | custom-call | flops 40000000000 | bytes 33554432 | tf_op jit(solution)/shard_map/columns/pallas_call | solution.py:348
  272.2 8.7 %all-to-all-start.2 = ((bf16[32,16,32,128]{3,2,1,0:T(8,128)(2,1)}), bf16[32,16,32,128]{3,2,1,0:T(8,128)(2,1)}, u32[]{:S(2)}, u32[]{:S(2)}) async-start(bf16[32,16,32,128]{3,2,1,0:T(8,128)(2,1)} %get-tuple-element.45), calls=%async_computation.2 | async-start | bytes 8388608 | tf_op jit(solution)/shard_map/all_to_all | solution.py:409
  281.6 16.5 %collective-permute-start.10 = (f32[1]{0:T(128)}, f32[1]{0:T(128)}, u32[]{:S(2)}, u32[]{:S(2)}) collective-permute-start(f32[1]{0:T(128)} %bitcast.24), channel_id=1, source_target_pairs={{0,4},{4,0},{1,5},{5,1},{2,6},{6,2},{3,7},{7,3},{8,12},{12,8},{9,1... | collective-permute-start | bytes 20 | tf_op jit(solution)/shard_map/ppermute | solution.py:366
  302.4 2.2 collective-permute-done.11
  305.3 3.4 collective-permute-start.12
  308.7 3.1 collective-permute-done.12
  312.4 3.9 collective-permute-start.13
  317.0 16.2 %all-to-all-done.2.field = bf16[32,16,32,128]{3,2,1,0:T(8,128)(2,1)} async-done(((bf16[32,16,32,128]{3,2,1,0:T(8,128)(2,1)}), bf16[32,16,32,128]{3,2,1,0:T(8,128)(2,1)}, u32[]{:S(2)}, u32[]{:S(2)}) %all-to-all-start.2) | async-done | bytes 4194336 | tf_op jit(solution)/shard_map/all_to_all | solution.py:409
  333.1 9.2 %row_inverse.2 = bf16[8,2,16,64,128]{4,3,2,1,0:T(8,128)(2,1)S(1)} custom-call(s32[9]{0:T(128)S(1)} %pad_add_fusion.scalars, bf16[32,16,32,128]{3,2,1,0:T(8,128)(2,1)} %all-to-all-done.2.field, bf16[128,128]{1,0:T(8,128)(2,1)S(1)} %copy-done.10, bf16[256,256]{1,0:T(8,128)(2,1)S(1)} %copy-done.7, f32[2,512,128]{2,1,0:T(8,128)S(1)} %copy-done.6), custom_call_target="tpu_custom_call" | custom-call | flops 16000000000 | bytes 8388608 | tf_op jit(solution)/shard_map/row_inverse/pallas_call | solution.py:320
  344.4 7.2 %all-to-all-start.3 = ((bf16[32,16,32,128]{3,2,1,0:T(8,128)(2,1)}), bf16[32,16,32,128]{3,2,1,0:T(8,128)(2,1)}, u32[]{:S(2)}, u32[]{:S(2)}) async-start(bf16[32,16,32,128]{3,2,1,0:T(8,128)(2,1)} %get-tuple-element.49), calls=%async_computation.4 | async-start | bytes 8388608 | tf_op jit(solution)/shard_map/all_to_all | solution.py:409
  351.6 49.7 %collective-permute-start.14 = (f32[1]{0:T(128)}, f32[1]{0:T(128)}, u32[]{:S(2)}, u32[]{:S(2)}) collective-permute-start(f32[1]{0:T(128)} %add.128), channel_id=1, source_target_pairs={{0,64},{64,0},{128,192},{192,128},{1,65},{65,1},{129,193},{193,129... | collective-permute-start | bytes 20 | tf_op jit(solution)/shard_map/ppermute | solution.py:366
  404.7 2.3 collective-permute-done.15
  411.2 4.8 collective-permute-start.17
  416.8 9.2 %row_inverse.3 = bf16[8,2,16,64,128]{4,3,2,1,0:T(8,128)(2,1)S(1)} custom-call(s32[9]{0:T(128)S(1)} %pad_add_fusion.scalars, bf16[32,16,32,128]{3,2,1,0:T(8,128)(2,1)} %all-to-all-done.3.field, bf16[128,128]{1,0:T(8,128)(2,1)S(1)} %copy-done.10, bf16[256,256]{1,0:T(8,128)(2,1)S(1)} %copy-done.7, f32[2,512,128]{2,1,0:T(8,128)S(1)} %copy-done.6), custom_call_target="tpu_custom_call" | custom-call | flops 16000000000 | bytes 8388608 | tf_op jit(solution)/shard_map/row_inverse/pallas_call | solution.py:320
  429.3 70.8 %reduce-scatter.5.cloned.1.call-done = bf16[1,2,16,64,128]{4,3,2,1,0:T(8,128)(2,1)} async-done(((bf16[8,2,16,64,128]{4,3,2,1,0:T(8,128)(2,1)}), bf16[1,2,16,64,128]{4,3,2,1,0:T(8,128)(2,1)}) %reduce-scatter.5.cloned.1.call-update) | async-done | bytes 524304 | tf_op jit(solution)/shard_map/reduce_scatter | solution.py:417
  (93 shorter events, 46.3 us)
Async XLA Ops:
  7.2 61.5 %all-gather.5.cloned.1.call-start = ((), (), s32[]{:S(2)}) async-start(), calls=%async_computation.8 | async-start | bytes 4718592 | tf_op jit(solution)/shard_map/all_gather | solution.py:380
  8.7 60.3 %copy-start.8 = (bf16[256,256]{1,0:T(8,128)(2,1)S(1)}, bf16[256,256]{1,0:T(8,128)(2,1)}, u32[]{:S(2)}) copy-start(bf16[256,256]{1,0:T(8,128)(2,1)} %constant.117.clone.sub_table) | copy-start | bytes 393220
  8.7 60.3 %copy-start.9 = (f32[2,64,128]{2,1,0:T(8,128)S(1)}, f32[2,64,128]{2,1,0:T(8,128)}, u32[]{:S(2)}) copy-start(f32[2,64,128]{2,1,0:T(8,128)} %constant.118.clone.turn) | copy-start | bytes 196612
  8.7 60.3 %copy-start.11 = (bf16[128,128]{1,0:T(8,128)(2,1)S(1)}, bf16[128,128]{1,0:T(8,128)(2,1)}, u32[]{:S(2)}) copy-start(bf16[128,128]{1,0:T(8,128)(2,1)} %constant.116.clone.lead_table) | copy-start | bytes 98308
  9.8 142.1 %all-gather.7.cloned.1.call-start = ((), (), s32[]{:S(2)}) async-start(), calls=%async_computation.9 | async-start | bytes 4718592 | tf_op jit(solution)/shard_map/all_gather | solution.py:380
  18.1 24.7 %collective-permute-start.1 = (bf16[4096,128]{1,0:T(8,128)(2,1)}, bf16[4096,128]{1,0:T(8,128)(2,1)S(1)}, u32[]{:S(2)}, u32[]{:S(2)}) collective-permute-start(bf16[4096,128]{1,0:T(8,128)(2,1)} %get-tuple-element.28), channel_id=1, source_target_pairs={{0,1},{1,2},{2,3},{3,0},{4,5},{5,6},{6,7},{7,4},{8,9},{9,10},{10,1... | collective-permute-start | bytes 3145736 | tf_op jit(solution)/shard_map/ppermute | solution.py:362
  20.2 47.9 %collective-permute-start.2 = (bf16[4096,128]{1,0:T(8,128)(2,1)}, bf16[4096,128]{1,0:T(8,128)(2,1)S(1)}, u32[]{:S(2)}, u32[]{:S(2)}) collective-permute-start(bf16[4096,128]{1,0:T(8,128)(2,1)} %get-tuple-element.29), channel_id=1, source_target_pairs={{0,2},{1,3},{2,0},{3,1},{4,6},{5,7},{6,4},{7,5},{8,10},{9,11},{10,... | collective-permute-start | bytes 3145736 | tf_op jit(solution)/shard_map/ppermute | solution.py:362
  22.8 45.2 %collective-permute-start.3 = (bf16[4096,128]{1,0:T(8,128)(2,1)}, bf16[4096,128]{1,0:T(8,128)(2,1)}, u32[]{:S(2)}, u32[]{:S(2)}) collective-permute-start(bf16[4096,128]{1,0:T(8,128)(2,1)} %get-tuple-element.30), channel_id=1, source_target_pairs={{0,3},{1,0},{2,1},{3,2},{4,7},{5,4},{6,5},{7,6},{8,11},{9,8},{10,9... | collective-permute-start | bytes 3145736 | tf_op jit(solution)/shard_map/ppermute | solution.py:362
  23.9 1.9 collective-permute-start
  80.7 71.2 %all-to-all-start = ((bf16[32,16,32,128]{3,2,1,0:T(8,128)(2,1)}), bf16[32,16,32,128]{3,2,1,0:T(8,128)(2,1)}, u32[]{:S(2)}, u32[]{:S(2)}) async-start(bf16[32,16,32,128]{3,2,1,0:T(8,128)(2,1)} %copy-done), calls=%async_computation | async-start | bytes 8388608 | tf_op jit(solution)/shard_map/all_to_all | solution.py:387
  92.1 59.8 %collective-permute-start.6 = (bf16[1280,128]{1,0:T(8,128)(2,1)S(1)}, bf16[1280,128]{1,0:T(8,128)(2,1)S(1)}, u32[]{:S(2)}, u32[]{:S(2)}) collective-permute-start(bf16[1280,128]{1,0:T(8,128)(2,1)S(1)} %get-tuple-element.56), channel_id=1, source_target_pairs={{0,48},{16,0},{32,16},{48,32},{1,49},{17,1},{33,17},{49,33},{2,50}... | collective-permute-start | bytes 983048 | tf_op jit(solution)/shard_map/ppermute | solution.py:362
  98.2 53.7 %collective-permute-start.5 = (bf16[1280,128]{1,0:T(8,128)(2,1)S(1)}, bf16[1280,128]{1,0:T(8,128)(2,1)S(1)}, u32[]{:S(2)}, u32[]{:S(2)}) collective-permute-start(bf16[1280,128]{1,0:T(8,128)(2,1)S(1)} %get-tuple-element.57), channel_id=1, source_target_pairs={{0,32},{16,48},{32,0},{48,16},{1,33},{17,49},{33,1},{49,17},{2,34}... | collective-permute-start | bytes 983048 | tf_op jit(solution)/shard_map/ppermute | solution.py:362
  99.2 52.7 %collective-permute-start.4 = (bf16[1280,128]{1,0:T(8,128)(2,1)S(1)}, bf16[1280,128]{1,0:T(8,128)(2,1)S(1)}, u32[]{:S(2)}, u32[]{:S(2)}) collective-permute-start(bf16[1280,128]{1,0:T(8,128)(2,1)S(1)} %get-tuple-element.58), channel_id=1, source_target_pairs={{0,16},{16,32},{32,48},{48,0},{1,17},{17,33},{33,49},{49,1},{2,18}... | collective-permute-start | bytes 983048 | tf_op jit(solution)/shard_map/ppermute | solution.py:362
  163.6 65.1 %all-to-all-start.1 = ((bf16[32,16,32,128]{3,2,1,0:T(8,128)(2,1)}), bf16[32,16,32,128]{3,2,1,0:T(8,128)(2,1)}, u32[]{:S(2)}, u32[]{:S(2)}) async-start(bf16[32,16,32,128]{3,2,1,0:T(8,128)(2,1)} %copy-done.2), calls=%async_computation.1 | async-start | bytes 8388608 | tf_op jit(solution)/shard_map/all_to_all | solution.py:401
  173.2 30.9 %collective-permute-start.9 = (bf16[2816,128]{1,0:T(8,128)(2,1)S(1)}, bf16[2816,128]{1,0:T(8,128)(2,1)S(1)}, u32[]{:S(2)}, u32[]{:S(2)}) collective-permute-start(bf16[2816,128]{1,0:T(8,128)(2,1)S(1)} %get-tuple-element.53), channel_id=1, source_target_pairs={{0,48},{16,0},{32,16},{48,32},{1,49},{17,1},{33,17},{49,33},{2,50}... | collective-permute-start | bytes 2162696 | tf_op jit(solution)/shard_map/ppermute | solution.py:362
  175.2 36.0 %collective-permute-start.8 = (bf16[2816,128]{1,0:T(8,128)(2,1)S(1)}, bf16[2816,128]{1,0:T(8,128)(2,1)S(1)}, u32[]{:S(2)}, u32[]{:S(2)}) collective-permute-start(bf16[2816,128]{1,0:T(8,128)(2,1)S(1)} %get-tuple-element.54), channel_id=1, source_target_pairs={{0,32},{16,48},{32,0},{48,16},{1,33},{17,49},{33,1},{49,17},{2,34}... | collective-permute-start | bytes 2162696 | tf_op jit(solution)/shard_map/ppermute | solution.py:362
  177.1 48.6 %collective-permute-start.7 = (bf16[2816,128]{1,0:T(8,128)(2,1)S(1)}, bf16[2816,128]{1,0:T(8,128)(2,1)S(1)}, u32[]{:S(2)}, u32[]{:S(2)}) collective-permute-start(bf16[2816,128]{1,0:T(8,128)(2,1)S(1)} %get-tuple-element.55), channel_id=1, source_target_pairs={{0,16},{16,32},{32,48},{48,0},{1,17},{17,33},{33,49},{49,1},{2,18}... | collective-permute-start | bytes 2162696 | tf_op jit(solution)/shard_map/ppermute | solution.py:362
  272.2 61.0 %copy-start.6 = (f32[2,512,128]{2,1,0:T(8,128)S(1)}, f32[2,512,128]{2,1,0:T(8,128)}, u32[]{:S(2)}) copy-start(f32[2,512,128]{2,1,0:T(8,128)} %constant.130.clone.turn) | copy-start | bytes 1572868
  272.2 61.0 %copy-start.7 = (bf16[256,256]{1,0:T(8,128)(2,1)S(1)}, bf16[256,256]{1,0:T(8,128)(2,1)}, u32[]{:S(2)}) copy-start(bf16[256,256]{1,0:T(8,128)(2,1)} %constant.129.clone.sub_table) | copy-start | bytes 393220
  272.2 61.0 %copy-start.10 = (bf16[128,128]{1,0:T(8,128)(2,1)S(1)}, bf16[128,128]{1,0:T(8,128)(2,1)}, u32[]{:S(2)}) copy-start(bf16[128,128]{1,0:T(8,128)(2,1)} %constant.128.clone.lead_table) | copy-start | bytes 98308
  272.2 60.9 %all-to-all-start.2 = ((bf16[32,16,32,128]{3,2,1,0:T(8,128)(2,1)}), bf16[32,16,32,128]{3,2,1,0:T(8,128)(2,1)}, u32[]{:S(2)}, u32[]{:S(2)}) async-start(bf16[32,16,32,128]{3,2,1,0:T(8,128)(2,1)} %get-tuple-element.45), calls=%async_computation.2 | async-start | bytes 8388608 | tf_op jit(solution)/shard_map/all_to_all | solution.py:409
  280.9 147.1 %reduce-scatter.3.cloned.1.call-start = ((), (), s32[]{:S(2)}) async-start(), calls=%async_computation.6 | async-start | bytes 4718592 | tf_op jit(solution)/shard_map/reduce_scatter | solution.py:417
  281.6 18.0 %collective-permute-start.10 = (f32[1]{0:T(128)}, f32[1]{0:T(128)}, u32[]{:S(2)}, u32[]{:S(2)}) collective-permute-start(f32[1]{0:T(128)} %bitcast.24), channel_id=1, source_target_pairs={{0,4},{4,0},{1,5},{5,1},{2,6},{6,2},{3,7},{7,3},{8,12},{12,8},{9,1... | collective-permute-start | bytes 20 | tf_op jit(solution)/shard_map/ppermute | solution.py:366
  300.9 3.8 collective-permute-start.11
  305.3 6.5 %collective-permute-start.12 = (f32[1]{0:T(128)}, f32[1]{0:T(128)}, u32[]{:S(2)}, u32[]{:S(2)}) collective-permute-start(f32[1]{0:T(128)} %add.126), channel_id=1, source_target_pairs={{0,32},{16,48},{32,0},{48,16},{1,33},{17,49},{33,1},{49,17},{2,34}... | collective-permute-start | bytes 20 | tf_op jit(solution)/shard_map/ppermute | solution.py:366
  312.4 3.9 collective-permute-start.13
  344.4 72.4 %all-to-all-start.3 = ((bf16[32,16,32,128]{3,2,1,0:T(8,128)(2,1)}), bf16[32,16,32,128]{3,2,1,0:T(8,128)(2,1)}, u32[]{:S(2)}, u32[]{:S(2)}) async-start(bf16[32,16,32,128]{3,2,1,0:T(8,128)(2,1)} %get-tuple-element.49), calls=%async_computation.4 | async-start | bytes 8388608 | tf_op jit(solution)/shard_map/all_to_all | solution.py:409
  351.6 148.6 %reduce-scatter.5.cloned.1.call-start = ((), (), s32[]{:S(2)}) async-start(), calls=%async_computation.7 | async-start | bytes 4718592 | tf_op jit(solution)/shard_map/reduce_scatter | solution.py:417
  351.6 50.8 %collective-permute-start.14 = (f32[1]{0:T(128)}, f32[1]{0:T(128)}, u32[]{:S(2)}, u32[]{:S(2)}) collective-permute-start(f32[1]{0:T(128)} %add.128), channel_id=1, source_target_pairs={{0,64},{64,0},{128,192},{192,128},{1,65},{65,1},{129,193},{193,129... | collective-permute-start | bytes 20 | tf_op jit(solution)/shard_map/ppermute | solution.py:366
  403.1 4.0 collective-permute-start.15
  407.7 2.9 collective-permute-start.16
  411.2 4.9 collective-permute-start.17
  (18 other events, 71.7 us)
Sparse Core Ops, SparseCore 0:
  10.0 58.6 all-gather.4
  70.4 81.4 all-gather.6
  344.5 68.7 reduce-scatter.2
  428.1 71.9 reduce-scatter.4

commit v3 on v2

--- a/solution.py
+++ b/solution.py
@@ -401,7 +401,7 @@
     fields.extend(lax.all_to_all(piece, plane, 0, 0, tiled=True) for piece in sent[1:])
     returned, loss = columns(table, fields, zh[None].astype(jnp.int32), packed, forward_lead, inverse_lead)
     loss_total = jnp.sum(loss).reshape(1)
-    for axis, distance in (("zl", 1), ("zh", 1), ("zh", 2), ("core", 1)):
+    for axis, distance in (("zl", 1), ("zh", 1), ("zh", 2)):
         loss_total = fold(loss_total, axis, distance)
     pieces = []
     returned = list(returned)
@@ -409,12 +409,14 @@
         back = lax.all_to_all(returned[c], plane, 0, 0, tiled=True)
         if c == 0:
             loss_total, back, returned[1:] = lax.optimization_barrier((loss_total, back, returned[1:]))
-            for axis, distance in (("x", 1), ("x", 2), ("y", 1), ("y", 2)):
-                loss_total = fold(loss_total, axis, distance)
-        else:
+            loss_total = fold(loss_total, "core", 1)
             loss_total, back = lax.optimization_barrier((loss_total, back))
         term = row_inverse(table, c * count, scalars, back)
+        if c == CHUNKS - 1:
+            loss_total, term = lax.optimization_barrier((loss_total, term))
         pieces.append(lax.psum_scatter(term, ("zh", "zl"), scatter_dimension=0, tiled=False))
+    for axis, distance in (("x", 1), ("x", 2), ("y", 1), ("y", 2)):
+        loss_total = fold(loss_total, axis, distance)
     gradient = jnp.concatenate(pieces, axis=1).astype(F32).reshape(2, SLAB, N)
     return gradient, loss_total[0] / (8 * N * N)
 

time: 511 us -> 491 us (0.961)
  starting transfers between devices: 136 us -> 74.8 us
  blocking collectives: 0 us -> 57.1 us
  waiting for transfers between devices: 231 us -> 217 us
    all_to_all x0 -> x1, blocking collectives: none -> 57.1 us  [shards(): back = lax.all_to_all(returned[c], plane, 0, 0, tiled=True)]
    ppermute x8, starting transfers between devices: 83.2 us -> 28.6 us  [fold(): lax.ppermute(value, axis, [(i, i ^ distance) for i in range(lax.axis_size...]
    reduce_scatter x2, waiting for transfers between devices: 70.8 us -> 49.3 us  [shards(): lax.psum_scatter(term, ('zh', 'zl'), scatter_dimension=0, tiled=False)]
    all_to_all x2 -> x1, starting transfers between devices: 15.9 us -> 8.81 us  [shards(): back = lax.all_to_all(returned[c], plane, 0, 0, tiled=True)]
    all_to_all x2 -> x1, waiting for transfers between devices: 16.2 us -> 21 us  [shards(): back = lax.all_to_all(returned[c], plane, 0, 0, tiled=True)]
  transfers between devices with their start and end apart: 26 -> 25, of which waited for: 16 -> 16; matrix products, arithmetic and copies ran while one was open for 3% -> 3% of each run, Pallas kernels for 5% -> 5%
where the time goes in v3:
time: 491 us; the launch traced here: 490 us
  waiting for transfers between devices  217 us (44%)
  Pallas kernels  82.6 us (17%)
  starting transfers between devices  74.8 us (15%)
  blocking collectives  57.1 us (12%)
  local copies, waits for them, and re-layouts  22.1 us (5%)
  between operations  21.2 us (4%)
  other arithmetic  14.6 us (3%)
    ppermute x9, waiting for transfers between devices, shift_by(): lax.ppermute(piece, axis, [(i, (i + shift) % 4) for i in range(4)])  81.1 us
    all_to_all x1, blocking collectives, shards(): back = lax.all_to_all(returned[c], plane, 0, 0, tiled=True)  57.1 us
    all_gather x2, waiting for transfers between devices, shards(): lax.all_gather(image[:, c * count:(c + 1) * count], ('zh', 'zl'), axis=0)  51 us
    reduce_scatter x2, waiting for transfers between devices, shards(): lax.psum_scatter(term, ('zh', 'zl'), scatter_dimension=0, tiled=False)  49.3 us
    pallas_call x1, Pallas kernels, columns(): pl.pallas_call(column_kernel, out_shape=[jax.ShapeDtypeStruct((32, count,...  43.5 us
    ppermute x8, starting transfers between devices, fold(): lax.ppermute(value, axis, [(i, i ^ distance) for i in range(lax.axis_size...  28.6 us
    all_to_all x1, waiting for transfers between devices, shards(): back = lax.all_to_all(returned[c], plane, 0, 0, tiled=True)  21 us
    ppermute x9, starting transfers between devices, shift_by(): lax.ppermute(piece, axis, [(i, (i + shift) % 4) for i in range(4)])  20.4 us
  transfers between devices with their start and end apart: 25, of which 16 were waited for; matrix products, arithmetic and copies ran while one was open for 3% of the time, Pallas kernels for 5%

profile of v3, /device:TPU:1, one launch (start us, length us, event | category | flops | bytes accessed | tf_op | source)
XLA Modules:
  0.0 489.7 jit_solution(15460275759906505058)
XLA Ops:
  10.6 7.5 %pack.1 = (bf16[4096,128]{1,0:T(8,128)(2,1)}, bf16[4096,128]{1,0:T(8,128)(2,1)}, bf16[4096,128]{1,0:T(8,128)(2,1)}, bf16[4096,128]{1,0:T(8,128)(2,1)}) custom-call(s32[1]{0:T(128)} %bitcast.place, bf16[2,4096,256]{2,1,0:T(8,128)(2,1)} %bitcast.43), custom_call_target="tpu_custom_call" | custom-call | flops 10000000 | bytes 8388608 | tf_op jit(solution)/shard_map/pack/pallas_call | solution.py:335
  18.1 2.1 collective-permute-start.1
  20.2 2.6 collective-permute-start.2
  26.5 16.3 %collective-permute-done.1 = bf16[4096,128]{1,0:T(8,128)(2,1)S(1)} collective-permute-done((bf16[4096,128]{1,0:T(8,128)(2,1)}, bf16[4096,128]{1,0:T(8,128)(2,1)S(1)}, u32[]{:S(2)}, u32[]{:S(2)}) %collective-permute-start.1) | collective-permute-done | bytes 1048608 | tf_op jit(solution)/shard_map/ppermute | solution.py:362
  42.8 25.3 %collective-permute-done.2 = bf16[4096,128]{1,0:T(8,128)(2,1)S(1)} collective-permute-done((bf16[4096,128]{1,0:T(8,128)(2,1)}, bf16[4096,128]{1,0:T(8,128)(2,1)S(1)}, u32[]{:S(2)}, u32[]{:S(2)}) %collective-permute-start.2) | collective-permute-done | bytes 1048608 | tf_op jit(solution)/shard_map/ppermute | solution.py:362
  69.0 2.2 copy-done.5
  71.2 7.4 %row_forward.2 = bf16[32,16,32,128]{3,2,1,0:T(8,128)(2,1)S(1)} custom-call(s32[9]{0:T(128)S(1)} %pad_add_fusion.scalars, bf16[8,2,16,64,128]{4,3,2,1,0:T(8,128)(2,1)S(1)} %bitcast.42, bf16[128,128]{1,0:T(8,128)(2,1)S(1)} %copy-done.11, bf16[256,256]{1,0:T(8,128)(2,1)S(1)} %copy-done.8, f32[2,64,128]{2,1,0:T(8,128)S(1)} %copy-done.9), custom_call_target="tpu_custom_call" | custom-call | flops 16000000000 | bytes 8388608 | tf_op jit(solution)/shard_map/row_forward/pallas_call | solution.py:306
  78.7 2.1 copy-done
  80.7 7.3 %all-to-all-start = ((bf16[32,16,32,128]{3,2,1,0:T(8,128)(2,1)}), bf16[32,16,32,128]{3,2,1,0:T(8,128)(2,1)}, u32[]{:S(2)}, u32[]{:S(2)}) async-start(bf16[32,16,32,128]{3,2,1,0:T(8,128)(2,1)} %copy-done), calls=%async_computation | async-start | bytes 8388608 | tf_op jit(solution)/shard_map/all_to_all | solution.py:387
  92.1 6.1 %collective-permute-start.6 = (bf16[1280,128]{1,0:T(8,128)(2,1)S(1)}, bf16[1280,128]{1,0:T(8,128)(2,1)S(1)}, u32[]{:S(2)}, u32[]{:S(2)}) collective-permute-start(bf16[1280,128]{1,0:T(8,128)(2,1)S(1)} %get-tuple-element.60), channel_id=1, source_target_pairs={{0,48},{16,0},{32,16},{48,32},{1,49},{17,1},{33,17},{49,33},{2,50}... | collective-permute-start | bytes 983048 | tf_op jit(solution)/shard_map/ppermute | solution.py:362
  99.2 2.3 collective-permute-start.4
  101.5 50.5 %all-gather.7.cloned.1.call-done = bf16[16,16,64,128]{3,2,1,0:T(8,128)(2,1)} async-done(((bf16[2,16,64,128]{3,2,1,0:T(8,128)(2,1)}), bf16[16,16,64,128]{3,2,1,0:T(8,128)(2,1)}) %all-gather.7.cloned.1.call-update) | async-done | bytes 4194320 | tf_op jit(solution)/shard_map/all_gather | solution.py:380
  152.0 2.2 copy-done.4
  154.2 7.4 %row_forward.3 = bf16[32,16,32,128]{3,2,1,0:T(8,128)(2,1)S(1)} custom-call(s32[9]{0:T(128)S(1)} %pad_add_fusion.scalars, bf16[8,2,16,64,128]{4,3,2,1,0:T(8,128)(2,1)S(1)} %bitcast.41, bf16[128,128]{1,0:T(8,128)(2,1)S(1)} %copy-done.11, bf16[256,256]{1,0:T(8,128)(2,1)S(1)} %copy-done.8, f32[2,64,128]{2,1,0:T(8,128)S(1)} %copy-done.9), custom_call_target="tpu_custom_call" | custom-call | flops 16000000000 | bytes 8388608 | tf_op jit(solution)/shard_map/row_forward/pallas_call | solution.py:306
  163.6 7.6 %all-to-all-start.1 = ((bf16[32,16,32,128]{3,2,1,0:T(8,128)(2,1)}), bf16[32,16,32,128]{3,2,1,0:T(8,128)(2,1)}, u32[]{:S(2)}, u32[]{:S(2)}) async-start(bf16[32,16,32,128]{3,2,1,0:T(8,128)(2,1)} %copy-done.2), calls=%async_computation.1 | async-start | bytes 8388608 | tf_op jit(solution)/shard_map/all_to_all | solution.py:401
  178.5 7.7 %add_convert_fusion = (bf16[128,128,128]{2,1,0:T(8,128)(2,1)}, bf16[128,128,128]{2,1,0:T(8,128)(2,1)}) fusion(f32[128,128]{1,0:T(8,128)S(1)} %copy-done.16, f32[128,128]{1,0:T(8,128)S(1)} %copy-done.17, f32[128,128]{1,0:T(8,128)S(1)} %copy-done.15, f32[128,128]{1,0:T(8,128)S(1)} %copy-done.18, f32[128,128]{1,0:T(8,128)S(1)} %copy-done.19, ...), kind=kLoop, calls=%fused_computation | loop fusion | flops 16777216 | bytes 8847360 | tf_op jit(solution)/shard_map/convert_element_type | solution.py:87
  186.2 18.0 %collective-permute-done.9 = bf16[2816,128]{1,0:T(8,128)(2,1)S(1)} collective-permute-done((bf16[2816,128]{1,0:T(8,128)(2,1)S(1)}, bf16[2816,128]{1,0:T(8,128)(2,1)S(1)}, u32[]{:S(2)}, u32[]{:S(2)}) %collective-permute-start.9) | collective-permute-done | bytes 720928 | tf_op jit(solution)/shard_map/ppermute | solution.py:362
  204.2 7.1 %collective-permute-done.8 = bf16[2816,128]{1,0:T(8,128)(2,1)S(1)} collective-permute-done((bf16[2816,128]{1,0:T(8,128)(2,1)S(1)}, bf16[2816,128]{1,0:T(8,128)(2,1)S(1)}, u32[]{:S(2)}, u32[]{:S(2)}) %collective-permute-start.8) | collective-permute-done | bytes 720928 | tf_op jit(solution)/shard_map/ppermute | solution.py:362
  211.2 14.5 %collective-permute-done.7 = bf16[2816,128]{1,0:T(8,128)(2,1)S(1)} collective-permute-done((bf16[2816,128]{1,0:T(8,128)(2,1)S(1)}, bf16[2816,128]{1,0:T(8,128)(2,1)S(1)}, u32[]{:S(2)}, u32[]{:S(2)}) %collective-permute-start.7) | collective-permute-done | bytes 720928 | tf_op jit(solution)/shard_map/ppermute | solution.py:362
  228.7 43.5 %columns.1 = (bf16[32,16,32,128]{3,2,1,0:T(8,128)(2,1)}, bf16[32,16,32,128]{3,2,1,0:T(8,128)(2,1)}, f32[8,256]{1,0:T(8,128)}) custom-call(bf16[32,16,32,128]{3,2,1,0:T(8,128)(2,1)} %all-to-all-done.refs_0_, bf16[32,16,32,128]{3,2,1,0:T(8,128)(2,1)} %all-to-all-done.1.refs_1_, s32[1]{0:T(128)} %bitcast.12.refs_2_, ...), custom_call_target="tpu_custom_call" | custom-call | flops 40000000000 | bytes 33554432 | tf_op jit(solution)/shard_map/columns/pallas_call | solution.py:348
  272.2 8.8 %all-to-all-start.2 = ((bf16[32,16,32,128]{3,2,1,0:T(8,128)(2,1)}), bf16[32,16,32,128]{3,2,1,0:T(8,128)(2,1)}, u32[]{:S(2)}, u32[]{:S(2)}) async-start(bf16[32,16,32,128]{3,2,1,0:T(8,128)(2,1)} %get-tuple-element.47), calls=%async_computation.2 | async-start | bytes 8388608 | tf_op jit(solution)/shard_map/all_to_all | solution.py:409
  281.7 16.5 %collective-permute-start.10 = (f32[1]{0:T(128)}, f32[1]{0:T(128)}, u32[]{:S(2)}, u32[]{:S(2)}) collective-permute-start(f32[1]{0:T(128)} %bitcast.24), channel_id=1, source_target_pairs={{0,4},{4,0},{1,5},{5,1},{2,6},{6,2},{3,7},{7,3},{8,12},{12,8},{9,1... | collective-permute-start | bytes 20 | tf_op jit(solution)/shard_map/ppermute | solution.py:366
  302.3 2.2 collective-permute-done.11
  305.1 3.4 collective-permute-start.12
  308.6 3.1 collective-permute-done.12
  312.2 21.0 %all-to-all-done.2.field = bf16[32,16,32,128]{3,2,1,0:T(8,128)(2,1)} async-done(((bf16[32,16,32,128]{3,2,1,0:T(8,128)(2,1)}), bf16[32,16,32,128]{3,2,1,0:T(8,128)(2,1)}, u32[]{:S(2)}, u32[]{:S(2)}) %all-to-all-start.2) | async-done | bytes 4194336 | tf_op jit(solution)/shard_map/all_to_all | solution.py:409
  335.7 9.2 %row_inverse.2 = bf16[8,2,16,64,128]{4,3,2,1,0:T(8,128)(2,1)S(1)} custom-call(s32[9]{0:T(128)S(1)} %pad_add_fusion.scalars, bf16[32,16,32,128]{3,2,1,0:T(8,128)(2,1)} %all-to-all-done.2.field, bf16[128,128]{1,0:T(8,128)(2,1)S(1)} %copy-done.10, bf16[256,256]{1,0:T(8,128)(2,1)S(1)} %copy-done.7, f32[2,512,128]{2,1,0:T(8,128)S(1)} %copy-done.6), custom_call_target="tpu_custom_call" | custom-call | flops 16000000000 | bytes 8388608 | tf_op jit(solution)/shard_map/row_inverse/pallas_call | solution.py:320
  346.9 57.1 %all_to_all.20.field = bf16[32,16,32,128]{3,2,1,0:T(8,128)(2,1)S(1)} all-to-all(bf16[32,16,32,128]{3,2,1,0:T(8,128)(2,1)} %get-tuple-element.53), channel_id=1, replica_groups=mesh['x'=4,'zh'=4,'core'=2,'zl'=2,'y'=4] {'x','y','core'}, dimensions={0} | all-to-all | bytes 8388608 | tf_op jit(solution)/shard_map/all_to_all | solution.py:409
  404.1 7.5 %row_inverse.3 = bf16[8,2,16,64,128]{4,3,2,1,0:T(8,128)(2,1)S(1)} custom-call(s32[9]{0:T(128)S(1)} %pad_add_fusion.scalars, bf16[32,16,32,128]{3,2,1,0:T(8,128)(2,1)S(1)} %all_to_all.20.field, bf16[128,128]{1,0:T(8,128)(2,1)S(1)} %copy-done.10, bf16[256,256]{1,0:T(8,128)(2,1)S(1)} %copy-done.7, f32[2,512,128]{2,1,0:T(8,128)S(1)} %copy-done.6), custom_call_target="tpu_custom_call" | custom-call | flops 16000000000 | bytes 8388608 | tf_op jit(solution)/shard_map/row_inverse/pallas_call | solution.py:320
  416.6 2.1 collective-permute-start.15
  426.0 2.1 collective-permute-done.17
  430.0 49.3 %reduce-scatter.5.cloned.1.call-done = bf16[1,2,16,64,128]{4,3,2,1,0:T(8,128)(2,1)} async-done(((bf16[8,2,16,64,128]{4,3,2,1,0:T(8,128)(2,1)}), bf16[1,2,16,64,128]{4,3,2,1,0:T(8,128)(2,1)}) %reduce-scatter.5.cloned.1.call-update) | async-done | bytes 524304 | tf_op jit(solution)/shard_map/reduce_scatter | solution.py:417
  (92 shorter events, 46.5 us)
Async XLA Ops:
  7.2 61.5 %all-gather.5.cloned.1.call-start = ((), (), s32[]{:S(2)}) async-start(), calls=%async_computation.8 | async-start | bytes 4718592 | tf_op jit(solution)/shard_map/all_gather | solution.py:380
  8.7 60.3 %copy-start.8 = (bf16[256,256]{1,0:T(8,128)(2,1)S(1)}, bf16[256,256]{1,0:T(8,128)(2,1)}, u32[]{:S(2)}) copy-start(bf16[256,256]{1,0:T(8,128)(2,1)} %constant.117.clone.sub_table) | copy-start | bytes 393220
  8.7 60.3 %copy-start.9 = (f32[2,64,128]{2,1,0:T(8,128)S(1)}, f32[2,64,128]{2,1,0:T(8,128)}, u32[]{:S(2)}) copy-start(f32[2,64,128]{2,1,0:T(8,128)} %constant.118.clone.turn) | copy-start | bytes 196612
  8.7 60.3 %copy-start.11 = (bf16[128,128]{1,0:T(8,128)(2,1)S(1)}, bf16[128,128]{1,0:T(8,128)(2,1)}, u32[]{:S(2)}) copy-start(bf16[128,128]{1,0:T(8,128)(2,1)} %constant.116.clone.lead_table) | copy-start | bytes 98308
  9.8 142.1 %all-gather.7.cloned.1.call-start = ((), (), s32[]{:S(2)}) async-start(), calls=%async_computation.9 | async-start | bytes 4718592 | tf_op jit(solution)/shard_map/all_gather | solution.py:380
  18.1 24.7 %collective-permute-start.1 = (bf16[4096,128]{1,0:T(8,128)(2,1)}, bf16[4096,128]{1,0:T(8,128)(2,1)S(1)}, u32[]{:S(2)}, u32[]{:S(2)}) collective-permute-start(bf16[4096,128]{1,0:T(8,128)(2,1)} %get-tuple-element.30), channel_id=1, source_target_pairs={{0,1},{1,2},{2,3},{3,0},{4,5},{5,6},{6,7},{7,4},{8,9},{9,10},{10,1... | collective-permute-start | bytes 3145736 | tf_op jit(solution)/shard_map/ppermute | solution.py:362
  20.2 47.9 %collective-permute-start.2 = (bf16[4096,128]{1,0:T(8,128)(2,1)}, bf16[4096,128]{1,0:T(8,128)(2,1)S(1)}, u32[]{:S(2)}, u32[]{:S(2)}) collective-permute-start(bf16[4096,128]{1,0:T(8,128)(2,1)} %get-tuple-element.31), channel_id=1, source_target_pairs={{0,2},{1,3},{2,0},{3,1},{4,6},{5,7},{6,4},{7,5},{8,10},{9,11},{10,... | collective-permute-start | bytes 3145736 | tf_op jit(solution)/shard_map/ppermute | solution.py:362
  22.8 45.2 %collective-permute-start.3 = (bf16[4096,128]{1,0:T(8,128)(2,1)}, bf16[4096,128]{1,0:T(8,128)(2,1)}, u32[]{:S(2)}, u32[]{:S(2)}) collective-permute-start(bf16[4096,128]{1,0:T(8,128)(2,1)} %get-tuple-element.32), channel_id=1, source_target_pairs={{0,3},{1,0},{2,1},{3,2},{4,7},{5,4},{6,5},{7,6},{8,11},{9,8},{10,9... | collective-permute-start | bytes 3145736 | tf_op jit(solution)/shard_map/ppermute | solution.py:362
  23.9 1.9 collective-permute-start
  80.7 71.3 %all-to-all-start = ((bf16[32,16,32,128]{3,2,1,0:T(8,128)(2,1)}), bf16[32,16,32,128]{3,2,1,0:T(8,128)(2,1)}, u32[]{:S(2)}, u32[]{:S(2)}) async-start(bf16[32,16,32,128]{3,2,1,0:T(8,128)(2,1)} %copy-done), calls=%async_computation | async-start | bytes 8388608 | tf_op jit(solution)/shard_map/all_to_all | solution.py:387
  92.1 59.8 %collective-permute-start.6 = (bf16[1280,128]{1,0:T(8,128)(2,1)S(1)}, bf16[1280,128]{1,0:T(8,128)(2,1)S(1)}, u32[]{:S(2)}, u32[]{:S(2)}) collective-permute-start(bf16[1280,128]{1,0:T(8,128)(2,1)S(1)} %get-tuple-element.60), channel_id=1, source_target_pairs={{0,48},{16,0},{32,16},{48,32},{1,49},{17,1},{33,17},{49,33},{2,50}... | collective-permute-start | bytes 983048 | tf_op jit(solution)/shard_map/ppermute | solution.py:362
  98.2 53.7 %collective-permute-start.5 = (bf16[1280,128]{1,0:T(8,128)(2,1)S(1)}, bf16[1280,128]{1,0:T(8,128)(2,1)S(1)}, u32[]{:S(2)}, u32[]{:S(2)}) collective-permute-start(bf16[1280,128]{1,0:T(8,128)(2,1)S(1)} %get-tuple-element.61), channel_id=1, source_target_pairs={{0,32},{16,48},{32,0},{48,16},{1,33},{17,49},{33,1},{49,17},{2,34}... | collective-permute-start | bytes 983048 | tf_op jit(solution)/shard_map/ppermute | solution.py:362
  99.2 52.7 %collective-permute-start.4 = (bf16[1280,128]{1,0:T(8,128)(2,1)S(1)}, bf16[1280,128]{1,0:T(8,128)(2,1)S(1)}, u32[]{:S(2)}, u32[]{:S(2)}) collective-permute-start(bf16[1280,128]{1,0:T(8,128)(2,1)S(1)} %get-tuple-element.62), channel_id=1, source_target_pairs={{0,16},{16,32},{32,48},{48,0},{1,17},{17,33},{33,49},{49,1},{2,18}... | collective-permute-start | bytes 983048 | tf_op jit(solution)/shard_map/ppermute | solution.py:362
  163.6 65.1 %all-to-all-start.1 = ((bf16[32,16,32,128]{3,2,1,0:T(8,128)(2,1)}), bf16[32,16,32,128]{3,2,1,0:T(8,128)(2,1)}, u32[]{:S(2)}, u32[]{:S(2)}) async-start(bf16[32,16,32,128]{3,2,1,0:T(8,128)(2,1)} %copy-done.2), calls=%async_computation.1 | async-start | bytes 8388608 | tf_op jit(solution)/shard_map/all_to_all | solution.py:401
  173.2 30.9 %collective-permute-start.9 = (bf16[2816,128]{1,0:T(8,128)(2,1)S(1)}, bf16[2816,128]{1,0:T(8,128)(2,1)S(1)}, u32[]{:S(2)}, u32[]{:S(2)}) collective-permute-start(bf16[2816,128]{1,0:T(8,128)(2,1)S(1)} %get-tuple-element.57), channel_id=1, source_target_pairs={{0,48},{16,0},{32,16},{48,32},{1,49},{17,1},{33,17},{49,33},{2,50}... | collective-permute-start | bytes 2162696 | tf_op jit(solution)/shard_map/ppermute | solution.py:362
  175.2 36.0 %collective-permute-start.8 = (bf16[2816,128]{1,0:T(8,128)(2,1)S(1)}, bf16[2816,128]{1,0:T(8,128)(2,1)S(1)}, u32[]{:S(2)}, u32[]{:S(2)}) collective-permute-start(bf16[2816,128]{1,0:T(8,128)(2,1)S(1)} %get-tuple-element.58), channel_id=1, source_target_pairs={{0,32},{16,48},{32,0},{48,16},{1,33},{17,49},{33,1},{49,17},{2,34}... | collective-permute-start | bytes 2162696 | tf_op jit(solution)/shard_map/ppermute | solution.py:362
  177.1 48.6 %collective-permute-start.7 = (bf16[2816,128]{1,0:T(8,128)(2,1)S(1)}, bf16[2816,128]{1,0:T(8,128)(2,1)S(1)}, u32[]{:S(2)}, u32[]{:S(2)}) collective-permute-start(bf16[2816,128]{1,0:T(8,128)(2,1)S(1)} %get-tuple-element.59), channel_id=1, source_target_pairs={{0,16},{16,32},{32,48},{48,0},{1,17},{17,33},{33,49},{49,1},{2,18}... | collective-permute-start | bytes 2162696 | tf_op jit(solution)/shard_map/ppermute | solution.py:362
  272.2 8.9 %copy-start.22 = (f32[8,256]{1,0:T(8,128)S(1)}, f32[8,256]{1,0:T(8,128)}, u32[]{:S(2)}) copy-start(f32[8,256]{1,0:T(8,128)} %get-tuple-element.46) | copy-start | bytes 24580
  272.2 63.4 %copy-start.6 = (f32[2,512,128]{2,1,0:T(8,128)S(1)}, f32[2,512,128]{2,1,0:T(8,128)}, u32[]{:S(2)}) copy-start(f32[2,512,128]{2,1,0:T(8,128)} %constant.130.clone.turn) | copy-start | bytes 1572868
  272.2 63.5 %copy-start.7 = (bf16[256,256]{1,0:T(8,128)(2,1)S(1)}, bf16[256,256]{1,0:T(8,128)(2,1)}, u32[]{:S(2)}) copy-start(bf16[256,256]{1,0:T(8,128)(2,1)} %constant.129.clone.sub_table) | copy-start | bytes 393220
  272.2 63.5 %copy-start.10 = (bf16[128,128]{1,0:T(8,128)(2,1)S(1)}, bf16[128,128]{1,0:T(8,128)(2,1)}, u32[]{:S(2)}) copy-start(bf16[128,128]{1,0:T(8,128)(2,1)} %constant.128.clone.lead_table) | copy-start | bytes 98308
  272.2 61.0 %all-to-all-start.2 = ((bf16[32,16,32,128]{3,2,1,0:T(8,128)(2,1)}), bf16[32,16,32,128]{3,2,1,0:T(8,128)(2,1)}, u32[]{:S(2)}, u32[]{:S(2)}) async-start(bf16[32,16,32,128]{3,2,1,0:T(8,128)(2,1)} %get-tuple-element.47), calls=%async_computation.2 | async-start | bytes 8388608 | tf_op jit(solution)/shard_map/all_to_all | solution.py:409
  281.0 147.7 %reduce-scatter.3.cloned.1.call-start = ((), (), s32[]{:S(2)}) async-start(), calls=%async_computation.6 | async-start | bytes 4718592 | tf_op jit(solution)/shard_map/reduce_scatter | solution.py:417
  281.7 17.9 %collective-permute-start.10 = (f32[1]{0:T(128)}, f32[1]{0:T(128)}, u32[]{:S(2)}, u32[]{:S(2)}) collective-permute-start(f32[1]{0:T(128)} %bitcast.24), channel_id=1, source_target_pairs={{0,4},{4,0},{1,5},{5,1},{2,6},{6,2},{3,7},{7,3},{8,12},{12,8},{9,1... | collective-permute-start | bytes 20 | tf_op jit(solution)/shard_map/ppermute | solution.py:366
  300.8 3.8 collective-permute-start.11
  305.1 6.5 %collective-permute-start.12 = (f32[1]{0:T(128)}, f32[1]{0:T(128)}, u32[]{:S(2)}, u32[]{:S(2)}) collective-permute-start(f32[1]{0:T(128)} %add.126), channel_id=1, source_target_pairs={{0,32},{16,48},{32,0},{48,16},{1,33},{17,49},{33,1},{49,17},{2,34}... | collective-permute-start | bytes 20 | tf_op jit(solution)/shard_map/ppermute | solution.py:366
  333.2 1.7 collective-permute-start.13
  346.9 132.4 %reduce-scatter.5.cloned.1.call-start = ((), (), s32[]{:S(2)}) async-start(), calls=%async_computation.7 | async-start | bytes 4718592 | tf_op jit(solution)/shard_map/reduce_scatter | solution.py:417
  413.6 2.4 collective-permute-start.14
  416.6 3.9 collective-permute-start.15
  421.2 2.4 collective-permute-start.16
  424.2 3.9 collective-permute-start.17
  (17 other events, 62.8 us)
Sparse Core Ops, SparseCore 0:
  10.0 58.6 all-gather.4
  70.4 81.4 all-gather.6
  347.0 68.0 reduce-scatter.2
  417.5 61.7 reduce-scatter.4

commit v4 on v3

--- a/solution.py
+++ b/solution.py
@@ -19,6 +19,7 @@
 EPSILON = 0.25
 CHUNKS = 2
 EARLY = 1280
+BLOCK = 4
 ROW_PRIME, COLUMN_PRIME, MASK_PRIME, MIX_PRIME = 73856093, 19349663, 83492791, 1274126177
 BF16 = jnp.bfloat16
 F32 = jnp.float32
@@ -112,13 +113,13 @@
 
 
 def row_forward_kernel(first_row, scalars, image, lead_table, sub_table, turn, out, swap):
-    count = image.shape[2]
     columns = column_hash()
+    block_row = first_row + pl.program_id(0) * BLOCK
 
     def body(r, carry):
         stacked = []
         for zs in range(8):
-            row = scalars[zs] + first_row + r
+            row = scalars[zs] + block_row + r
             code = phase_code(columns, (row * jnp.int32(ROW_PRIME)) ^ scalars[8])
             real_part, imag_part = image[zs, 0, r].astype(F32), image[zs, 1, r].astype(F32)
             real_part, imag_part = quarter_turn(real_part, imag_part, code, True)
@@ -142,12 +143,12 @@
                         out[(x * 4 + jh * 2 + half) * 2 + core, r] = swap[half, at : at + 32, :].astype(BF16)
         return carry
 
-    lax.fori_loop(0, count, body, 0, unroll=4)
+    lax.fori_loop(0, BLOCK, body, 0, unroll=True)
 
 
 def row_inverse_kernel(first_row, scalars, field, lead_table, sub_table, turn, out, swap):
-    count = field.shape[1]
     columns = column_hash()
+    block_row = first_row + pl.program_id(0) * BLOCK
 
     def body(r, carry):
         blocks = []
@@ -168,7 +169,7 @@
         second = jnp.dot(lead_table[...], jnp.concatenate(middle, axis=1), preferred_element_type=F32)
         second = second * (1.0 / N)
         for zs in range(8):
-            row = scalars[zs] + first_row + r
+            row = scalars[zs] + block_row + r
             code = phase_code(columns, (row * jnp.int32(ROW_PRIME)) ^ scalars[8])
             real_part, imag_part = second[:LEAD, zs * 128 : zs * 128 + 128], second[LEAD:, zs * 128 : zs * 128 + 128]
             real_part, imag_part = quarter_turn(real_part, imag_part, code, False)
@@ -176,7 +177,7 @@
             out[zs, 1, r] = imag_part.astype(BF16)
         return carry
 
-    lax.fori_loop(0, count, body, 0, unroll=4)
+    lax.fori_loop(0, BLOCK, body, 0, unroll=True)
 
 
 def pair_up(first, second, low):
@@ -197,10 +198,23 @@
     fields = refs[:CHUNKS]
     place, early, late, forward_lead, inverse_lead, forward_sub, inverse_sub = refs[CHUNKS : CHUNKS + 7]
     outs = refs[CHUNKS + 7 : 2 * CHUNKS + 7]
-    loss, hold = refs[2 * CHUNKS + 7 :]
+    loss, hold = refs[2 * CHUNKS + 7 : 2 * CHUNKS + 9]
+    buffers, sems = refs[2 * CHUNKS + 9 : -1], refs[-1]
     count = SLAB // CHUNKS
 
+    operands = list(fields) + [forward_lead, early, late, inverse_lead]
+    order = [0, CHUNKS] + list(range(1, CHUNKS)) + list(range(CHUNKS + 1, CHUNKS + 4))
+    loads = [pltpu.make_async_copy(operand, buffers[n], sems.at[n]) for n, operand in enumerate(operands)]
+    for n in order:
+        loads[n].start()
+    fields = buffers[:CHUNKS]
+    forward_lead, early, late, inverse_lead = buffers[CHUNKS : CHUNKS + 4]
+    stores = [pltpu.make_async_copy(buffers[CHUNKS + 4 + n], outs[n], sems.at[CHUNKS + 4 + n]) for n in range(CHUNKS)]
+    outs = buffers[CHUNKS + 4 :]
+    loads[CHUNKS].wait()
+
     for chunk in range(CHUNKS):
+        loads[chunk].wait()
 
         def forward(step, carry, chunk=chunk):
             y, r = step // count, lax.rem(step, count)
@@ -226,6 +240,8 @@
         lax.fori_loop(0, 4 * count, forward, 0, unroll=8)
 
     loss[...] = jnp.zeros_like(loss)
+    for n in range(CHUNKS + 1, CHUNKS + 3):
+        loads[n].wait()
 
     def middle(amplitudes, first_k1, index, carry):
         k1_low = first_k1 + index
@@ -264,6 +280,7 @@
     lax.fori_loop(0, EARLY // SUB, functools.partial(middle, early, 0), 0, unroll=2)
     lax.fori_loop(0, 32 - EARLY // SUB, functools.partial(middle, late, EARLY // SUB), 0, unroll=2)
 
+    loads[CHUNKS + 3].wait()
     for chunk in range(CHUNKS):
 
         def inverse(step, carry, chunk=chunk):
@@ -287,9 +304,14 @@
             return carry
 
         lax.fori_loop(0, 4 * count, inverse, 0, unroll=8)
+        stores[chunk].start()
+
+    for store in stores:
+        store.wait()
 
 
 VMEM = pl.BlockSpec(memory_space=pltpu.VMEM)
+ANY = pl.BlockSpec(memory_space=pl.ANY)
 SMEM = pl.BlockSpec(memory_space=pltpu.SMEM)
 
 
@@ -301,32 +323,40 @@
     return pl.CostEstimate(flops=flops, bytes_accessed=moved, transcendentals=0)
 
 
+def whole(array):
+    return pl.BlockSpec(array.shape, lambda i: (0,) * array.ndim, pipeline_mode=pl.Buffered(1))
+
+
 def row_forward(table, first_row, scalars, image):
     count = image.shape[2]
+    constants = [table["forward_row_lead"], table["forward_row_sub"], table["forward_turn"]]
     return pl.pallas_call(
         functools.partial(row_forward_kernel, first_row),
+        grid=(count // BLOCK,),
         out_shape=jax.ShapeDtypeStruct((32, count, 32, 128), BF16),
-        in_specs=[SMEM] + [VMEM] * 4,
-        out_specs=VMEM,
+        in_specs=[SMEM, pl.BlockSpec((8, 2, BLOCK, LEAD, SUB), lambda i: (0, 0, i, 0, 0))] + [whole(c) for c in constants],
+        out_specs=pl.BlockSpec((32, BLOCK, 32, 128), lambda i: (0, i, 0, 0)),
         scratch_shapes=[pltpu.VMEM((2, 512, 128), F32)],
-        compiler_params=params(40),
+        compiler_params=params(58),
         cost_estimate=cost(count * 10**9, count * 2**19),
         name="row_forward",
-    )(scalars, image, table["forward_row_lead"], table["forward_row_sub"], table["forward_turn"])
+    )(scalars, image, *constants)
 
 
 def row_inverse(table, first_row, scalars, field):
     count = field.shape[1]
+    constants = [table["inverse_row_lead"], table["inverse_row_sub"], table["inverse_turn"]]
     return pl.pallas_call(
         functools.partial(row_inverse_kernel, first_row),
+        grid=(count // BLOCK,),
         out_shape=jax.ShapeDtypeStruct((8, 2, count, LEAD, SUB), BF16),
-        in_specs=[SMEM] + [VMEM] * 4,
-        out_specs=VMEM,
+        in_specs=[SMEM, pl.BlockSpec((32, BLOCK, 32, 128), lambda i: (0, i, 0, 0))] + [whole(c) for c in constants],
+        out_specs=pl.BlockSpec((8, 2, BLOCK, LEAD, SUB), lambda i: (0, 0, i, 0, 0)),
         scratch_shapes=[pltpu.VMEM((2, 512, 128), F32)],
-        compiler_params=params(40),
+        compiler_params=params(58),
         cost_estimate=cost(count * 10**9, count * 2**19),
         name="row_inverse",
-    )(scalars, field, table["inverse_row_lead"], table["inverse_row_sub"], table["inverse_turn"])
+    )(scalars, field, *constants)
 
 
 def pack(place, amplitudes):
@@ -345,12 +375,16 @@
 
 def columns(table, fields, place, amplitudes, forward_lead, inverse_lead):
     count = SLAB // CHUNKS
+    moved = list(fields) + [forward_lead, *amplitudes, inverse_lead]
+    out = jax.ShapeDtypeStruct((32, count, 32, 128), BF16)
     result = pl.pallas_call(
         column_kernel,
-        out_shape=[jax.ShapeDtypeStruct((32, count, 32, 128), BF16)] * CHUNKS + [jax.ShapeDtypeStruct((8, 256), F32)],
-        in_specs=[VMEM] * CHUNKS + [SMEM] + [VMEM] * 6,
-        out_specs=[VMEM] * (CHUNKS + 1),
-        scratch_shapes=[pltpu.VMEM((2, 2, LEAD * STRIDE, 128), F32)],
+        out_shape=[out] * CHUNKS + [jax.ShapeDtypeStruct((8, 256), F32)],
+        in_specs=[ANY] * CHUNKS + [SMEM] + [ANY] * 4 + [VMEM] * 2,
+        out_specs=[ANY] * CHUNKS + [VMEM],
+        scratch_shapes=[pltpu.VMEM((2, 2, LEAD * STRIDE, 128), F32)]
+        + [pltpu.VMEM(array.shape, BF16) for array in moved + [out] * CHUNKS]
+        + [pltpu.SemaphoreType.DMA((2 * CHUNKS + 4,))],
         compiler_params=params(58),
         cost_estimate=cost(40 * 10**9, 2**25),
         name="columns",
@@ -409,13 +443,11 @@
         back = lax.all_to_all(returned[c], plane, 0, 0, tiled=True)
         if c == 0:
             loss_total, back, returned[1:] = lax.optimization_barrier((loss_total, back, returned[1:]))
-            loss_total = fold(loss_total, "core", 1)
-            loss_total, back = lax.optimization_barrier((loss_total, back))
         term = row_inverse(table, c * count, scalars, back)
         if c == CHUNKS - 1:
             loss_total, term = lax.optimization_barrier((loss_total, term))
         pieces.append(lax.psum_scatter(term, ("zh", "zl"), scatter_dimension=0, tiled=False))
-    for axis, distance in (("x", 1), ("x", 2), ("y", 1), ("y", 2)):
+    for axis, distance in (("core", 1), ("x", 1), ("x", 2), ("y", 1), ("y", 2)):
         loss_total = fold(loss_total, axis, distance)
     gradient = jnp.concatenate(pieces, axis=1).astype(F32).reshape(2, SLAB, N)
     return gradient, loss_total[0] / (8 * N * N)

time: 491 us -> 482 us (0.982)
  local copies, waits for them, and re-layouts: 22.1 us -> 9.69 us
    unnamed x47 -> x23, local copies, waits for them, and re-layouts: 16.3 us -> 3.89 us
  transfers between devices with their start and end apart: 25 -> 25, of which waited for: 16 -> 17; matrix products, arithmetic and copies ran while one was open for 3% -> 3% of each run, Pallas kernels for 5% -> 5%
where the time goes in v4:
time: 482 us; the launch traced here: 481 us
  waiting for transfers between devices  216 us (45%)
  Pallas kernels  85.5 us (18%)
  starting transfers between devices  75.5 us (16%)
  blocking collectives  57.8 us (12%)
  between operations  21.5 us (4%)
  other arithmetic  15 us (3%)
  local copies, waits for them, and re-layouts  9.69 us (2%)
    ppermute x9, waiting for transfers between devices, shift_by(): lax.ppermute(piece, axis, [(i, (i + shift) % 4) for i in range(4)])  80.6 us
    all_to_all x1, blocking collectives, shards(): back = lax.all_to_all(returned[c], plane, 0, 0, tiled=True)  57.8 us
    all_gather x2, waiting for transfers between devices, shards(): lax.all_gather(image[:, c * count:(c + 1) * count], ('zh', 'zl'), axis=0)  52.9 us
    reduce_scatter x2, waiting for transfers between devices, shards(): lax.psum_scatter(term, ('zh', 'zl'), scatter_dimension=0, tiled=False)  47.2 us
    pallas_call x1, Pallas kernels, columns(): pl.pallas_call(column_kernel, out_shape=[out] * CHUNKS + [jax.ShapeDtypeS...  40.2 us
    ppermute x8, starting transfers between devices, fold(): lax.ppermute(value, axis, [(i, i ^ distance) for i in range(lax.axis_size...  28.7 us
    all_to_all x1, waiting for transfers between devices, shards(): back = lax.all_to_all(returned[c], plane, 0, 0, tiled=True)  20.7 us
    ppermute x9, starting transfers between devices, shift_by(): lax.ppermute(piece, axis, [(i, (i + shift) % 4) for i in range(4)])  20.4 us
  transfers between devices with their start and end apart: 25, of which 17 were waited for; matrix products, arithmetic and copies ran while one was open for 3% of the time, Pallas kernels for 5%

profile of v4, /device:TPU:1, one launch (start us, length us, event | category | flops | bytes accessed | tf_op | source)
XLA Modules:
  0.0 480.7 jit_solution(17494792625359573295)
XLA Ops:
  10.6 7.5 %pack.1 = (bf16[4096,128]{1,0:T(8,128)(2,1)}, bf16[4096,128]{1,0:T(8,128)(2,1)}, bf16[4096,128]{1,0:T(8,128)(2,1)}, bf16[4096,128]{1,0:T(8,128)(2,1)}) custom-call(s32[1]{0:T(128)} %bitcast.place, bf16[2,4096,256]{2,1,0:T(8,128)(2,1)} %bitcast.41), custom_call_target="tpu_custom_call" | custom-call | flops 10000000 | bytes 8388608 | tf_op jit(solution)/shard_map/pack/pallas_call | solution.py:365
  18.0 2.1 collective-permute-start.1
  20.2 2.6 collective-permute-start.2
  27.0 15.8 %collective-permute-done.1 = bf16[4096,128]{1,0:T(8,128)(2,1)S(1)} collective-permute-done((bf16[4096,128]{1,0:T(8,128)(2,1)}, bf16[4096,128]{1,0:T(8,128)(2,1)S(1)}, u32[]{:S(2)}, u32[]{:S(2)}) %collective-permute-start.1) | collective-permute-done | bytes 1048608 | tf_op jit(solution)/shard_map/ppermute | solution.py:396
  42.8 25.3 %collective-permute-done.2 = bf16[4096,128]{1,0:T(8,128)(2,1)S(1)} collective-permute-done((bf16[4096,128]{1,0:T(8,128)(2,1)}, bf16[4096,128]{1,0:T(8,128)(2,1)S(1)}, u32[]{:S(2)}, u32[]{:S(2)}) %collective-permute-start.2) | collective-permute-done | bytes 1048608 | tf_op jit(solution)/shard_map/ppermute | solution.py:396
  69.0 9.2 %row_forward.2 = bf16[32,16,32,128]{3,2,1,0:T(8,128)(2,1)} custom-call(s32[9]{0:T(128)} %pad_add_fusion.scalars, bf16[8,2,16,64,128]{4,3,2,1,0:T(8,128)(2,1)} %bitcast.57, bf16[128,128]{1,0:T(8,128)(2,1)} %constant.116.clone.lead_table, bf16[256,256]{1,0:T(8,128)(2,1)} %constant.117.clone.sub_table, f32[2,64,128]{2,1,0:T(8,128)} %constant.118.clone.turn), custom_call_target="tpu_custom_call" | custom-call | flops 16000000000 | bytes 8388608 | tf_op jit(solution)/shard_map/row_forward/pallas_call | solution.py:333
  78.3 8.2 %all-to-all-start = ((bf16[32,16,32,128]{3,2,1,0:T(8,128)(2,1)}), bf16[32,16,32,128]{3,2,1,0:T(8,128)(2,1)}, u32[]{:S(2)}, u32[]{:S(2)}) async-start(bf16[32,16,32,128]{3,2,1,0:T(8,128)(2,1)} %row_forward.2), calls=%async_computation | async-start | bytes 8388608 | tf_op jit(solution)/shard_map/all_to_all | solution.py:421
  88.1 2.0 copy-done
  90.3 6.1 %collective-permute-start.6 = (bf16[1280,128]{1,0:T(8,128)(2,1)S(1)}, bf16[1280,128]{1,0:T(8,128)(2,1)S(1)}, u32[]{:S(2)}, u32[]{:S(2)}) collective-permute-start(bf16[1280,128]{1,0:T(8,128)(2,1)S(1)} %get-tuple-element.56), channel_id=1, source_target_pairs={{0,48},{16,0},{32,16},{48,32},{1,49},{17,1},{33,17},{49,33},{2,50}... | collective-permute-start | bytes 983048 | tf_op jit(solution)/shard_map/ppermute | solution.py:396
  97.4 2.3 collective-permute-start.4
  99.6 52.3 %all-gather.7.cloned.1.call-done = bf16[16,16,64,128]{3,2,1,0:T(8,128)(2,1)} async-done(((bf16[2,16,64,128]{3,2,1,0:T(8,128)(2,1)}), bf16[16,16,64,128]{3,2,1,0:T(8,128)(2,1)}) %all-gather.7.cloned.1.call-update) | async-done | bytes 4194320 | tf_op jit(solution)/shard_map/all_gather | solution.py:414
  151.9 9.3 %row_forward.3 = bf16[32,16,32,128]{3,2,1,0:T(8,128)(2,1)} custom-call(s32[9]{0:T(128)} %pad_add_fusion.scalars, bf16[8,2,16,64,128]{4,3,2,1,0:T(8,128)(2,1)} %bitcast.56, bf16[128,128]{1,0:T(8,128)(2,1)} %constant.116.clone.lead_table, bf16[256,256]{1,0:T(8,128)(2,1)} %constant.117.clone.sub_table, f32[2,64,128]{2,1,0:T(8,128)} %constant.118.clone.turn), custom_call_target="tpu_custom_call" | custom-call | flops 16000000000 | bytes 8388608 | tf_op jit(solution)/shard_map/row_forward/pallas_call | solution.py:333
  161.2 7.6 %all-to-all-start.1 = ((bf16[32,16,32,128]{3,2,1,0:T(8,128)(2,1)}), bf16[32,16,32,128]{3,2,1,0:T(8,128)(2,1)}, u32[]{:S(2)}, u32[]{:S(2)}) async-start(bf16[32,16,32,128]{3,2,1,0:T(8,128)(2,1)} %row_forward.3), calls=%async_computation.1 | async-start | bytes 8388608 | tf_op jit(solution)/shard_map/all_to_all | solution.py:435
  170.9 2.0 collective-permute-start.9
  172.9 1.9 collective-permute-start.8
  176.1 7.7 %add_convert_fusion = (bf16[128,128,128]{2,1,0:T(8,128)(2,1)}, bf16[128,128,128]{2,1,0:T(8,128)(2,1)}) fusion(f32[128,128]{1,0:T(8,128)S(1)} %copy-done.4, f32[128,128]{1,0:T(8,128)S(1)} %copy-done.5, f32[128,128]{1,0:T(8,128)S(1)} %copy-done.3, f32[128,128]{1,0:T(8,128)S(1)} %copy-done.6, f32[128,128]{1,0:T(8,128)S(1)} %copy-done.7, ...), kind=kLoop, calls=%fused_computation | loop fusion | flops 16777216 | bytes 8847360 | tf_op jit(solution)/shard_map/convert_element_type | solution.py:88
  183.8 18.0 %collective-permute-done.9 = bf16[2816,128]{1,0:T(8,128)(2,1)S(1)} collective-permute-done((bf16[2816,128]{1,0:T(8,128)(2,1)S(1)}, bf16[2816,128]{1,0:T(8,128)(2,1)S(1)}, u32[]{:S(2)}, u32[]{:S(2)}) %collective-permute-start.9) | collective-permute-done | bytes 720928 | tf_op jit(solution)/shard_map/ppermute | solution.py:396
  201.8 7.0 %collective-permute-done.8 = bf16[2816,128]{1,0:T(8,128)(2,1)S(1)} collective-permute-done((bf16[2816,128]{1,0:T(8,128)(2,1)S(1)}, bf16[2816,128]{1,0:T(8,128)(2,1)S(1)}, u32[]{:S(2)}, u32[]{:S(2)}) %collective-permute-start.8) | collective-permute-done | bytes 720928 | tf_op jit(solution)/shard_map/ppermute | solution.py:396
  208.9 14.5 %collective-permute-done.7 = bf16[2816,128]{1,0:T(8,128)(2,1)S(1)} collective-permute-done((bf16[2816,128]{1,0:T(8,128)(2,1)S(1)}, bf16[2816,128]{1,0:T(8,128)(2,1)S(1)}, u32[]{:S(2)}, u32[]{:S(2)}) %collective-permute-start.7) | collective-permute-done | bytes 720928 | tf_op jit(solution)/shard_map/ppermute | solution.py:396
  226.3 40.2 %columns.1 = (bf16[32,16,32,128]{3,2,1,0:T(8,128)(2,1)}, bf16[32,16,32,128]{3,2,1,0:T(8,128)(2,1)}, f32[8,256]{1,0:T(8,128)}) custom-call(bf16[32,16,32,128]{3,2,1,0:T(8,128)(2,1)} %all-to-all-done.refs_0_, bf16[32,16,32,128]{3,2,1,0:T(8,128)(2,1)} %all-to-all-done.1.refs_1_, s32[1]{0:T(128)} %bitcast.12.refs_2_, ...), custom_call_target="tpu_custom_call" | custom-call | flops 40000000000 | bytes 33554432 | tf_op jit(solution)/shard_map/columns/pallas_call | solution.py:380
  266.5 8.6 %all-to-all-start.2 = ((bf16[32,16,32,128]{3,2,1,0:T(8,128)(2,1)}), bf16[32,16,32,128]{3,2,1,0:T(8,128)(2,1)}, u32[]{:S(2)}, u32[]{:S(2)}) async-start(bf16[32,16,32,128]{3,2,1,0:T(8,128)(2,1)} %get-tuple-element.45), calls=%async_computation.2 | async-start | bytes 8388608 | tf_op jit(solution)/shard_map/all_to_all | solution.py:443
  275.8 16.5 %collective-permute-start.10 = (f32[1]{0:T(128)}, f32[1]{0:T(128)}, u32[]{:S(2)}, u32[]{:S(2)}) collective-permute-start(f32[1]{0:T(128)} %bitcast.24), channel_id=1, source_target_pairs={{0,4},{4,0},{1,5},{5,1},{2,6},{6,2},{3,7},{7,3},{8,12},{12,8},{9,1... | collective-permute-start | bytes 20 | tf_op jit(solution)/shard_map/ppermute | solution.py:400
  296.6 2.3 collective-permute-done.11
  299.5 3.5 collective-permute-start.12
  302.9 3.1 collective-permute-done.12
  306.6 20.7 %all-to-all-done.2.field = bf16[32,16,32,128]{3,2,1,0:T(8,128)(2,1)} async-done(((bf16[32,16,32,128]{3,2,1,0:T(8,128)(2,1)}), bf16[32,16,32,128]{3,2,1,0:T(8,128)(2,1)}, u32[]{:S(2)}, u32[]{:S(2)}) %all-to-all-start.2) | async-done | bytes 4194336 | tf_op jit(solution)/shard_map/all_to_all | solution.py:443
  327.3 9.6 %row_inverse.2 = bf16[8,2,16,64,128]{4,3,2,1,0:T(8,128)(2,1)} custom-call(s32[9]{0:T(128)} %pad_add_fusion.scalars, bf16[32,16,32,128]{3,2,1,0:T(8,128)(2,1)} %all-to-all-done.2.field, bf16[128,128]{1,0:T(8,128)(2,1)} %constant.128.clone.lead_table, bf16[256,256]{1,0:T(8,128)(2,1)} %constant.129.clone.sub_table, f32[2,512,128]{2,1,0:T(8,128)} %constant.130.clone.turn), custom_call_target="tpu_custom_call" | custom-call | flops 16000000000 | bytes 8388608 | tf_op jit(solution)/shard_map/row_inverse/pallas_call | solution.py:349
  337.0 57.8 %all_to_all.20.field = bf16[32,16,32,128]{3,2,1,0:T(8,128)(2,1)} all-to-all(bf16[32,16,32,128]{3,2,1,0:T(8,128)(2,1)} %get-tuple-element.49), channel_id=1, replica_groups=mesh['x'=4,'zh'=4,'core'=2,'zl'=2,'y'=4] {'x','y','core'}, dimensions={0} | all-to-all | bytes 8388608 | tf_op jit(solution)/shard_map/all_to_all | solution.py:443
  394.9 9.6 %row_inverse.3 = bf16[8,2,16,64,128]{4,3,2,1,0:T(8,128)(2,1)} custom-call(s32[9]{0:T(128)} %pad_add_fusion.scalars, bf16[32,16,32,128]{3,2,1,0:T(8,128)(2,1)} %all_to_all.20.field, bf16[128,128]{1,0:T(8,128)(2,1)} %constant.128.clone.lead_table, bf16[256,256]{1,0:T(8,128)(2,1)} %constant.129.clone.sub_table, f32[2,512,128]{2,1,0:T(8,128)} %constant.130.clone.turn), custom_call_target="tpu_custom_call" | custom-call | flops 16000000000 | bytes 8388608 | tf_op jit(solution)/shard_map/row_inverse/pallas_call | solution.py:349
  409.6 2.1 collective-permute-start.15
  417.2 2.2 collective-permute-start.17
  423.1 47.2 %reduce-scatter.5.cloned.1.call-done = bf16[1,2,16,64,128]{4,3,2,1,0:T(8,128)(2,1)} async-done(((bf16[8,2,16,64,128]{4,3,2,1,0:T(8,128)(2,1)}), bf16[1,2,16,64,128]{4,3,2,1,0:T(8,128)(2,1)}) %reduce-scatter.5.cloned.1.call-update) | async-done | bytes 524304 | tf_op jit(solution)/shard_map/reduce_scatter | solution.py:449
  (68 shorter events, 34.6 us)
Async XLA Ops:
  7.2 61.5 %all-gather.5.cloned.1.call-start = ((), (), s32[]{:S(2)}) async-start(), calls=%async_computation.8 | async-start | bytes 4718592 | tf_op jit(solution)/shard_map/all_gather | solution.py:414
  9.8 142.1 %all-gather.7.cloned.1.call-start = ((), (), s32[]{:S(2)}) async-start(), calls=%async_computation.9 | async-start | bytes 4718592 | tf_op jit(solution)/shard_map/all_gather | solution.py:414
  18.0 24.7 %collective-permute-start.1 = (bf16[4096,128]{1,0:T(8,128)(2,1)}, bf16[4096,128]{1,0:T(8,128)(2,1)S(1)}, u32[]{:S(2)}, u32[]{:S(2)}) collective-permute-start(bf16[4096,128]{1,0:T(8,128)(2,1)} %get-tuple-element.28), channel_id=1, source_target_pairs={{0,1},{1,2},{2,3},{3,0},{4,5},{5,6},{6,7},{7,4},{8,9},{9,10},{10,1... | collective-permute-start | bytes 3145736 | tf_op jit(solution)/shard_map/ppermute | solution.py:396
  20.2 47.9 %collective-permute-start.2 = (bf16[4096,128]{1,0:T(8,128)(2,1)}, bf16[4096,128]{1,0:T(8,128)(2,1)S(1)}, u32[]{:S(2)}, u32[]{:S(2)}) collective-permute-start(bf16[4096,128]{1,0:T(8,128)(2,1)} %get-tuple-element.29), channel_id=1, source_target_pairs={{0,2},{1,3},{2,0},{3,1},{4,6},{5,7},{6,4},{7,5},{8,10},{9,11},{10,... | collective-permute-start | bytes 3145736 | tf_op jit(solution)/shard_map/ppermute | solution.py:396
  22.8 45.2 %collective-permute-start.3 = (bf16[4096,128]{1,0:T(8,128)(2,1)}, bf16[4096,128]{1,0:T(8,128)(2,1)S(1)}, u32[]{:S(2)}, u32[]{:S(2)}) collective-permute-start(bf16[4096,128]{1,0:T(8,128)(2,1)} %get-tuple-element.30), channel_id=1, source_target_pairs={{0,3},{1,0},{2,1},{3,2},{4,7},{5,4},{6,5},{7,6},{8,11},{9,8},{10,9... | collective-permute-start | bytes 3145736 | tf_op jit(solution)/shard_map/ppermute | solution.py:396
  23.9 1.9 collective-permute-start
  78.3 8.2 %copy-start.1 = (bf16[4096,128]{1,0:T(8,128)(2,1)S(1)}, bf16[4096,128]{1,0:T(8,128)(2,1)}, u32[]{:S(2)}) copy-start(bf16[4096,128]{1,0:T(8,128)(2,1)} %get-tuple-element.31) | copy-start | bytes 3145732
  78.3 73.7 %all-to-all-start = ((bf16[32,16,32,128]{3,2,1,0:T(8,128)(2,1)}), bf16[32,16,32,128]{3,2,1,0:T(8,128)(2,1)}, u32[]{:S(2)}, u32[]{:S(2)}) async-start(bf16[32,16,32,128]{3,2,1,0:T(8,128)(2,1)} %row_forward.2), calls=%async_computation | async-start | bytes 8388608 | tf_op jit(solution)/shard_map/all_to_all | solution.py:421
  90.3 61.6 %collective-permute-start.6 = (bf16[1280,128]{1,0:T(8,128)(2,1)S(1)}, bf16[1280,128]{1,0:T(8,128)(2,1)S(1)}, u32[]{:S(2)}, u32[]{:S(2)}) collective-permute-start(bf16[1280,128]{1,0:T(8,128)(2,1)S(1)} %get-tuple-element.56), channel_id=1, source_target_pairs={{0,48},{16,0},{32,16},{48,32},{1,49},{17,1},{33,17},{49,33},{2,50}... | collective-permute-start | bytes 983048 | tf_op jit(solution)/shard_map/ppermute | solution.py:396
  96.4 55.5 %collective-permute-start.5 = (bf16[1280,128]{1,0:T(8,128)(2,1)S(1)}, bf16[1280,128]{1,0:T(8,128)(2,1)S(1)}, u32[]{:S(2)}, u32[]{:S(2)}) collective-permute-start(bf16[1280,128]{1,0:T(8,128)(2,1)S(1)} %get-tuple-element.57), channel_id=1, source_target_pairs={{0,32},{16,48},{32,0},{48,16},{1,33},{17,49},{33,1},{49,17},{2,34}... | collective-permute-start | bytes 983048 | tf_op jit(solution)/shard_map/ppermute | solution.py:396
  97.4 54.6 %collective-permute-start.4 = (bf16[1280,128]{1,0:T(8,128)(2,1)S(1)}, bf16[1280,128]{1,0:T(8,128)(2,1)S(1)}, u32[]{:S(2)}, u32[]{:S(2)}) collective-permute-start(bf16[1280,128]{1,0:T(8,128)(2,1)S(1)} %get-tuple-element.58), channel_id=1, source_target_pairs={{0,16},{16,32},{32,48},{48,0},{1,17},{17,33},{33,49},{49,1},{2,18}... | collective-permute-start | bytes 983048 | tf_op jit(solution)/shard_map/ppermute | solution.py:396
  161.2 65.1 %all-to-all-start.1 = ((bf16[32,16,32,128]{3,2,1,0:T(8,128)(2,1)}), bf16[32,16,32,128]{3,2,1,0:T(8,128)(2,1)}, u32[]{:S(2)}, u32[]{:S(2)}) async-start(bf16[32,16,32,128]{3,2,1,0:T(8,128)(2,1)} %row_forward.3), calls=%async_computation.1 | async-start | bytes 8388608 | tf_op jit(solution)/shard_map/all_to_all | solution.py:435
  170.6 5.5 %copy-start.3 = (f32[128,128]{1,0:T(8,128)S(1)}, f32[128,128]{1,0:T(8,128)}, u32[]{:S(2)}) copy-start(f32[128,128]{1,0:T(8,128)} %constant.121.clone) | copy-start | bytes 196612
  170.6 5.5 %copy-start.4 = (f32[128,128]{1,0:T(8,128)S(1)}, f32[128,128]{1,0:T(8,128)}, u32[]{:S(2)}) copy-start(f32[128,128]{1,0:T(8,128)} %constant.125.clone) | copy-start | bytes 196612
  170.6 5.5 %copy-start.5 = (f32[128,128]{1,0:T(8,128)S(1)}, f32[128,128]{1,0:T(8,128)}, u32[]{:S(2)}) copy-start(f32[128,128]{1,0:T(8,128)} %constant.124.clone) | copy-start | bytes 196612
  170.6 5.5 %copy-start.6 = (f32[128,128]{1,0:T(8,128)S(1)}, f32[128,128]{1,0:T(8,128)}, u32[]{:S(2)}) copy-start(f32[128,128]{1,0:T(8,128)} %constant.123.clone) | copy-start | bytes 196612
  170.6 5.5 %copy-start.7 = (f32[128,128]{1,0:T(8,128)S(1)}, f32[128,128]{1,0:T(8,128)}, u32[]{:S(2)}) copy-start(f32[128,128]{1,0:T(8,128)} %constant.122.clone) | copy-start | bytes 196612
  170.9 30.9 %collective-permute-start.9 = (bf16[2816,128]{1,0:T(8,128)(2,1)S(1)}, bf16[2816,128]{1,0:T(8,128)(2,1)S(1)}, u32[]{:S(2)}, u32[]{:S(2)}) collective-permute-start(bf16[2816,128]{1,0:T(8,128)(2,1)S(1)} %get-tuple-element.53), channel_id=1, source_target_pairs={{0,48},{16,0},{32,16},{48,32},{1,49},{17,1},{33,17},{49,33},{2,50}... | collective-permute-start | bytes 2162696 | tf_op jit(solution)/shard_map/ppermute | solution.py:396
  172.9 36.0 %collective-permute-start.8 = (bf16[2816,128]{1,0:T(8,128)(2,1)S(1)}, bf16[2816,128]{1,0:T(8,128)(2,1)S(1)}, u32[]{:S(2)}, u32[]{:S(2)}) collective-permute-start(bf16[2816,128]{1,0:T(8,128)(2,1)S(1)} %get-tuple-element.54), channel_id=1, source_target_pairs={{0,32},{16,48},{32,0},{48,16},{1,33},{17,49},{33,1},{49,17},{2,34}... | collective-permute-start | bytes 2162696 | tf_op jit(solution)/shard_map/ppermute | solution.py:396
  174.7 48.6 %collective-permute-start.7 = (bf16[2816,128]{1,0:T(8,128)(2,1)S(1)}, bf16[2816,128]{1,0:T(8,128)(2,1)S(1)}, u32[]{:S(2)}, u32[]{:S(2)}) collective-permute-start(bf16[2816,128]{1,0:T(8,128)(2,1)S(1)} %get-tuple-element.55), channel_id=1, source_target_pairs={{0,16},{16,32},{32,48},{48,0},{1,17},{17,33},{33,49},{49,1},{2,18}... | collective-permute-start | bytes 2162696 | tf_op jit(solution)/shard_map/ppermute | solution.py:396
  266.5 8.7 %copy-start.10 = (f32[8,256]{1,0:T(8,128)S(1)}, f32[8,256]{1,0:T(8,128)}, u32[]{:S(2)}) copy-start(f32[8,256]{1,0:T(8,128)} %get-tuple-element.44) | copy-start | bytes 24580
  266.5 60.8 %all-to-all-start.2 = ((bf16[32,16,32,128]{3,2,1,0:T(8,128)(2,1)}), bf16[32,16,32,128]{3,2,1,0:T(8,128)(2,1)}, u32[]{:S(2)}, u32[]{:S(2)}) async-start(bf16[32,16,32,128]{3,2,1,0:T(8,128)(2,1)} %get-tuple-element.45), calls=%async_computation.2 | async-start | bytes 8388608 | tf_op jit(solution)/shard_map/all_to_all | solution.py:443
  275.1 146.7 %reduce-scatter.3.cloned.1.call-start = ((), (), s32[]{:S(2)}) async-start(), calls=%async_computation.6 | async-start | bytes 4718592 | tf_op jit(solution)/shard_map/reduce_scatter | solution.py:449
  275.8 18.0 %collective-permute-start.10 = (f32[1]{0:T(128)}, f32[1]{0:T(128)}, u32[]{:S(2)}, u32[]{:S(2)}) collective-permute-start(f32[1]{0:T(128)} %bitcast.24), channel_id=1, source_target_pairs={{0,4},{4,0},{1,5},{5,1},{2,6},{6,2},{3,7},{7,3},{8,12},{12,8},{9,1... | collective-permute-start | bytes 20 | tf_op jit(solution)/shard_map/ppermute | solution.py:400
  295.1 3.8 collective-permute-start.11
  299.5 6.5 %collective-permute-start.12 = (f32[1]{0:T(128)}, f32[1]{0:T(128)}, u32[]{:S(2)}, u32[]{:S(2)}) collective-permute-start(f32[1]{0:T(128)} %add.126), channel_id=1, source_target_pairs={{0,32},{16,48},{32,0},{48,16},{1,33},{17,49},{33,1},{49,17},{2,34}... | collective-permute-start | bytes 20 | tf_op jit(solution)/shard_map/ppermute | solution.py:400
  337.0 133.3 %reduce-scatter.5.cloned.1.call-start = ((), (), s32[]{:S(2)}) async-start(), calls=%async_computation.7 | async-start | bytes 4718592 | tf_op jit(solution)/shard_map/reduce_scatter | solution.py:449
  404.5 1.3 collective-permute-start.13
  406.5 2.4 collective-permute-start.14
  409.6 3.9 collective-permute-start.15
  414.2 2.4 collective-permute-start.16
  417.2 3.9 collective-permute-start.17
  (5 other events, 15.7 us)
Sparse Core Ops, SparseCore 0:
  9.9 58.6 all-gather.4
  70.4 81.4 all-gather.6
  337.1 68.7 reduce-scatter.2
  408.3 61.9 reduce-scatter.4

commit v5 on v4

--- a/solution.py
+++ b/solution.py
@@ -196,21 +196,28 @@
 
 def column_kernel(*refs):
     fields = refs[:CHUNKS]
-    place, early, late, forward_lead, inverse_lead, forward_sub, inverse_sub = refs[CHUNKS : CHUNKS + 7]
-    outs = refs[CHUNKS + 7 : 2 * CHUNKS + 7]
-    loss, hold = refs[2 * CHUNKS + 7 : 2 * CHUNKS + 9]
-    buffers, sems = refs[2 * CHUNKS + 9 : -1], refs[-1]
+    place, pieces = refs[CHUNKS], refs[CHUNKS + 1 : CHUNKS + 9]
+    forward_lead, inverse_lead, forward_sub, inverse_sub = refs[CHUNKS + 9 : CHUNKS + 13]
+    outs = refs[CHUNKS + 13 : 2 * CHUNKS + 13]
+    loss, hold = refs[2 * CHUNKS + 13 : 2 * CHUNKS + 15]
+    buffers, sems, piece_sems = refs[2 * CHUNKS + 15 : -2], refs[-2], refs[-1]
     count = SLAB // CHUNKS
 
-    operands = list(fields) + [forward_lead, early, late, inverse_lead]
-    order = [0, CHUNKS] + list(range(1, CHUNKS)) + list(range(CHUNKS + 1, CHUNKS + 4))
+    early, late = buffers[-2:]
+    operands = list(fields) + [forward_lead, inverse_lead]
     loads = [pltpu.make_async_copy(operand, buffers[n], sems.at[n]) for n, operand in enumerate(operands)]
-    for n in order:
+    amplitude_loads = [
+        pltpu.make_async_copy(piece, (early, late)[n // 4].at[n % 4], piece_sems.at[n]) for n, piece in enumerate(pieces)
+    ]
+    for n in [0, CHUNKS] + list(range(1, CHUNKS)):
         loads[n].start()
+    for load in amplitude_loads:
+        load.start()
+    loads[CHUNKS + 1].start()
     fields = buffers[:CHUNKS]
-    forward_lead, early, late, inverse_lead = buffers[CHUNKS : CHUNKS + 4]
-    stores = [pltpu.make_async_copy(buffers[CHUNKS + 4 + n], outs[n], sems.at[CHUNKS + 4 + n]) for n in range(CHUNKS)]
-    outs = buffers[CHUNKS + 4 :]
+    forward_lead, inverse_lead = buffers[CHUNKS : CHUNKS + 2]
+    stores = [pltpu.make_async_copy(buffers[CHUNKS + 2 + n], outs[n], sems.at[CHUNKS + 2 + n]) for n in range(CHUNKS)]
+    outs = buffers[CHUNKS + 2 : 2 * CHUNKS + 2]
     loads[CHUNKS].wait()
 
     for chunk in range(CHUNKS):
@@ -240,8 +247,8 @@
         lax.fori_loop(0, 4 * count, forward, 0, unroll=8)
 
     loss[...] = jnp.zeros_like(loss)
-    for n in range(CHUNKS + 1, CHUNKS + 3):
-        loads[n].wait()
+    for load in amplitude_loads:
+        load.wait()
 
     def middle(amplitudes, first_k1, index, carry):
         k1_low = first_k1 + index
@@ -280,7 +287,7 @@
     lax.fori_loop(0, EARLY // SUB, functools.partial(middle, early, 0), 0, unroll=2)
     lax.fori_loop(0, 32 - EARLY // SUB, functools.partial(middle, late, EARLY // SUB), 0, unroll=2)
 
-    loads[CHUNKS + 3].wait()
+    loads[CHUNKS + 1].wait()
     for chunk in range(CHUNKS):
 
         def inverse(step, carry, chunk=chunk):
@@ -375,20 +382,23 @@
 
 def columns(table, fields, place, amplitudes, forward_lead, inverse_lead):
     count = SLAB // CHUNKS
-    moved = list(fields) + [forward_lead, *amplitudes, inverse_lead]
+    pieces = [piece for group in amplitudes for piece in group]
+    moved = list(fields) + [forward_lead, inverse_lead]
+    together = [pltpu.VMEM((4,) + group[0].shape, BF16) for group in amplitudes]
     out = jax.ShapeDtypeStruct((32, count, 32, 128), BF16)
     result = pl.pallas_call(
         column_kernel,
         out_shape=[out] * CHUNKS + [jax.ShapeDtypeStruct((8, 256), F32)],
-        in_specs=[ANY] * CHUNKS + [SMEM] + [ANY] * 4 + [VMEM] * 2,
+        in_specs=[ANY] * CHUNKS + [SMEM] + [ANY] * 10 + [VMEM] * 2,
         out_specs=[ANY] * CHUNKS + [VMEM],
         scratch_shapes=[pltpu.VMEM((2, 2, LEAD * STRIDE, 128), F32)]
         + [pltpu.VMEM(array.shape, BF16) for array in moved + [out] * CHUNKS]
-        + [pltpu.SemaphoreType.DMA((2 * CHUNKS + 4,))],
+        + together
+        + [pltpu.SemaphoreType.DMA((2 * CHUNKS + 2,)), pltpu.SemaphoreType.DMA((8,))],
         compiler_params=params(58),
         cost_estimate=cost(40 * 10**9, 2**25),
         name="columns",
-    )(*fields, place, *amplitudes, forward_lead, inverse_lead, table["forward_sub"], table["inverse_sub"])
+    )(*fields, place, *pieces, forward_lead, inverse_lead, table["forward_sub"], table["inverse_sub"])
     return result[:-1], result[-1]
 
 
@@ -428,7 +438,7 @@
     spread, slabs[-1] = lax.optimization_barrier((spread, slabs[-1]))
     late = to_planes(spread, EARLY, N // 2)
     slabs[-1], fields[0], early = lax.optimization_barrier((slabs[-1], fields[0], early))
-    packed = [jnp.stack(pieces).reshape(4, -1, SUB, 128) for pieces in (early, late)]
+    packed = [[piece.reshape(-1, SUB, 128) for piece in pieces] for pieces in (early, late)]
     forward_lead = column_tables(table, "forward")
     inverse_lead = column_tables(table, "inverse")
     sent.extend(row_forward(table, c * count, scalars, slabs[c]) for c in range(1, CHUNKS))

time: 482 us -> 481 us (level)
  no operation moved by 1% of the time
where the time goes in v5:
time: 481 us
  waiting for transfers between devices  216 us (45%)
  Pallas kernels  86.6 us (18%)
  starting transfers between devices  75.1 us (16%)
  blocking collectives  57.9 us (12%)
  between operations  21 us (4%)
  local copies, waits for them, and re-layouts  12.2 us (3%)
  other arithmetic  11.9 us (2%)
    ppermute x9, waiting for transfers between devices, shift_by(): lax.ppermute(piece, axis, [(i, (i + shift) % 4) for i in range(4)])  80.8 us
    all_to_all x1, blocking collectives, shards(): back = lax.all_to_all(returned[c], plane, 0, 0, tiled=True)  57.9 us
    all_gather x2, waiting for transfers between devices, shards(): lax.all_gather(image[:, c * count:(c + 1) * count], ('zh', 'zl'), axis=0)  52.2 us
    reduce_scatter x2, waiting for transfers between devices, shards(): lax.psum_scatter(term, ('zh', 'zl'), scatter_dimension=0, tiled=False)  47.4 us
    pallas_call x1, Pallas kernels, columns(): pl.pallas_call(column_kernel, out_shape=[out] * CHUNKS + [jax.ShapeDtypeS...  41.1 us
    ppermute x8, starting transfers between devices, fold(): lax.ppermute(value, axis, [(i, i ^ distance) for i in range(lax.axis_size...  28.5 us
    all_to_all x1, waiting for transfers between devices, shards(): back = lax.all_to_all(returned[c], plane, 0, 0, tiled=True)  21 us
    ppermute x9, starting transfers between devices, shift_by(): lax.ppermute(piece, axis, [(i, (i + shift) % 4) for i in range(4)])  20.2 us
  transfers between devices with their start and end apart: 25, of which 17 were waited for; matrix products, arithmetic and copies ran while one was open for 3% of the time, Pallas kernels for 5%

profile of v5, /device:TPU:1, one launch (start us, length us, event | category | flops | bytes accessed | tf_op | source)
XLA Modules:
  0.0 480.5 jit_solution(3587031660980555731)
XLA Ops:
  10.6 7.5 %pack.1 = (bf16[4096,128]{1,0:T(8,128)(2,1)}, bf16[4096,128]{1,0:T(8,128)(2,1)}, bf16[4096,128]{1,0:T(8,128)(2,1)}, bf16[4096,128]{1,0:T(8,128)(2,1)}) custom-call(s32[1]{0:T(128)} %bitcast.place, bf16[2,4096,256]{2,1,0:T(8,128)(2,1)} %bitcast.41), custom_call_target="tpu_custom_call" | custom-call | flops 10000000 | bytes 8388608 | tf_op jit(solution)/shard_map/pack/pallas_call | solution.py:372
  18.1 2.1 collective-permute-start.1
  20.2 2.6 collective-permute-start.2
  26.9 15.9 %collective-permute-done.1 = bf16[4096,128]{1,0:T(8,128)(2,1)S(1)} collective-permute-done((bf16[4096,128]{1,0:T(8,128)(2,1)}, bf16[4096,128]{1,0:T(8,128)(2,1)S(1)}, u32[]{:S(2)}, u32[]{:S(2)}) %collective-permute-start.1) | collective-permute-done | bytes 1048608 | tf_op jit(solution)/shard_map/ppermute | solution.py:406
  42.8 25.3 %collective-permute-done.2 = bf16[4096,128]{1,0:T(8,128)(2,1)S(1)} collective-permute-done((bf16[4096,128]{1,0:T(8,128)(2,1)}, bf16[4096,128]{1,0:T(8,128)(2,1)S(1)}, u32[]{:S(2)}, u32[]{:S(2)}) %collective-permute-start.2) | collective-permute-done | bytes 1048608 | tf_op jit(solution)/shard_map/ppermute | solution.py:406
  69.0 9.3 %row_forward.2 = bf16[32,16,32,128]{3,2,1,0:T(8,128)(2,1)} custom-call(s32[9]{0:T(128)} %pad_add_fusion.scalars, bf16[8,2,16,64,128]{4,3,2,1,0:T(8,128)(2,1)} %bitcast.51, bf16[128,128]{1,0:T(8,128)(2,1)} %constant.116.clone.lead_table, bf16[256,256]{1,0:T(8,128)(2,1)} %constant.117.clone.sub_table, f32[2,64,128]{2,1,0:T(8,128)} %constant.118.clone.turn), custom_call_target="tpu_custom_call" | custom-call | flops 16000000000 | bytes 8388608 | tf_op jit(solution)/shard_map/row_forward/pallas_call | solution.py:340
  78.3 8.2 %all-to-all-start = ((bf16[32,16,32,128]{3,2,1,0:T(8,128)(2,1)}), bf16[32,16,32,128]{3,2,1,0:T(8,128)(2,1)}, u32[]{:S(2)}, u32[]{:S(2)}) async-start(bf16[32,16,32,128]{3,2,1,0:T(8,128)(2,1)} %row_forward.2), calls=%async_computation | async-start | bytes 8388608 | tf_op jit(solution)/shard_map/all_to_all | solution.py:431
  88.2 2.0 copy-done
  91.1 6.0 %collective-permute-start.6 = (bf16[1280,128]{1,0:T(8,128)(2,1)S(1)}, bf16[1280,128]{1,0:T(8,128)(2,1)S(1)}, u32[]{:S(2)}, u32[]{:S(2)}) collective-permute-start(bf16[1280,128]{1,0:T(8,128)(2,1)S(1)} %get-tuple-element.56), channel_id=1, source_target_pairs={{0,48},{16,0},{32,16},{48,32},{1,49},{17,1},{33,17},{49,33},{2,50}... | collective-permute-start | bytes 983048 | tf_op jit(solution)/shard_map/ppermute | solution.py:406
  98.0 2.4 collective-permute-start.4
  100.4 51.6 %all-gather.7.cloned.1.call-done = bf16[16,16,64,128]{3,2,1,0:T(8,128)(2,1)} async-done(((bf16[2,16,64,128]{3,2,1,0:T(8,128)(2,1)}), bf16[16,16,64,128]{3,2,1,0:T(8,128)(2,1)}) %all-gather.7.cloned.1.call-update) | async-done | bytes 4194320 | tf_op jit(solution)/shard_map/all_gather | solution.py:424
  152.0 9.6 %row_forward.3 = bf16[32,16,32,128]{3,2,1,0:T(8,128)(2,1)} custom-call(s32[9]{0:T(128)} %pad_add_fusion.scalars, bf16[8,2,16,64,128]{4,3,2,1,0:T(8,128)(2,1)} %bitcast.50, bf16[128,128]{1,0:T(8,128)(2,1)} %constant.116.clone.lead_table, bf16[256,256]{1,0:T(8,128)(2,1)} %constant.117.clone.sub_table, f32[2,64,128]{2,1,0:T(8,128)} %constant.118.clone.turn), custom_call_target="tpu_custom_call" | custom-call | flops 16000000000 | bytes 8388608 | tf_op jit(solution)/shard_map/row_forward/pallas_call | solution.py:340
  161.6 7.6 %all-to-all-start.1 = ((bf16[32,16,32,128]{3,2,1,0:T(8,128)(2,1)}), bf16[32,16,32,128]{3,2,1,0:T(8,128)(2,1)}, u32[]{:S(2)}, u32[]{:S(2)}) async-start(bf16[32,16,32,128]{3,2,1,0:T(8,128)(2,1)} %row_forward.3), calls=%async_computation.1 | async-start | bytes 8388608 | tf_op jit(solution)/shard_map/all_to_all | solution.py:445
  172.1 1.9 collective-permute-start.9
  174.0 1.9 collective-permute-start.8
  177.3 7.7 %add_convert_fusion = (bf16[128,128,128]{2,1,0:T(8,128)(2,1)}, bf16[128,128,128]{2,1,0:T(8,128)(2,1)}) fusion(f32[128,128]{1,0:T(8,128)S(1)} %copy-done.4, f32[128,128]{1,0:T(8,128)S(1)} %copy-done.5, f32[128,128]{1,0:T(8,128)S(1)} %copy-done.3, f32[128,128]{1,0:T(8,128)S(1)} %copy-done.6, f32[128,128]{1,0:T(8,128)S(1)} %copy-done.7, ...), kind=kLoop, calls=%fused_computation | loop fusion | flops 16777216 | bytes 8847360 | tf_op jit(solution)/shard_map/convert_element_type | solution.py:88
  185.0 18.0 %collective-permute-done.9 = bf16[2816,128]{1,0:T(8,128)(2,1)S(1)} collective-permute-done((bf16[2816,128]{1,0:T(8,128)(2,1)S(1)}, bf16[2816,128]{1,0:T(8,128)(2,1)S(1)}, u32[]{:S(2)}, u32[]{:S(2)}) %collective-permute-start.9) | collective-permute-done | bytes 720928 | tf_op jit(solution)/shard_map/ppermute | solution.py:406
  203.0 7.1 %collective-permute-done.8 = bf16[2816,128]{1,0:T(8,128)(2,1)S(1)} collective-permute-done((bf16[2816,128]{1,0:T(8,128)(2,1)S(1)}, bf16[2816,128]{1,0:T(8,128)(2,1)S(1)}, u32[]{:S(2)}, u32[]{:S(2)}) %collective-permute-start.8) | collective-permute-done | bytes 720928 | tf_op jit(solution)/shard_map/ppermute | solution.py:406
  210.1 14.5 %collective-permute-done.7 = bf16[2816,128]{1,0:T(8,128)(2,1)S(1)} collective-permute-done((bf16[2816,128]{1,0:T(8,128)(2,1)S(1)}, bf16[2816,128]{1,0:T(8,128)(2,1)S(1)}, u32[]{:S(2)}, u32[]{:S(2)}) %collective-permute-start.7) | collective-permute-done | bytes 720928 | tf_op jit(solution)/shard_map/ppermute | solution.py:406
  225.5 41.1 %columns.1 = (bf16[32,16,32,128]{3,2,1,0:T(8,128)(2,1)}, bf16[32,16,32,128]{3,2,1,0:T(8,128)(2,1)}, f32[8,256]{1,0:T(8,128)}) custom-call(bf16[32,16,32,128]{3,2,1,0:T(8,128)(2,1)} %all-to-all-done.refs_0_, bf16[32,16,32,128]{3,2,1,0:T(8,128)(2,1)} %all-to-all-done.1.refs_1_, s32[1]{0:T(128)} %bitcast.12.refs_2_, bf16[10,128,128]{2,1,0:T(8,128)(2,1)} %bitcast.49, ...), custom_call_target="tpu_custom_call" | custom-call | flops 40000000000 | bytes 33554432 | tf_op jit(solution)/shard_map/columns/pallas_call | solution.py:389
  266.6 8.6 %all-to-all-start.2 = ((bf16[32,16,32,128]{3,2,1,0:T(8,128)(2,1)}), bf16[32,16,32,128]{3,2,1,0:T(8,128)(2,1)}, u32[]{:S(2)}, u32[]{:S(2)}) async-start(bf16[32,16,32,128]{3,2,1,0:T(8,128)(2,1)} %get-tuple-element.45), calls=%async_computation.2 | async-start | bytes 8388608 | tf_op jit(solution)/shard_map/all_to_all | solution.py:453
  275.8 16.5 %collective-permute-start.10 = (f32[1]{0:T(128)}, f32[1]{0:T(128)}, u32[]{:S(2)}, u32[]{:S(2)}) collective-permute-start(f32[1]{0:T(128)} %bitcast.24), channel_id=1, source_target_pairs={{0,4},{4,0},{1,5},{5,1},{2,6},{6,2},{3,7},{7,3},{8,12},{12,8},{9,1... | collective-permute-start | bytes 20 | tf_op jit(solution)/shard_map/ppermute | solution.py:410
  296.5 2.3 collective-permute-done.11
  299.3 3.3 collective-permute-start.12
  302.7 3.2 collective-permute-done.12
  306.4 21.0 %all-to-all-done.2.field = bf16[32,16,32,128]{3,2,1,0:T(8,128)(2,1)} async-done(((bf16[32,16,32,128]{3,2,1,0:T(8,128)(2,1)}), bf16[32,16,32,128]{3,2,1,0:T(8,128)(2,1)}, u32[]{:S(2)}, u32[]{:S(2)}) %all-to-all-start.2) | async-done | bytes 4194336 | tf_op jit(solution)/shard_map/all_to_all | solution.py:453
  327.4 9.6 %row_inverse.2 = bf16[8,2,16,64,128]{4,3,2,1,0:T(8,128)(2,1)} custom-call(s32[9]{0:T(128)} %pad_add_fusion.scalars, bf16[32,16,32,128]{3,2,1,0:T(8,128)(2,1)} %all-to-all-done.2.field, bf16[128,128]{1,0:T(8,128)(2,1)} %constant.128.clone.lead_table, bf16[256,256]{1,0:T(8,128)(2,1)} %constant.129.clone.sub_table, f32[2,512,128]{2,1,0:T(8,128)} %constant.130.clone.turn), custom_call_target="tpu_custom_call" | custom-call | flops 16000000000 | bytes 8388608 | tf_op jit(solution)/shard_map/row_inverse/pallas_call | solution.py:356
  337.0 57.9 %all_to_all.20.field = bf16[32,16,32,128]{3,2,1,0:T(8,128)(2,1)} all-to-all(bf16[32,16,32,128]{3,2,1,0:T(8,128)(2,1)} %get-tuple-element.49), channel_id=1, replica_groups=mesh['x'=4,'zh'=4,'core'=2,'zl'=2,'y'=4] {'x','y','core'}, dimensions={0} | all-to-all | bytes 8388608 | tf_op jit(solution)/shard_map/all_to_all | solution.py:453
  394.9 9.6 %row_inverse.3 = bf16[8,2,16,64,128]{4,3,2,1,0:T(8,128)(2,1)} custom-call(s32[9]{0:T(128)} %pad_add_fusion.scalars, bf16[32,16,32,128]{3,2,1,0:T(8,128)(2,1)} %all_to_all.20.field, bf16[128,128]{1,0:T(8,128)(2,1)} %constant.128.clone.lead_table, bf16[256,256]{1,0:T(8,128)(2,1)} %constant.129.clone.sub_table, f32[2,512,128]{2,1,0:T(8,128)} %constant.130.clone.turn), custom_call_target="tpu_custom_call" | custom-call | flops 16000000000 | bytes 8388608 | tf_op jit(solution)/shard_map/row_inverse/pallas_call | solution.py:356
  409.4 2.1 collective-permute-start.15
  417.0 2.2 collective-permute-start.17
  422.8 47.4 %reduce-scatter.5.cloned.1.call-done = bf16[1,2,16,64,128]{4,3,2,1,0:T(8,128)(2,1)} async-done(((bf16[8,2,16,64,128]{4,3,2,1,0:T(8,128)(2,1)}), bf16[1,2,16,64,128]{4,3,2,1,0:T(8,128)(2,1)}) %reduce-scatter.5.cloned.1.call-update) | async-done | bytes 524304 | tf_op jit(solution)/shard_map/reduce_scatter | solution.py:459
  (78 shorter events, 33.9 us)
Async XLA Ops:
  7.2 61.5 %all-gather.5.cloned.1.call-start = ((), (), s32[]{:S(2)}) async-start(), calls=%async_computation.8 | async-start | bytes 4718592 | tf_op jit(solution)/shard_map/all_gather | solution.py:424
  9.8 142.1 %all-gather.7.cloned.1.call-start = ((), (), s32[]{:S(2)}) async-start(), calls=%async_computation.9 | async-start | bytes 4718592 | tf_op jit(solution)/shard_map/all_gather | solution.py:424
  18.1 24.7 %collective-permute-start.1 = (bf16[4096,128]{1,0:T(8,128)(2,1)}, bf16[4096,128]{1,0:T(8,128)(2,1)S(1)}, u32[]{:S(2)}, u32[]{:S(2)}) collective-permute-start(bf16[4096,128]{1,0:T(8,128)(2,1)} %get-tuple-element.28), channel_id=1, source_target_pairs={{0,1},{1,2},{2,3},{3,0},{4,5},{5,6},{6,7},{7,4},{8,9},{9,10},{10,1... | collective-permute-start | bytes 3145736 | tf_op jit(solution)/shard_map/ppermute | solution.py:406
  20.2 47.9 %collective-permute-start.2 = (bf16[4096,128]{1,0:T(8,128)(2,1)}, bf16[4096,128]{1,0:T(8,128)(2,1)S(1)}, u32[]{:S(2)}, u32[]{:S(2)}) collective-permute-start(bf16[4096,128]{1,0:T(8,128)(2,1)} %get-tuple-element.29), channel_id=1, source_target_pairs={{0,2},{1,3},{2,0},{3,1},{4,6},{5,7},{6,4},{7,5},{8,10},{9,11},{10,... | collective-permute-start | bytes 3145736 | tf_op jit(solution)/shard_map/ppermute | solution.py:406
  22.8 45.2 %collective-permute-start.3 = (bf16[4096,128]{1,0:T(8,128)(2,1)}, bf16[4096,128]{1,0:T(8,128)(2,1)S(1)}, u32[]{:S(2)}, u32[]{:S(2)}) collective-permute-start(bf16[4096,128]{1,0:T(8,128)(2,1)} %get-tuple-element.30), channel_id=1, source_target_pairs={{0,3},{1,0},{2,1},{3,2},{4,7},{5,4},{6,5},{7,6},{8,11},{9,8},{10,9... | collective-permute-start | bytes 3145736 | tf_op jit(solution)/shard_map/ppermute | solution.py:406
  23.9 1.8 collective-permute-start
  78.3 8.2 %copy-start.1 = (bf16[4096,128]{1,0:T(8,128)(2,1)S(1)}, bf16[4096,128]{1,0:T(8,128)(2,1)}, u32[]{:S(2)}) copy-start(bf16[4096,128]{1,0:T(8,128)(2,1)} %get-tuple-element.31) | copy-start | bytes 3145732
  78.3 73.7 %all-to-all-start = ((bf16[32,16,32,128]{3,2,1,0:T(8,128)(2,1)}), bf16[32,16,32,128]{3,2,1,0:T(8,128)(2,1)}, u32[]{:S(2)}, u32[]{:S(2)}) async-start(bf16[32,16,32,128]{3,2,1,0:T(8,128)(2,1)} %row_forward.2), calls=%async_computation | async-start | bytes 8388608 | tf_op jit(solution)/shard_map/all_to_all | solution.py:431
  91.1 60.9 %collective-permute-start.6 = (bf16[1280,128]{1,0:T(8,128)(2,1)S(1)}, bf16[1280,128]{1,0:T(8,128)(2,1)S(1)}, u32[]{:S(2)}, u32[]{:S(2)}) collective-permute-start(bf16[1280,128]{1,0:T(8,128)(2,1)S(1)} %get-tuple-element.56), channel_id=1, source_target_pairs={{0,48},{16,0},{32,16},{48,32},{1,49},{17,1},{33,17},{49,33},{2,50}... | collective-permute-start | bytes 983048 | tf_op jit(solution)/shard_map/ppermute | solution.py:406
  97.1 54.8 %collective-permute-start.5 = (bf16[1280,128]{1,0:T(8,128)(2,1)S(1)}, bf16[1280,128]{1,0:T(8,128)(2,1)S(1)}, u32[]{:S(2)}, u32[]{:S(2)}) collective-permute-start(bf16[1280,128]{1,0:T(8,128)(2,1)S(1)} %get-tuple-element.57), channel_id=1, source_target_pairs={{0,32},{16,48},{32,0},{48,16},{1,33},{17,49},{33,1},{49,17},{2,34}... | collective-permute-start | bytes 983048 | tf_op jit(solution)/shard_map/ppermute | solution.py:406
  98.0 54.0 %collective-permute-start.4 = (bf16[1280,128]{1,0:T(8,128)(2,1)S(1)}, bf16[1280,128]{1,0:T(8,128)(2,1)S(1)}, u32[]{:S(2)}, u32[]{:S(2)}) collective-permute-start(bf16[1280,128]{1,0:T(8,128)(2,1)S(1)} %get-tuple-element.58), channel_id=1, source_target_pairs={{0,16},{16,32},{32,48},{48,0},{1,17},{17,33},{33,49},{49,1},{2,18}... | collective-permute-start | bytes 983048 | tf_op jit(solution)/shard_map/ppermute | solution.py:406
  151.9 9.7 %copy-start.14 = (bf16[1280,128]{1,0:T(8,128)(2,1)}, bf16[1280,128]{1,0:T(8,128)(2,1)S(1)}, u32[]{:S(2)}) copy-start(bf16[1280,128]{1,0:T(8,128)(2,1)S(1)} %collective-permute-done.6) | copy-start | bytes 983044
  151.9 9.7 %copy-start.15 = (bf16[1280,128]{1,0:T(8,128)(2,1)}, bf16[1280,128]{1,0:T(8,128)(2,1)S(1)}, u32[]{:S(2)}) copy-start(bf16[1280,128]{1,0:T(8,128)(2,1)S(1)} %collective-permute-done.5) | copy-start | bytes 983044
  152.0 9.6 %copy-start.16 = (bf16[1280,128]{1,0:T(8,128)(2,1)}, bf16[1280,128]{1,0:T(8,128)(2,1)S(1)}, u32[]{:S(2)}) copy-start(bf16[1280,128]{1,0:T(8,128)(2,1)S(1)} %collective-permute-done.4) | copy-start | bytes 983044
  161.6 63.0 %all-to-all-start.1 = ((bf16[32,16,32,128]{3,2,1,0:T(8,128)(2,1)}), bf16[32,16,32,128]{3,2,1,0:T(8,128)(2,1)}, u32[]{:S(2)}, u32[]{:S(2)}) async-start(bf16[32,16,32,128]{3,2,1,0:T(8,128)(2,1)} %row_forward.3), calls=%async_computation.1 | async-start | bytes 8388608 | tf_op jit(solution)/shard_map/all_to_all | solution.py:445
  172.1 30.8 %collective-permute-start.9 = (bf16[2816,128]{1,0:T(8,128)(2,1)S(1)}, bf16[2816,128]{1,0:T(8,128)(2,1)S(1)}, u32[]{:S(2)}, u32[]{:S(2)}) collective-permute-start(bf16[2816,128]{1,0:T(8,128)(2,1)S(1)} %get-tuple-element.52), channel_id=1, source_target_pairs={{0,48},{16,0},{32,16},{48,32},{1,49},{17,1},{33,17},{49,33},{2,50}... | collective-permute-start | bytes 2162696 | tf_op jit(solution)/shard_map/ppermute | solution.py:406
  174.0 36.0 %collective-permute-start.8 = (bf16[2816,128]{1,0:T(8,128)(2,1)S(1)}, bf16[2816,128]{1,0:T(8,128)(2,1)S(1)}, u32[]{:S(2)}, u32[]{:S(2)}) collective-permute-start(bf16[2816,128]{1,0:T(8,128)(2,1)S(1)} %get-tuple-element.53), channel_id=1, source_target_pairs={{0,32},{16,48},{32,0},{48,16},{1,33},{17,49},{33,1},{49,17},{2,34}... | collective-permute-start | bytes 2162696 | tf_op jit(solution)/shard_map/ppermute | solution.py:406
  175.9 48.7 %collective-permute-start.7 = (bf16[2816,128]{1,0:T(8,128)(2,1)S(1)}, bf16[2816,128]{1,0:T(8,128)(2,1)S(1)}, u32[]{:S(2)}, u32[]{:S(2)}) collective-permute-start(bf16[2816,128]{1,0:T(8,128)(2,1)S(1)} %get-tuple-element.54), channel_id=1, source_target_pairs={{0,16},{16,32},{32,48},{48,0},{1,17},{17,33},{33,49},{49,1},{2,18}... | collective-permute-start | bytes 2162696 | tf_op jit(solution)/shard_map/ppermute | solution.py:406
  203.0 21.6 %copy-start.11 = (bf16[2816,128]{1,0:T(8,128)(2,1)}, bf16[2816,128]{1,0:T(8,128)(2,1)S(1)}, u32[]{:S(2)}) copy-start(bf16[2816,128]{1,0:T(8,128)(2,1)S(1)} %collective-permute-done.9) | copy-start | bytes 2162692
  210.1 14.6 %copy-start.12 = (bf16[2816,128]{1,0:T(8,128)(2,1)}, bf16[2816,128]{1,0:T(8,128)(2,1)S(1)}, u32[]{:S(2)}) copy-start(bf16[2816,128]{1,0:T(8,128)(2,1)S(1)} %collective-permute-done.8) | copy-start | bytes 2162692
  266.6 8.7 %copy-start.10 = (f32[8,256]{1,0:T(8,128)S(1)}, f32[8,256]{1,0:T(8,128)}, u32[]{:S(2)}) copy-start(f32[8,256]{1,0:T(8,128)} %get-tuple-element.44) | copy-start | bytes 24580
  266.6 60.8 %all-to-all-start.2 = ((bf16[32,16,32,128]{3,2,1,0:T(8,128)(2,1)}), bf16[32,16,32,128]{3,2,1,0:T(8,128)(2,1)}, u32[]{:S(2)}, u32[]{:S(2)}) async-start(bf16[32,16,32,128]{3,2,1,0:T(8,128)(2,1)} %get-tuple-element.45), calls=%async_computation.2 | async-start | bytes 8388608 | tf_op jit(solution)/shard_map/all_to_all | solution.py:453
  275.2 146.3 %reduce-scatter.3.cloned.1.call-start = ((), (), s32[]{:S(2)}) async-start(), calls=%async_computation.6 | async-start | bytes 4718592 | tf_op jit(solution)/shard_map/reduce_scatter | solution.py:459
  275.8 18.0 %collective-permute-start.10 = (f32[1]{0:T(128)}, f32[1]{0:T(128)}, u32[]{:S(2)}, u32[]{:S(2)}) collective-permute-start(f32[1]{0:T(128)} %bitcast.24), channel_id=1, source_target_pairs={{0,4},{4,0},{1,5},{5,1},{2,6},{6,2},{3,7},{7,3},{8,12},{12,8},{9,1... | collective-permute-start | bytes 20 | tf_op jit(solution)/shard_map/ppermute | solution.py:410
  295.0 3.8 collective-permute-start.11
  299.3 6.5 %collective-permute-start.12 = (f32[1]{0:T(128)}, f32[1]{0:T(128)}, u32[]{:S(2)}, u32[]{:S(2)}) collective-permute-start(f32[1]{0:T(128)} %add.126), channel_id=1, source_target_pairs={{0,32},{16,48},{32,0},{48,16},{1,33},{17,49},{33,1},{49,17},{2,34}... | collective-permute-start | bytes 20 | tf_op jit(solution)/shard_map/ppermute | solution.py:410
  337.0 133.1 %reduce-scatter.5.cloned.1.call-start = ((), (), s32[]{:S(2)}) async-start(), calls=%async_computation.7 | async-start | bytes 4718592 | tf_op jit(solution)/shard_map/reduce_scatter | solution.py:459
  404.5 1.3 collective-permute-start.13
  406.4 2.4 collective-permute-start.14
  409.4 3.9 collective-permute-start.15
  413.9 2.4 collective-permute-start.16
  417.0 3.9 collective-permute-start.17
  (11 other events, 49.3 us)
Sparse Core Ops, SparseCore 0:
  9.9 58.6 all-gather.4
  70.4 81.4 all-gather.6
  337.1 68.6 reduce-scatter.2
  408.2 61.9 reduce-scatter.4
